TPU v7x, 32 devices: a whole 2x2x4 slice. The times are simulated.
32 devices in a mesh: dp: 8 (over z, y), mp: 4 (over x, core).
Axes of the slice: x: 2, y: 2, z: 4, core: 2. Of those that a mesh axis runs over, the one named last changes fastest.
Arguments:
- tokens: bfloat16 [4096, 2048], P('dp'), may hold values from -6 to 6
- text: bfloat16 [2048, 4096], P('dp', 'mp'), may hold values from -6 to 6
- image_seg: int32 [8, 512], P('dp'), may hold values from 0 to 1, never falling along the last dimension, each value on 1 to 320 neighbouring positions
- text_seg: int32 [8, 256], P('dp'), may hold values from 0 to 1, never falling along the last dimension, each value on 1 to 160 neighbouring positions
- w_qkv: bfloat16 [3, 2048, 2048], P(None, 'dp', 'mp'), may hold values from -0.125 to 0.125
- w_out: bfloat16 [2048, 2048], P('mp', 'dp'), may hold values from -1 to 1
- c_q: bfloat16 [2048, 2048], P('dp', 'mp'), may hold values from -0.125 to 0.125
- c_kv: bfloat16 [2, 4096, 2048], P(None, 'dp', 'mp'), may hold values from -0.09375 to 0.09375
- c_out: bfloat16 [2048, 2048], P('mp', 'dp'), may hold values from -1 to 1
- w_up: bfloat16 [2048, 8192], P('dp', 'mp'), may hold values from -0.125 to 0.125
- w_down: bfloat16 [8192, 2048], P('mp', 'dp'), may hold values from -0.0625 to 0.0625
- norm_gain: float32 [4, 2048], replicated, may hold values from 0.25 to 1.75
- norm_bias: float32 [4, 2048], replicated, may hold values from -4 to 4
- out_bias: float32 [3, 2048], replicated, may hold values from -4 to 4
- up_bias: float32 [8192], P('mp'), may hold values from -4 to 4
- cotangent: bfloat16 [4096, 2048], P('dp'), may hold values from -6 to 6
Outputs:
- output: bfloat16 [4096, 2048], P('dp')
- grad_tokens: float32 [4096, 2048], P('dp')
- grad_text: float32 [2048, 4096], P('dp', 'mp')
- grad_w_qkv: float32 [3, 2048, 2048], P(None, 'dp', 'mp')
- grad_w_out: float32 [2048, 2048], P('mp', 'dp')
- grad_c_q: float32 [2048, 2048], P('dp', 'mp')
- grad_c_kv: float32 [2, 4096, 2048], P(None, 'dp', 'mp')
- grad_c_out: float32 [2048, 2048], P('mp', 'dp')
- grad_w_up: float32 [2048, 8192], P('dp', 'mp')
- grad_w_down: float32 [8192, 2048], P('mp', 'dp')
- grad_norm_gain: float32 [4, 2048], replicated
- grad_norm_bias: float32 [4, 2048], replicated
- grad_out_bias: float32 [3, 2048], replicated
- grad_up_bias: float32 [8192], P('mp')
Inputs may be any that keep to these rules, and one draw needn't show every extreme that they name: In each row image_seg is 0 on the first image and 1 on the second; both images are present, and none has more than 320 tokens. In each row text_seg is 0 on the first caption and 1 on the second; both captions are present, and none has more than 160 tokens.
All inputs are finite; a program needn't handle non-finite values.
Results may differ from a plain program's by a relative error of at most 0.02.
Values may be sent and summed in bfloat16 or wider, within the bound.
No kernel may reach another device: no remote copies, remote signals or barrier semaphores. Data moves between devices by JAX's collectives and lax.ppermute only.
A program may use at most 256 MiB of HBM per device.

v0:
```python
import jax
import jax.numpy as jnp
from jax import lax
from jax.sharding import PartitionSpec as P

HD = 128


eps = 1e-05
masked = -1e30


def normalize(values, gain, shift):
    center = values - jnp.mean(values, axis=-1, keepdims=True)
    spread = jnp.mean(center * center, axis=-1, keepdims=True)
    return center * lax.rsqrt(spread + eps) * gain + shift


def gelu_tanh(values):
    return (
        0.5
        * values
        * (1.0 + jnp.tanh(0.7978845608028654 * (values + 0.044715 * values * values * values)))
    )


def heads_sum(partial_value):
    return lax.psum(partial_value, "mp")


def input_sum(partial_value):
    return lax.psum(partial_value, "mp")


def split_heads(values):
    return values.reshape(values.shape[0], values.shape[1] // HD, HD)


def scores_of(queries, key_rows, allowed):
    raw = jnp.einsum(
        "qhd,khd->hqk",
        split_heads(queries),
        split_heads(key_rows),
        preferred_element_type=jnp.float32,
    ) * HD ** (-0.5)
    return jnp.where(allowed[None], raw, masked)


def attend_forward(queries, key_rows, value_rows, allowed):
    scores = scores_of(queries, key_rows, allowed)
    top = jnp.max(scores, axis=-1, keepdims=True)
    expo = jnp.exp(scores - top)
    total = jnp.sum(expo, axis=-1, keepdims=True)
    probs = (expo / total).astype(jnp.bfloat16)
    mixed = jnp.einsum(
        "hqk,khd->qhd", probs, split_heads(value_rows), preferred_element_type=jnp.float32
    )
    return (
        mixed.reshape(queries.shape[0], queries.shape[1]).astype(jnp.bfloat16),
        top + jnp.log(total),
    )


def attend_backward(queries, key_rows, value_rows, grad_mixed, logsum, allowed):
    scores = scores_of(queries, key_rows, allowed)
    probs = jnp.exp(scores - logsum)
    grad_heads = split_heads(grad_mixed)
    grad_values = jnp.einsum(
        "hqk,qhd->khd", probs.astype(jnp.bfloat16), grad_heads, preferred_element_type=jnp.float32
    )
    grad_probs = jnp.einsum(
        "qhd,khd->hqk", grad_heads, split_heads(value_rows), preferred_element_type=jnp.float32
    )
    grad_scores = (
        probs * (grad_probs - jnp.sum(probs * grad_probs, axis=-1, keepdims=True))
    ).astype(jnp.bfloat16)
    grad_queries = jnp.einsum(
        "hqk,khd->qhd", grad_scores, split_heads(key_rows), preferred_element_type=jnp.float32
    ) * HD ** (-0.5)
    grad_keys = jnp.einsum(
        "hqk,qhd->khd", grad_scores, split_heads(queries), preferred_element_type=jnp.float32
    ) * HD ** (-0.5)
    return (
        grad_queries.reshape(queries.shape),
        grad_keys.reshape(key_rows.shape),
        grad_values.reshape(value_rows.shape),
    )


def on_device(
    tokens,
    text,
    image_seg,
    text_seg,
    w_qkv,
    w_out,
    c_q,
    c_kv,
    c_out,
    w_up,
    w_down,
    norm_gain,
    norm_bias,
    out_bias,
    up_bias,
    cotangent,
):
    row_count = image_seg.shape[0]
    length = image_seg.shape[1]
    text_len = text_seg.shape[1]
    gathered = (
        lax.all_gather(w_qkv, "dp", axis=1, tiled=True),
        lax.all_gather(w_out, "dp", axis=1, tiled=True),
        lax.all_gather(c_q, "dp", axis=0, tiled=True),
        lax.all_gather(c_kv, "dp", axis=1, tiled=True),
        lax.all_gather(c_out, "dp", axis=1, tiled=True),
        lax.all_gather(w_up, "dp", axis=0, tiled=True),
        lax.all_gather(w_down, "dp", axis=1, tiled=True),
    )
    full_qkv, full_out, full_cq, full_ckv, full_cout, full_up, full_down = gathered
    words = lax.all_gather(text, "mp", axis=1, tiled=True)
    same_image = image_seg[:, :, None] == image_seg[:, None, :]
    caption = image_seg[:, :, None] == text_seg[:, None, :]
    residual = tokens.astype(jnp.float32)
    width = full_qkv.shape[2]
    normed_one, pull_one = jax.vjp(normalize, residual, norm_gain[0], norm_bias[0])
    hidden_one = normed_one.astype(jnp.bfloat16)
    projected = jnp.einsum(
        "td,cde->cte", hidden_one, full_qkv, preferred_element_type=jnp.float32
    ).astype(jnp.bfloat16)
    self_inputs = (
        projected[0].reshape(row_count, length, width),
        projected[1].reshape(row_count, length, width),
        projected[2].reshape(row_count, length, width),
    )
    self_mixed, self_logsum = lax.map(
        lambda pieces: attend_forward(*pieces), self_inputs + (same_image,)
    )
    self_flat = self_mixed.reshape(row_count * length, width)
    after_self = (
        residual
        + heads_sum(jnp.dot(self_flat, full_out, preferred_element_type=jnp.float32))
        + out_bias[0]
    )
    normed_two, pull_two = jax.vjp(normalize, after_self, norm_gain[1], norm_bias[1])
    hidden_two = normed_two.astype(jnp.bfloat16)
    cross_query = jnp.dot(hidden_two, full_cq, preferred_element_type=jnp.float32).astype(
        jnp.bfloat16
    )
    text_kv = jnp.einsum("td,cde->cte", words, full_ckv, preferred_element_type=jnp.float32).astype(
        jnp.bfloat16
    )
    cross_inputs = (
        cross_query.reshape(row_count, length, width),
        text_kv[0].reshape(row_count, text_len, width),
        text_kv[1].reshape(row_count, text_len, width),
    )
    cross_mixed, cross_logsum = lax.map(
        lambda pieces: attend_forward(*pieces), cross_inputs + (caption,)
    )
    cross_flat = cross_mixed.reshape(row_count * length, width)
    after_cross = (
        after_self
        + heads_sum(jnp.dot(cross_flat, full_cout, preferred_element_type=jnp.float32))
        + out_bias[1]
    )
    normed_three, pull_three = jax.vjp(normalize, after_cross, norm_gain[2], norm_bias[2])
    hidden_three = normed_three.astype(jnp.bfloat16)
    pre_act = jnp.dot(hidden_three, full_up, preferred_element_type=jnp.float32) + up_bias
    activated, pull_gelu = jax.vjp(gelu_tanh, pre_act)
    act_low = activated.astype(jnp.bfloat16)
    after_mlp = (
        after_cross
        + heads_sum(jnp.dot(act_low, full_down, preferred_element_type=jnp.float32))
        + out_bias[2]
    )
    final, pull_four = jax.vjp(normalize, after_mlp, norm_gain[3], norm_bias[3])
    output = final.astype(jnp.bfloat16)
    grad_mlp, gain_four, shift_four = pull_four(cotangent.astype(jnp.float32))
    grad_mlp_low = grad_mlp.astype(jnp.bfloat16)
    grad_down = jnp.einsum("tf,td->fd", act_low, grad_mlp_low, preferred_element_type=jnp.float32)
    grad_act = jnp.einsum("td,fd->tf", grad_mlp_low, full_down, preferred_element_type=jnp.float32)
    grad_pre = pull_gelu(grad_act)[0].astype(jnp.bfloat16)
    up_bias_grad = jnp.sum(grad_pre.astype(jnp.float32), axis=0)
    grad_up = jnp.einsum("td,tf->df", hidden_three, grad_pre, preferred_element_type=jnp.float32)
    grad_hidden_three = input_sum(
        jnp.einsum("tf,df->td", grad_pre, full_up, preferred_element_type=jnp.float32)
    )
    grad_cross_in, gain_three, shift_three = pull_three(grad_hidden_three)
    grad_after_cross = grad_mlp + grad_cross_in
    grad_cross_low = grad_after_cross.astype(jnp.bfloat16)
    grad_cout = jnp.einsum(
        "te,td->ed", cross_flat, grad_cross_low, preferred_element_type=jnp.float32
    )
    grad_cmix = jnp.einsum(
        "td,ed->te", grad_cross_low, full_cout, preferred_element_type=jnp.float32
    ).astype(jnp.bfloat16)
    cq_grad, ck_grad, cv_grad = lax.map(
        lambda pieces: attend_backward(*pieces),
        cross_inputs + (grad_cmix.reshape(row_count, length, width), cross_logsum, caption),
    )
    cq_low = cq_grad.reshape(row_count * length, width).astype(jnp.bfloat16)
    ckv_low = jnp.stack(
        [ck_grad.reshape(row_count * text_len, width), cv_grad.reshape(row_count * text_len, width)]
    ).astype(jnp.bfloat16)
    grad_cq = jnp.einsum("td,te->de", hidden_two, cq_low, preferred_element_type=jnp.float32)
    grad_ckv = jnp.einsum("td,cte->cde", words, ckv_low, preferred_element_type=jnp.float32)
    text_term = jnp.einsum("cte,cde->td", ckv_low, full_ckv, preferred_element_type=jnp.float32)
    grad_text = lax.psum_scatter(
        text_term.astype(jnp.bfloat16), "mp", scatter_dimension=1, tiled=True
    ).astype(jnp.float32)
    grad_hidden_two = input_sum(
        jnp.einsum("te,de->td", cq_low, full_cq, preferred_element_type=jnp.float32)
    )
    grad_self_in, gain_two, shift_two = pull_two(grad_hidden_two)
    grad_after_self = grad_after_cross + grad_self_in
    grad_self_low = grad_after_self.astype(jnp.bfloat16)
    grad_wout = jnp.einsum(
        "te,td->ed", self_flat, grad_self_low, preferred_element_type=jnp.float32
    )
    grad_smix = jnp.einsum(
        "td,ed->te", grad_self_low, full_out, preferred_element_type=jnp.float32
    ).astype(jnp.bfloat16)
    sq_grad, sk_grad, sv_grad = lax.map(
        lambda pieces: attend_backward(*pieces),
        self_inputs + (grad_smix.reshape(row_count, length, width), self_logsum, same_image),
    )
    qkv_low = jnp.stack(
        [
            sq_grad.reshape(row_count * length, width),
            sk_grad.reshape(row_count * length, width),
            sv_grad.reshape(row_count * length, width),
        ]
    ).astype(jnp.bfloat16)
    grad_qkv = jnp.einsum("td,cte->cde", hidden_one, qkv_low, preferred_element_type=jnp.float32)
    grad_hidden_one = input_sum(
        jnp.einsum("cte,cde->td", qkv_low, full_qkv, preferred_element_type=jnp.float32)
    )
    grad_in_one, gain_one, shift_one = pull_one(grad_hidden_one)
    grad_tokens = grad_after_self + grad_in_one
    gain_terms = jnp.stack([gain_one, gain_two, gain_three, gain_four])
    shift_terms = jnp.stack([shift_one, shift_two, shift_three, shift_four])
    bias_terms = jnp.stack(
        [
            jnp.sum(grad_after_self, axis=0),
            jnp.sum(grad_after_cross, axis=0),
            jnp.sum(grad_mlp, axis=0),
        ]
    )
    gain_total, shift_total, bias_total, up_total = (
        lax.psum(gain_terms.astype(jnp.bfloat16), "dp").astype(jnp.float32),
        lax.psum(shift_terms.astype(jnp.bfloat16), "dp").astype(jnp.float32),
        lax.psum(bias_terms.astype(jnp.bfloat16), "dp").astype(jnp.float32),
        lax.psum(up_bias_grad.astype(jnp.bfloat16), "dp").astype(jnp.float32),
    )
    sum_qkv, sum_wout, sum_cq, sum_ckv, sum_cout, sum_up, sum_down = (
        lax.psum_scatter(
            grad_qkv.astype(jnp.bfloat16), "dp", scatter_dimension=1, tiled=True
        ).astype(jnp.float32),
        lax.psum_scatter(
            grad_wout.astype(jnp.bfloat16), "dp", scatter_dimension=1, tiled=True
        ).astype(jnp.float32),
        lax.psum_scatter(
            grad_cq.astype(jnp.bfloat16), "dp", scatter_dimension=0, tiled=True
        ).astype(jnp.float32),
        lax.psum_scatter(
            grad_ckv.astype(jnp.bfloat16), "dp", scatter_dimension=1, tiled=True
        ).astype(jnp.float32),
        lax.psum_scatter(
            grad_cout.astype(jnp.bfloat16), "dp", scatter_dimension=1, tiled=True
        ).astype(jnp.float32),
        lax.psum_scatter(
            grad_up.astype(jnp.bfloat16), "dp", scatter_dimension=0, tiled=True
        ).astype(jnp.float32),
        lax.psum_scatter(
            grad_down.astype(jnp.bfloat16), "dp", scatter_dimension=1, tiled=True
        ).astype(jnp.float32),
    )
    return (
        output,
        grad_tokens,
        grad_text,
        sum_qkv,
        sum_wout,
        sum_cq,
        sum_ckv,
        sum_cout,
        sum_up,
        sum_down,
        gain_total,
        shift_total,
        bias_total,
        up_total,
    )


def solution(mesh):
    in_specs = (
        P("dp", None),
        P("dp", "mp"),
        P("dp", None),
        P("dp", None),
        P(None, "dp", "mp"),
        P("mp", "dp"),
        P("dp", "mp"),
        P(None, "dp", "mp"),
        P("mp", "dp"),
        P("dp", "mp"),
        P("mp", "dp"),
        P(),
        P(),
        P(),
        P("mp"),
        P("dp", None),
    )
    out_specs = (
        P("dp", None),
        P("dp", None),
        P("dp", "mp"),
        P(None, "dp", "mp"),
        P("mp", "dp"),
        P("dp", "mp"),
        P(None, "dp", "mp"),
        P("mp", "dp"),
        P("dp", "mp"),
        P("mp", "dp"),
        P(),
        P(),
        P(),
        P("mp"),
    )
    return jax.shard_map(
        on_device, mesh=mesh, in_specs=in_specs, out_specs=out_specs, check_vma=False
    )
```

profile of v0, /device:TPU:0, one launch (start us, length us, event | category | flops | bytes accessed | tf_op | source)
XLA Modules:
  0.0 2110.1 jit_solution(6485817762568258638)
XLA Ops:
  13.9 99.0 %all-gather.9.cloned.1.call-done = bf16[3,2048,512]{1,2,0:T(8,128)(2,1)} async-done(((bf16[3,256,512]{1,2,0:T(8,128)(2,1)}), bf16[3,2048,512]{1,2,0:T(8,128)(2,1)}) %all-gather.9.cloned.1.call-update) | async-done | bytes 6291472 | tf_op jit(solution)/shard_map/all_gather | solution.py:112
  112.9 6.6 fusion.35
  124.3 39.2 %all-gather.11.cloned.1.call-done = bf16[512,2048]{1,0:T(8,128)(2,1)} async-done(((bf16[512,256]{1,0:T(8,128)(2,1)}), bf16[512,2048]{1,0:T(8,128)(2,1)}) %all-gather.11.cloned.1.call-update) | async-done | bytes 2097168 | tf_op jit(solution)/shard_map/all_gather | solution.py:113
  163.5 4.9 fusion.88
  172.1 80.1 %all-reduce.8.cloned.1.call-done = f32[512,2048]{1,0:T(8,128)} async-done(((f32[512,2048]{1,0:T(8,128)}), f32[512,2048]{1,0:T(8,128)}) %all-reduce.8.cloned.1.call-update) | async-done | bytes 4194320 | tf_op jit(solution)/shard_map/psum | solution.py:28
  257.8 45.6 %all-gather.17.cloned.1.call-done = bf16[2048,512]{1,0:T(8,128)(2,1)} async-done(((bf16[256,512]{1,0:T(8,128)(2,1)}), bf16[2048,512]{1,0:T(8,128)(2,1)}) %all-gather.17.cloned.1.call-update) | async-done | bytes 2097168 | tf_op jit(solution)/shard_map/all_gather | solution.py:114
  306.4 19.6 all-gather.15.cloned.1.call-done
  326.0 127.4 %all-gather.13.cloned.1.call-done = bf16[2,4096,512]{1,2,0:T(8,128)(2,1)} async-done(((bf16[2,512,512]{1,2,0:T(8,128)(2,1)}), bf16[2,4096,512]{1,2,0:T(8,128)(2,1)}) %all-gather.13.cloned.1.call-update) | async-done | bytes 8388624 | tf_op jit(solution)/shard_map/all_gather | solution.py:115
  453.4 6.4 fusion.46
  461.3 42.7 %all-gather.19.cloned.1.call-done = bf16[512,2048]{1,0:T(8,128)(2,1)} async-done(((bf16[512,256]{1,0:T(8,128)(2,1)}), bf16[512,2048]{1,0:T(8,128)(2,1)}) %all-gather.19.cloned.1.call-update) | async-done | bytes 2097168 | tf_op jit(solution)/shard_map/all_gather | solution.py:116
  504.0 4.8 fusion.89
  510.5 82.2 %all-reduce.10.cloned.1.call-done = f32[512,2048]{1,0:T(8,128)} async-done(((f32[512,2048]{1,0:T(8,128)}), f32[512,2048]{1,0:T(8,128)}) %all-reduce.10.cloned.1.call-update) | async-done | bytes 4194320 | tf_op jit(solution)/shard_map/psum | solution.py:28
  592.7 4.0 fusion.77
  599.3 120.2 %all-gather.21.cloned.1.call-done = bf16[2048,2048]{1,0:T(8,128)(2,1)} async-done(((bf16[256,2048]{1,0:T(8,128)(2,1)}), bf16[2048,2048]{1,0:T(8,128)(2,1)}) %all-gather.21.cloned.1.call-update) | async-done | bytes 8388624 | tf_op jit(solution)/shard_map/all_gather | solution.py:117
  719.5 11.2 fusion.69
  730.7 113.8 %all-gather.23.cloned.1.call-done = bf16[2048,2048]{1,0:T(8,128)(2,1)} async-done(((bf16[2048,256]{1,0:T(8,128)(2,1)}), bf16[2048,2048]{1,0:T(8,128)(2,1)}) %all-gather.23.cloned.1.call-update) | async-done | bytes 8388624 | tf_op jit(solution)/shard_map/all_gather | solution.py:118
  844.5 11.5 fusion.68
  856.4 83.5 %all-reduce.12.cloned.1.call-done = f32[512,2048]{1,0:T(8,128)} async-done(((f32[512,2048]{1,0:T(8,128)}), f32[512,2048]{1,0:T(8,128)}) %all-reduce.12.cloned.1.call-update) | async-done | bytes 4194320 | tf_op jit(solution)/shard_map/psum | solution.py:28
  939.9 4.0 fusion.76
  947.0 2.9 fusion.75
  949.9 12.0 fusion.87
  963.2 6.1 fusion.90
  969.9 85.3 %all-reduce.14.cloned.1.call-done = f32[512,2048]{1,0:T(8,128)} async-done(((f32[512,2048]{1,0:T(8,128)}), f32[512,2048]{1,0:T(8,128)}) %all-reduce.14.cloned.1.call-update) | async-done | bytes 4194320 | tf_op jit(solution)/shard_map/psum | solution.py:32
  1055.2 4.8 multiply_reduce_fusion
  1068.7 3.3 fusion.91
  1072.2 85.5 %all-reduce.16.cloned.1.call-done = f32[512,2048]{1,0:T(8,128)} async-done(((f32[512,2048]{1,0:T(8,128)}), f32[512,2048]{1,0:T(8,128)}) %all-reduce.16.cloned.1.call-update) | async-done | bytes 4194320 | tf_op jit(solution)/shard_map/psum | solution.py:32
  1157.7 4.7 multiply_reduce_fusion.1
  1183.2 8.6 convolution_bitcast_fusion.1
  1191.9 4.3 convolution_convert_fusion.3
  1201.6 7.2 fusion.4
  1208.8 4.9 convolution_convert_fusion.2
  1213.8 4.8 convolution_convert_fusion.4
  1218.7 12.4 convolution_convert_fusion
  1232.8 9.4 convolution_convert_fusion.1
  1244.1 7.1 convert_bitcast_fusion.1
  1251.3 7.2 convert_bitcast_fusion
  1260.7 16.9 all-reduce.18.cloned.1.call-done
  1277.6 3.3 fusion.70
  1283.1 38.5 %all-reduce = (bf16[4,2048]{1,0:T(4,128)(2,1)S(1)}, bf16[4,2048]{1,0:T(4,128)(2,1)S(1)}, bf16[3,2048]{1,0:T(4,128)(2,1)S(1)}, bf16[2048]{0:T(1024)(128)(2,1)S(1)}) all-reduce(bf16[4,2048]{1,0:T(4,128)(2,1)S(1)} %get-tuple-element.190, bf16[4,2048]{1,0:T(4,128)(2,1)S(1)} %get-tuple-element.191, ...), channel_id=1, replica_groups=mesh['dp'=8,'mp'=4] {'dp'}, use_global_device_ids=true, to_apply=%region_40.41 | all-reduce | flops 24576 | bytes 98304 | tf_op jit(solution)/shard_map/psum | solution.py:251
  1324.1 5.6 add_add_fusion.4
  1329.7 20.7 reduce-scatter.15.cloned.1.call-done
  1352.2 31.3 %reduce-scatter.9.cloned.1.call-done = bf16[256,1024]{1,0:T(8,128)(2,1)} async-done(((bf16[256,4096]{1,0:T(8,128)(2,1)}), bf16[256,1024]{1,0:T(8,128)(2,1)}) %reduce-scatter.9.cloned.1.call-update) | async-done | bytes 524304 | tf_op jit(solution)/shard_map/reduce_scatter | solution.py:209
  1385.6 70.2 %reduce-scatter.19.cloned.1.call-done = bf16[512,256]{1,0:T(8,128)(2,1)} async-done(((bf16[512,2048]{1,0:T(8,128)(2,1)}), bf16[512,256]{1,0:T(8,128)(2,1)}) %reduce-scatter.19.cloned.1.call-update) | async-done | bytes 262160 | tf_op jit(solution)/shard_map/reduce_scatter | solution.py:269
  1457.6 70.1 %reduce-scatter.13.cloned.1.call-done = bf16[512,256]{1,0:T(8,128)(2,1)} async-done(((bf16[512,2048]{1,0:T(8,128)(2,1)}), bf16[512,256]{1,0:T(8,128)(2,1)}) %reduce-scatter.13.cloned.1.call-update) | async-done | bytes 262160 | tf_op jit(solution)/shard_map/reduce_scatter | solution.py:260
  1529.5 148.7 %reduce-scatter.23.cloned.1.call-done = bf16[2048,256]{1,0:T(8,128)(2,1)} async-done(((bf16[2048,2048]{1,0:T(8,128)(2,1)}), bf16[2048,256]{1,0:T(8,128)(2,1)}) %reduce-scatter.23.cloned.1.call-update) | async-done | bytes 1048592 | tf_op jit(solution)/shard_map/reduce_scatter | solution.py:275
  1680.9 147.4 %reduce-scatter.21.cloned.1.call-done = bf16[256,2048]{1,0:T(8,128)(2,1)} async-done(((bf16[2048,2048]{1,0:T(8,128)(2,1)}), bf16[256,2048]{1,0:T(8,128)(2,1)}) %reduce-scatter.21.cloned.1.call-update) | async-done | bytes 1048592 | tf_op jit(solution)/shard_map/reduce_scatter | solution.py:272
  1831.0 118.4 %reduce-scatter.11.cloned.1.call-done = bf16[3,256,512]{1,2,0:T(8,128)(2,1)} async-done(((bf16[3,2048,512]{1,2,0:T(8,128)(2,1)}), bf16[3,256,512]{1,2,0:T(8,128)(2,1)}) %reduce-scatter.11.cloned.1.call-update) | async-done | bytes 786448 | tf_op jit(solution)/shard_map/reduce_scatter | solution.py:257
  1952.0 148.2 %reduce-scatter.17.cloned.1.call-done = bf16[2,512,512]{1,2,0:T(8,128)(2,1)} async-done(((bf16[2,4096,512]{1,2,0:T(8,128)(2,1)}), bf16[2,512,512]{1,2,0:T(8,128)(2,1)}) %reduce-scatter.17.cloned.1.call-update) | async-done | bytes 1048592 | tf_op jit(solution)/shard_map/reduce_scatter | solution.py:266
  (249 shorter events, 97.7 us)
Async XLA Ops:
  7.2 5.3 copy-start.6
  7.2 6.0 copy-start.42
  7.2 6.6 copy-start.40
  7.2 6.6 copy-start.41
  7.2 105.7 %all-gather.9.cloned.1.call-start = ((), (), s32[]{:S(2)}) async-start(), calls=%async_computation.8 | async-start | bytes 7077888 | tf_op jit(solution)/shard_map/all_gather | solution.py:112
  9.7 153.8 %all-gather.11.cloned.1.call-start = ((), (), s32[]{:S(2)}) async-start(), calls=%async_computation.9 | async-start | bytes 2359296 | tf_op jit(solution)/shard_map/all_gather | solution.py:113
  10.5 241.7 %all-reduce.8.cloned.1.call-start = ((), (), s32[]{:S(2)}) async-start(), calls=%async_computation.10 | async-start | bytes 8388608 | tf_op jit(solution)/shard_map/psum | solution.py:28
  12.5 107.0 %copy-start.38 = (f32[512]{0:T(512)}, f32[512]{0:T(512)S(1)}, u32[]{:S(2)}) copy-start(f32[512]{0:T(512)S(1)} %broadcast_multiply_fusion.3) | copy-start | bytes 6148
  13.8 105.7 %copy-start.43 = (f32[512]{0:T(512)}, f32[512]{0:T(512)S(1)}, u32[]{:S(2)}) copy-start(f32[512]{0:T(512)S(1)} %fusion.58) | copy-start | bytes 6148
  13.8 105.7 %copy-start.36 = (f32[1,2048]{1,0:T(1,128)}, f32[1,2048]{1,0:T(1,128)S(1)}, u32[]{:S(2)}) copy-start(f32[1,2048]{1,0:T(1,128)S(1)} %get-tuple-element.171) | copy-start | bytes 24580
  13.9 105.6 %copy-start.48 = (f32[1,2048]{1,0:T(1,128)}, f32[1,2048]{1,0:T(1,128)S(1)}, u32[]{:S(2)}) copy-start(f32[1,2048]{1,0:T(1,128)S(1)} %get-tuple-element.175) | copy-start | bytes 24580
  124.3 39.2 %copy-start.32 = (bf16[4,128,512]{2,1,0:T(8,128)(2,1)}, bf16[4,128,512]{2,1,0:T(8,128)(2,1)S(1)}, u32[]{:S(2)}) copy-start(bf16[4,128,512]{2,1,0:T(8,128)(2,1)S(1)} %fusion.45) | copy-start | bytes 1572868
  168.4 3.6 copy-start.45
  168.4 3.6 copy-start.50
  168.4 135.1 %all-gather.17.cloned.1.call-start = ((), (), s32[]{:S(2)}) async-start(), calls=%async_computation.13 | async-start | bytes 2359296 | tf_op jit(solution)/shard_map/all_gather | solution.py:114
  169.0 157.0 %all-gather.15.cloned.1.call-start = ((), (), s32[]{:S(2)}) async-start(), calls=%async_computation.12 | async-start | bytes 2621440 | tf_op jit(solution)/shard_map/all_gather | solution.py:121
  169.6 283.9 %all-gather.13.cloned.1.call-start = ((), (), s32[]{:S(2)}) async-start(), calls=%async_computation.11 | async-start | bytes 9437184 | tf_op jit(solution)/shard_map/all_gather | solution.py:115
  171.0 333.1 %all-gather.19.cloned.1.call-start = ((), (), s32[]{:S(2)}) async-start(), calls=%async_computation.14 | async-start | bytes 2359296 | tf_op jit(solution)/shard_map/all_gather | solution.py:116
  171.7 421.0 %all-reduce.10.cloned.1.call-start = ((), (), s32[]{:S(2)}) async-start(), calls=%async_computation.15 | async-start | bytes 8388608 | tf_op jit(solution)/shard_map/psum | solution.py:28
  257.8 48.5 %copy-start.28 = (bf16[512,2048]{1,0:T(8,128)(2,1)}, bf16[512,2048]{1,0:T(8,128)(2,1)S(1)}, u32[]{:S(2)}) copy-start(bf16[512,2048]{1,0:T(8,128)(2,1)S(1)} %add_convert_fusion.2) | copy-start | bytes 6291460
  306.4 153.5 %copy-start.26 = (bf16[512,512]{0,1:T(8,128)(2,1)}, bf16[512,512]{0,1:T(8,128)(2,1)S(1)}, u32[]{:S(2)}) copy-start(bf16[512,512]{0,1:T(8,128)(2,1)S(1)} %convolution_convert_fusion.9) | copy-start | bytes 1572868
  461.3 47.6 %copy-start.34 = (bf16[4,128,512]{2,1,0:T(8,128)(2,1)}, bf16[4,128,512]{2,1,0:T(8,128)(2,1)S(1)}, u32[]{:S(2)}) copy-start(bf16[4,128,512]{2,1,0:T(8,128)(2,1)S(1)} %convolution_convert_fusion.8) | copy-start | bytes 1572868
  508.9 210.6 %all-gather.21.cloned.1.call-start = ((), (), s32[]{:S(2)}) async-start(), calls=%async_computation.16 | async-start | bytes 9437184 | tf_op jit(solution)/shard_map/all_gather | solution.py:117
  509.6 334.9 %all-gather.23.cloned.1.call-start = ((), (), s32[]{:S(2)}) async-start(), calls=%async_computation.17 | async-start | bytes 9437184 | tf_op jit(solution)/shard_map/all_gather | solution.py:118
  510.2 429.7 %all-reduce.12.cloned.1.call-start = ((), (), s32[]{:S(2)}) async-start(), calls=%async_computation.18 | async-start | bytes 8388608 | tf_op jit(solution)/shard_map/psum | solution.py:28
  719.5 125.0 %copy-start.51 = (f32[2048]{0:T(1024)S(1)}, f32[2048]{0:T(1024)}, u32[]{:S(2)}) copy-start(f32[2048]{0:T(1024)} %param.30) | copy-start | bytes 24580
  856.1 199.1 %all-reduce.14.cloned.1.call-start = ((), (), s32[]{:S(2)}) async-start(), calls=%async_computation.19 | async-start | bytes 8388608 | tf_op jit(solution)/shard_map/psum | solution.py:32
  947.0 16.3 slice-start
  949.9 12.0 copy-start.10
  949.9 13.3 slice-start.1
  969.4 188.3 %all-reduce.16.cloned.1.call-start = ((), (), s32[]{:S(2)}) async-start(), calls=%async_computation.20 | async-start | bytes 8388608 | tf_op jit(solution)/shard_map/psum | solution.py:32
  1055.2 4.8 copy-start.5
  1055.2 5.9 copy-start.15
  1071.9 205.7 %all-reduce.18.cloned.1.call-start = ((), (), s32[]{:S(2)}) async-start(), calls=%async_computation.21 | async-start | bytes 8388608 | tf_op jit(solution)/shard_map/psum | solution.py:32
  1157.7 4.7 copy-start.1
  1157.7 5.9 copy-start.14
  1166.4 3.9 copy-start.3
  1191.8 158.6 %reduce-scatter.15.cloned.1.call-start = ((), (), s32[]{:S(2)}) async-start(), calls=%async_computation.25 | async-start | bytes 2359296 | tf_op jit(solution)/shard_map/reduce_scatter | solution.py:263
  1196.2 187.3 %reduce-scatter.9.cloned.1.call-start = ((), (), s32[]{:S(2)}) async-start(), calls=%async_computation.22 | async-start | bytes 2621440 | tf_op jit(solution)/shard_map/reduce_scatter | solution.py:209
  1201.6 7.3 copy-start.35
  1208.8 5.0 copy-start.33
  1208.8 247.0 %reduce-scatter.19.cloned.1.call-start = ((), (), s32[]{:S(2)}) async-start(), calls=%async_computation.27 | async-start | bytes 2359296 | tf_op jit(solution)/shard_map/reduce_scatter | solution.py:269
  1213.8 313.9 %reduce-scatter.13.cloned.1.call-start = ((), (), s32[]{:S(2)}) async-start(), calls=%async_computation.24 | async-start | bytes 2359296 | tf_op jit(solution)/shard_map/reduce_scatter | solution.py:260
  1218.7 459.5 %reduce-scatter.23.cloned.1.call-start = ((), (), s32[]{:S(2)}) async-start(), calls=%async_computation.29 | async-start | bytes 9437184 | tf_op jit(solution)/shard_map/reduce_scatter | solution.py:275
  1231.2 597.1 %reduce-scatter.21.cloned.1.call-start = ((), (), s32[]{:S(2)}) async-start(), calls=%async_computation.28 | async-start | bytes 9437184 | tf_op jit(solution)/shard_map/reduce_scatter | solution.py:272
  1242.3 707.1 %reduce-scatter.11.cloned.1.call-start = ((), (), s32[]{:S(2)}) async-start(), calls=%async_computation.23 | async-start | bytes 7077888 | tf_op jit(solution)/shard_map/reduce_scatter | solution.py:257
  1251.3 848.9 %reduce-scatter.17.cloned.1.call-start = ((), (), s32[]{:S(2)}) async-start(), calls=%async_computation.26 | async-start | bytes 9437184 | tf_op jit(solution)/shard_map/reduce_scatter | solution.py:266
  1258.5 22.4 %copy-start.47 = (f32[512]{0:T(512)S(1)}, f32[512]{0:T(512)}, u32[]{:S(2)}) copy-start(f32[512]{0:T(512)} %copy-done.46) | copy-start | bytes 6148
  (31 other events, 58.3 us)
Sparse Core Ops, SparseCore 0:
  10.6 102.1 all-gather.8
  114.9 48.5 all-gather.10
  168.5 83.6 all-reduce.7
  254.2 49.2 all-gather.16
  304.9 21.0 all-gather.14
  328.5 124.9 all-gather.12
  455.5 48.5 all-gather.18
  509.0 83.6 all-reduce.9
  594.8 124.6 all-gather.20
  721.4 123.1 all-gather.22
  856.2 83.6 all-reduce.11
  969.5 85.6 all-reduce.13
  1072.1 85.6 all-reduce.15
  1192.0 85.6 all-reduce.17
  1281.6 68.7 reduce-scatter.14
  1353.4 30.1 reduce-scatter.8
  1386.9 68.8 reduce-scatter.18
  1459.8 67.8 reduce-scatter.12
  1531.3 146.8 reduce-scatter.22
  1681.7 146.5 reduce-scatter.20
  1831.9 117.5 reduce-scatter.10
  1953.1 147.0 reduce-scatter.16
where the time goes:
time: 2120 us; the launch traced here: 2110 us
  waiting for transfers between devices  1800 us (85%)
  matrix products  151 us (7%)
  other arithmetic  65.1 us (3%)
  blocking collectives  38.5 us (2%)
  local copies, waits for them, and re-layouts  36.7 us (2%)
    psum x3, waiting for transfers between devices, heads_sum(): return lax.psum(partial_value, 'mp')  246 us
    psum x3, waiting for transfers between devices, input_sum(): return lax.psum(partial_value, 'mp')  188 us
    reduce_scatter x1, waiting for transfers between devices, on_device(): lax.psum_scatter(grad_down.astype(jnp.bfloat16), 'dp', scatter_dimension=...  149 us
    reduce_scatter x1, waiting for transfers between devices, on_device(): lax.psum_scatter(grad_ckv.astype(jnp.bfloat16), 'dp', scatter_dimension=1...  148 us
    reduce_scatter x1, waiting for transfers between devices, on_device(): lax.psum_scatter(grad_up.astype(jnp.bfloat16), 'dp', scatter_dimension=0,...  147 us
    all_gather x1, waiting for transfers between devices, on_device(): lax.all_gather(c_kv, 'dp', axis=1, tiled=True)  127 us
    all_gather x1, waiting for transfers between devices, on_device(): lax.all_gather(w_up, 'dp', axis=0, tiled=True)  120 us
    reduce_scatter x1, waiting for transfers between devices, on_device(): lax.psum_scatter(grad_qkv.astype(jnp.bfloat16), 'dp', scatter_dimension=1...  118 us
  transfers between devices with their start and end apart: 22, of which 22 were waited for; matrix products, arithmetic and copies ran while one was open for 7% of the time, Pallas kernels for 0%

commit v1 on v0

v1 whole, which is shorter than its diff:
```python
import jax
import jax.numpy as jnp
from jax import lax
from jax.experimental import pallas as pl
from jax.experimental.pallas import tpu as pltpu
from jax.sharding import PartitionSpec as P

HD = 128
BOTH = ("dp", "mp")

eps = 1e-05
masked = -1e30
f32 = jnp.float32
bf16 = jnp.bfloat16


def normalize(values, gain, shift):
    center = values - jnp.mean(values, axis=-1, keepdims=True)
    spread = jnp.mean(center * center, axis=-1, keepdims=True)
    return center * lax.rsqrt(spread + eps) * gain + shift


def gelu_tanh(values):
    return (
        0.5
        * values
        * (1.0 + jnp.tanh(0.7978845608028654 * (values + 0.044715 * values * values * values)))
    )


def dot(left, right, contract):
    return lax.dot_general(left, right, (contract, ((), ())), preferred_element_type=f32)


def softmax_of(q, k, q_seg, k_seg):
    scores = dot(q, k, ((1,), (1,))) * HD ** (-0.5)
    scores = jnp.where(q_seg == k_seg, scores, masked)
    top = jnp.max(scores, axis=-1, keepdims=True)
    expo = jnp.exp(scores - top)
    return expo / jnp.sum(expo, axis=-1, keepdims=True)


def forward_kernel(q_ref, k_ref, v_ref, qs_ref, ks_ref, o_ref):
    probs = softmax_of(q_ref[...], k_ref[...], qs_ref[...], ks_ref[...]).astype(bf16)
    o_ref[...] = dot(probs, v_ref[...], ((1,), (0,))).astype(bf16)


def backward_kernel(q_ref, k_ref, v_ref, g_ref, qs_ref, ks_ref, dq_ref, dk_ref, dv_ref):
    q, k, v, g = q_ref[...], k_ref[...], v_ref[...], g_ref[...]
    probs = softmax_of(q, k, qs_ref[...], ks_ref[...])
    dv_ref[...] = dot(probs.astype(bf16), g, ((0,), (0,))).astype(bf16)
    grad_probs = dot(g, v, ((1,), (1,)))
    shift = jnp.sum(probs * grad_probs, axis=-1, keepdims=True)
    grad_scores = (probs * (grad_probs - shift)).astype(bf16)
    dq_ref[...] = (dot(grad_scores, k, ((1,), (0,))) * HD ** (-0.5)).astype(bf16)
    dk_ref[...] = (dot(grad_scores, q, ((0,), (0,))) * HD ** (-0.5)).astype(bf16)


def column(rows, offset):
    return pl.BlockSpec((rows, HD), lambda h: (0, offset + h))


def whole(shape):
    return pl.BlockSpec(shape, lambda h: (0, 0))


def attend(q, q_at, k, k_at, v, v_at, q_seg, k_seg, heads):
    nq, nk = q.shape[0], k.shape[0]
    return pl.pallas_call(
        forward_kernel,
        grid=(heads,),
        in_specs=[
            column(nq, q_at),
            column(nk, k_at),
            column(nk, v_at),
            whole((nq, 1)),
            whole((1, nk)),
        ],
        out_specs=column(nq, 0),
        out_shape=jax.ShapeDtypeStruct((nq, heads * HD), bf16),
    )(q, k, v, q_seg, k_seg)


def attend_back(q, q_at, k, k_at, v, v_at, grad, q_seg, k_seg, heads):
    nq, nk = q.shape[0], k.shape[0]
    wide = heads * HD
    return pl.pallas_call(
        backward_kernel,
        grid=(heads,),
        in_specs=[
            column(nq, q_at),
            column(nk, k_at),
            column(nk, v_at),
            column(nq, 0),
            whole((nq, 1)),
            whole((1, nk)),
        ],
        out_specs=[column(nq, 0), column(nk, 0), column(nk, 0)],
        out_shape=[
            jax.ShapeDtypeStruct((nq, wide), bf16),
            jax.ShapeDtypeStruct((nk, wide), bf16),
            jax.ShapeDtypeStruct((nk, wide), bf16),
        ],
    )(q, k, v, grad, q_seg, k_seg)


def pick(values, index, axis=0):
    return lax.dynamic_index_in_dim(values, index, axis, keepdims=False)


def build(n_dp, n_mp):
    n_hi = n_dp // 4
    flip = {bit: [(i, i ^ bit) for i in range(n_dp)] for bit in (1, 2, 4)}
    core_swap = [(i, i ^ 1) for i in range(n_mp)]
    side = lambda i, m: i * n_mp + (m ^ 2)
    lower = lambda i, m: (i ^ 2) * n_mp + m
    pairs = [(i, m) for i in range(n_dp) for m in range(n_mp)]
    first_hop = [(i * n_mp + m, side(i, m) if m % 2 == 0 else lower(i, m)) for i, m in pairs]
    second_hop = [(i * n_mp + m, lower(i, m) if m % 2 == 0 else side(i, m)) for i, m in pairs]
    high_groups = [[h * 4 + low for h in range(n_hi)] for low in range(4)]

    def gather_tokens(own):
        near = lax.ppermute(own, BOTH, first_hop)
        two = jnp.concatenate([own, near], axis=0)
        four = jnp.concatenate([two, lax.ppermute(two, BOTH, second_hop)], axis=0)
        return jnp.concatenate([four, lax.ppermute(four, "mp", core_swap)], axis=0)

    def scatter_tokens(partial):
        part = partial.shape[0] // 8
        arrived = lax.ppermute(partial[4 * part :], "mp", core_swap)
        four = partial[: 4 * part].astype(f32) + arrived.astype(f32)
        arrived = lax.ppermute(four[2 * part :].astype(bf16), BOTH, second_hop)
        two = four[: 2 * part] + arrived.astype(f32)
        arrived = lax.ppermute(two[part:].astype(bf16), BOTH, first_hop)
        return two[:part] + arrived.astype(f32)

    def on_device(
        tokens,
        text,
        image_seg,
        text_seg,
        w_qkv,
        w_out,
        c_q,
        c_kv,
        c_out,
        w_up,
        w_down,
        norm_gain,
        norm_bias,
        out_bias,
        up_bias,
        cotangent,
    ):
        d, m = lax.axis_index("dp"), lax.axis_index("mp")
        high, low, near_y = d // 4, (d // 2) % 2, d % 2
        core = m % 2
        seq, dim = tokens.shape
        text_len = text_seg.shape[1]
        block = seq // 8
        place = low * 4 + m

        def ordered(mine, theirs, axis=0):
            return jnp.where(
                low == 0, jnp.stack([mine, theirs], axis), jnp.stack([theirs, mine], axis)
            )

        def swap_low(values):
            return lax.ppermute(values, "dp", flip[2])

        def spread(halves):
            rows, wide = halves.shape[1:]
            pair = ordered(pick(halves, low), swap_low(pick(halves, 1 - low)))
            if n_hi == 2:
                far = lax.ppermute(pair, "dp", flip[4])
                pair_y = lax.ppermute(pair, "dp", flip[1])
                far_y = lax.ppermute(far, "dp", flip[1])
                full = jnp.zeros((2, 2, 2, rows, wide), halves.dtype)
                for piece, h, y in (
                    (pair, high, near_y),
                    (far, 1 - high, near_y),
                    (pair_y, high, 1 - near_y),
                    (far_y, 1 - high, 1 - near_y),
                ):
                    full = lax.dynamic_update_slice(full, piece[None, :, None], (h, 0, y, 0, 0))
            else:
                mine = lax.all_gather(pair, "dp", axis=0, axis_index_groups=high_groups)
                theirs = lax.ppermute(mine, "dp", flip[1])
                full = jnp.where(
                    near_y == 0, jnp.stack([mine, theirs], 2), jnp.stack([theirs, mine], 2)
                )
            return full.reshape(n_dp * rows, wide)

        def collect(grad):
            rows, wide = grad.shape[0] // n_dp, grad.shape[1]
            grad = grad.reshape(n_hi, 2, 2, rows, wide)
            arrived = lax.ppermute(pick(grad, 1 - near_y, 2), "dp", flip[1])
            total = (pick(grad, near_y, 2).astype(f32) + arrived.astype(f32)).astype(bf16)
            if n_hi == 2:
                arrived = lax.ppermute(pick(total, 1 - high), "dp", flip[4])
                total = (pick(total, high).astype(f32) + arrived.astype(f32)).astype(bf16)
            else:
                total = lax.psum_scatter(
                    total, "dp", scatter_dimension=0, axis_index_groups=high_groups
                )
            theirs = swap_low(pick(total, 1 - low))
            return ordered(pick(total, low), theirs, 1).astype(f32)

        halve = lambda v: jnp.moveaxis(v.reshape(v.shape[0], 2, v.shape[1] // 2), 1, 0)
        qkv_halves = w_qkv.reshape(3, w_qkv.shape[1], 2, w_qkv.shape[2] // 2)
        qkv_halves = qkv_halves.transpose(2, 1, 0, 3).reshape(2, w_qkv.shape[1], -1)
        kv_halves = c_kv.reshape(2, c_kv.shape[1], 2, c_kv.shape[2] // 2)
        kv_halves = kv_halves.transpose(2, 1, 0, 3).reshape(2, c_kv.shape[1], -1)
        proj_halves = jnp.concatenate([halve(w_out.T), halve(c_q), halve(c_out.T)], axis=2)
        full_qkv = spread(qkv_halves)
        full_proj = spread(proj_halves)
        full_kv = spread(kv_halves)
        full_up = spread(halve(w_up))
        full_down = spread(halve(w_down.T))
        mine = proj_halves.shape[2] // 3
        heads = mine // HD
        full_out, full_cq, full_cout = (
            full_proj[:, :mine],
            full_proj[:, mine : 2 * mine],
            full_proj[:, 2 * mine :],
        )
        hidden = full_up.shape[1]
        bias_up = lax.dynamic_slice(up_bias, (low * hidden,), (hidden,))

        local = jnp.stack([tokens, cotangent])
        own = lax.dynamic_slice(local, (0, place * block, 0), (2, block, dim))
        away = lax.dynamic_slice(
            local, (0, ((1 - low) * 4 + m) * block, 0), (2, block, dim)
        )
        both = ordered(own, swap_low(away))
        segs = jnp.concatenate([image_seg[0], text_seg[0]])
        segs = ordered(segs, swap_low(segs))
        order = jnp.where(
            core == 0,
            jnp.array([0, 2, 4, 6, 1, 5, 3, 7], jnp.int32),
            jnp.array([0, 4, 2, 6, 1, 3, 5, 7], jnp.int32),
        )
        image_ids = jnp.take(segs[:, :seq].reshape(2, 8, block), place ^ order, axis=1)
        image_ids = image_ids.reshape(2, seq)
        text_ids = segs[:, seq:]
        words = lax.all_gather(ordered(text, swap_low(text)), "mp", axis=2, tiled=True)

        rows = (0, 1)
        residual = [both[r, 0].astype(f32) for r in rows]
        upstream = [both[r, 1].astype(f32) for r in rows]
        q_ids = [image_ids[r].reshape(seq, 1) for r in rows]
        i_ids = [image_ids[r].reshape(1, seq) for r in rows]
        t_ids = [text_ids[r].reshape(1, text_len) for r in rows]

        def norm(values, which):
            out, pull = jax.vjp(normalize, values, norm_gain[which], norm_bias[which])
            return out.astype(bf16), pull

        pulls = [[None] * 2 for _ in range(4)]
        hid_one, qkv, mixed, after_self = [], [], [], []
        for r in rows:
            normed, pulls[0][r] = norm(residual[r], 0)
            hid_one.append(gather_tokens(normed))
        for r in rows:
            qkv.append(dot(hid_one[r], full_qkv, ((1,), (0,))).astype(bf16))
            mixed.append(
                attend(qkv[r], 0, qkv[r], heads, qkv[r], 2 * heads, q_ids[r], i_ids[r], heads)
            )
            partial = dot(mixed[r], full_out, ((1,), (1,))).astype(bf16)
            after_self.append(residual[r] + scatter_tokens(partial) + out_bias[0])
        hid_two, cross_q, cross_kv, cross_mixed, after_cross = [], [], [], [], []
        for r in rows:
            cross_kv.append(dot(words[r], full_kv, ((1,), (0,))).astype(bf16))
        for r in rows:
            normed, pulls[1][r] = norm(after_self[r], 1)
            hid_two.append(gather_tokens(normed))
        for r in rows:
            cross_q.append(dot(hid_two[r], full_cq, ((1,), (0,))).astype(bf16))
            cross_mixed.append(
                attend(
                    cross_q[r], 0, cross_kv[r], 0, cross_kv[r], heads, q_ids[r], t_ids[r], heads
                )
            )
            partial = dot(cross_mixed[r], full_cout, ((1,), (1,))).astype(bf16)
            after_cross.append(after_self[r] + scatter_tokens(partial) + out_bias[1])
        hid_three, pre_act, act, after_mlp = [], [], [], []
        for r in rows:
            normed, pulls[2][r] = norm(after_cross[r], 2)
            hid_three.append(gather_tokens(normed))
        for r in rows:
            pre_act.append(dot(hid_three[r], full_up, ((1,), (0,))) + bias_up)
            act.append(gelu_tanh(pre_act[r]).astype(bf16))
            partial = dot(act[r], full_down, ((1,), (1,))).astype(bf16)
            after_mlp.append(after_cross[r] + scatter_tokens(partial) + out_bias[2])

        gains, shifts, biases = [0.0] * 4, [0.0] * 4, [0.0] * 3

        def back_norm(which, r, grad):
            out, gain, shift = pulls[which][r](grad)
            gains[which] = gains[which] + gain
            shifts[which] = shifts[which] + shift
            return out

        outs, grad_mlp, low_mlp = [], [], []
        for r in rows:
            final, pulls[3][r] = norm(after_mlp[r], 3)
            outs.append(final)
            grad_mlp.append(back_norm(3, r, upstream[r]))
            biases[2] = biases[2] + jnp.sum(grad_mlp[r], axis=0)
            low_mlp.append(gather_tokens(grad_mlp[r].astype(bf16)))
        grad_pre, grad_after_cross, low_cross = [], [], []
        for r in rows:
            grad_act = dot(low_mlp[r], full_down, ((1,), (0,)))
            grad_pre.append(jax.vjp(gelu_tanh, pre_act[r])[1](grad_act)[0].astype(bf16))
            partial = dot(grad_pre[r], full_up, ((1,), (1,))).astype(bf16)
            grad_in = scatter_tokens(partial)
            grad_after_cross.append(grad_mlp[r] + back_norm(2, r, grad_in))
            biases[1] = biases[1] + jnp.sum(grad_after_cross[r], axis=0)
            low_cross.append(gather_tokens(grad_after_cross[r].astype(bf16)))

        def weight_grad(left, right):
            return (
                dot(left[0], right[0], ((0,), (0,))) + dot(left[1], right[1], ((0,), (0,)))
            ).astype(bf16)

        sum_down = collect(weight_grad(low_mlp, act))
        sum_up = collect(weight_grad(hid_three, grad_pre))
        up_grad = jnp.sum(grad_pre[0].astype(f32), axis=0) + jnp.sum(
            grad_pre[1].astype(f32), axis=0
        )
        cq_low, ckv_low, grad_after_self, low_self = [], [], [], []
        for r in rows:
            grad_mixed = dot(low_cross[r], full_cout, ((1,), (0,))).astype(bf16)
            dq, dk, dv = attend_back(
                cross_q[r],
                0,
                cross_kv[r],
                0,
                cross_kv[r],
                heads,
                grad_mixed,
                q_ids[r],
                t_ids[r],
                heads,
            )
            cq_low.append(dq)
            ckv_low.append(jnp.concatenate([dk, dv], axis=1))
            partial = dot(dq, full_cq, ((1,), (1,))).astype(bf16)
            grad_in = scatter_tokens(partial)
            grad_after_self.append(grad_after_cross[r] + back_norm(1, r, grad_in))
            biases[0] = biases[0] + jnp.sum(grad_after_self[r], axis=0)
            low_self.append(gather_tokens(grad_after_self[r].astype(bf16)))
        sum_cross = collect(
            jnp.concatenate([weight_grad(hid_two, cq_low), weight_grad(low_cross, cross_mixed)], 1)
        )
        sum_kv = collect(weight_grad([words[0], words[1]], ckv_low))
        text_term = jnp.stack([dot(ckv_low[r], full_kv, ((1,), (1,))).astype(bf16) for r in rows])
        text_term = lax.psum_scatter(text_term, "mp", scatter_dimension=2, tiled=True)
        grad_text = pick(text_term, low).astype(f32) + swap_low(
            pick(text_term, 1 - low)
        ).astype(f32)
        qkv_low, grad_tokens = [], []
        for r in rows:
            grad_mixed = dot(low_self[r], full_out, ((1,), (0,))).astype(bf16)
            dq, dk, dv = attend_back(
                qkv[r],
                0,
                qkv[r],
                heads,
                qkv[r],
                2 * heads,
                grad_mixed,
                q_ids[r],
                i_ids[r],
                heads,
            )
            qkv_low.append(jnp.concatenate([dq, dk, dv], axis=1))
            partial = dot(qkv_low[r], full_qkv, ((1,), (1,))).astype(bf16)
            grad_in = scatter_tokens(partial)
            grad_tokens.append(grad_after_self[r] + back_norm(0, r, grad_in))
        sum_out = collect(weight_grad(low_self, mixed))
        sum_qkv = collect(weight_grad(hid_one, qkv_low))

        def whole_row(pieces):
            pieces = jnp.stack(pieces)
            pieces = ordered(pick(pieces, low), swap_low(pick(pieces, 1 - low)))
            pieces = lax.all_gather(pieces, "mp", axis=1)
            return pieces.reshape(seq, dim)

        output = whole_row(outs)
        grad_tokens = whole_row([piece.astype(bf16) for piece in grad_tokens]).astype(f32)

        small = jnp.concatenate([jnp.stack(gains), jnp.stack(shifts), jnp.stack(biases)]).reshape(-1)
        ups = lax.dynamic_update_slice(
            jnp.zeros((n_mp * 2 * hidden,), f32), up_grad, ((m * 2 + low) * hidden,)
        )
        small = lax.psum(jnp.concatenate([small, ups]), BOTH)
        gain_total = small[: 4 * dim].reshape(4, dim)
        shift_total = small[4 * dim : 8 * dim].reshape(4, dim)
        bias_total = small[8 * dim : 11 * dim].reshape(3, dim)
        up_total = lax.dynamic_slice(small, (11 * dim + m * 2 * hidden,), (2 * hidden,))

        flat = lambda v: v.reshape(v.shape[0], -1)
        apart = lambda v, n: v.reshape(v.shape[0], 2, n, -1).transpose(2, 0, 1, 3)
        cross_parts = apart(sum_cross, 2)
        qkv_parts = apart(sum_qkv, 3)
        kv_parts = apart(sum_kv, 2)
        return (
            output,
            grad_tokens,
            grad_text,
            qkv_parts.reshape(w_qkv.shape),
            flat(sum_out).T,
            flat(cross_parts[0]),
            kv_parts.reshape(c_kv.shape),
            flat(cross_parts[1]).T,
            flat(sum_up),
            flat(sum_down).T,
            gain_total,
            shift_total,
            bias_total,
            up_total,
        )

    return on_device


def solution(mesh):
    in_specs = (
        P("dp", None),
        P("dp", "mp"),
        P("dp", None),
        P("dp", None),
        P(None, "dp", "mp"),
        P("mp", "dp"),
        P("dp", "mp"),
        P(None, "dp", "mp"),
        P("mp", "dp"),
        P("dp", "mp"),
        P("mp", "dp"),
        P(),
        P(),
        P(),
        P("mp"),
        P("dp", None),
    )
    out_specs = (
        P("dp", None),
        P("dp", None),
        P("dp", "mp"),
        P(None, "dp", "mp"),
        P("mp", "dp"),
        P("dp", "mp"),
        P(None, "dp", "mp"),
        P("mp", "dp"),
        P("dp", "mp"),
        P("mp", "dp"),
        P(),
        P(),
        P(),
        P("mp"),
    )
    return jax.shard_map(
        build(mesh.shape["dp"], mesh.shape["mp"]),
        mesh=mesh,
        in_specs=in_specs,
        out_specs=out_specs,
        check_vma=False,
    )
```

time: 2120 us -> 1160 us (0.55)
  waiting for transfers between devices: 1800 us -> 579 us
  local copies, waits for them, and re-layouts: 36.7 us -> 161 us
  starting transfers between devices: 2.63 us -> 96.1 us
  other arithmetic: 65.1 us -> 118 us
  blocking collectives: 38.5 us -> 0 us
  Pallas kernels: 0 us -> 34.1 us
    reduce_scatter x8 -> x1, waiting for transfers between devices: 755 us -> 0.01 us  [on_device(): lax.psum_scatter(text_term, 'mp', scatter_dimension=2, tiled=True)]
    all_gather x8 -> x3, waiting for transfers between devices: 608 us -> 16.4 us  [the longest x2 16.4 us: whole_row(): pieces = lax.all_gather(pieces, 'mp', axis=1)]
    ppermute x0 -> x116, waiting for transfers between devices: none -> 491 us  [the longest x12 138 us: scatter_tokens(): arrived = lax.ppermute(four[2 * part:].astype(bf16), BOTH, second_hop)]
    psum x6 -> x1, waiting for transfers between devices: 433 us -> 71.4 us  [on_device(): small = lax.psum(jnp.concatenate([small, ups]), BOTH)]
    ppermute x0 -> x116, starting transfers between devices: none -> 95.9 us  [the longest x17 16.7 us: swap_low(): return lax.ppermute(values, 'dp', flip[2])]
    psum x1 -> x0, blocking collectives: 38.5 us -> none  [on_device(): lax.psum(gain_terms.astype(jnp.bfloat16), 'dp').astype(jnp.float32)]
    pallas_call x0 -> x8, Pallas kernels: none -> 34.1 us  [the longest x4 18.5 us: attend_back(): pl.pallas_call(backward_kernel, grid=(heads,), in_specs=[column(nq, q_at)...]
    concatenate x0 -> x28, other arithmetic: none -> 31.9 us  [the longest x12 18.7 us: gather_tokens(): four = jnp.concatenate([two, lax.ppermute(two, BOTH, second_hop)], axis=0)]
  transfers between devices with their start and end apart: 22 -> 121, of which waited for: 22 -> 50; matrix products, arithmetic and copies ran while one was open for 7% -> 33% of each run, Pallas kernels for 0% -> 3%
where the time goes in v1:
time: 1160 us; the launch traced here: 1150 us
  waiting for transfers between devices  579 us (50%)
  local copies, waits for them, and re-layouts  161 us (14%)
  matrix products  143 us (12%)
  other arithmetic  118 us (10%)
  starting transfers between devices  96.1 us (8%)
  Pallas kernels  34.1 us (3%)
  between operations  17.6 us (2%)
    dot_general x42, matrix products, dot(): lax.dot_general(left, right, (contract, ((), ())), preferred_element_type...  143 us
    ppermute x12, waiting for transfers between devices, scatter_tokens(): arrived = lax.ppermute(four[2 * part:].astype(bf16), BOTH, second_hop)  138 us
    psum x1, waiting for transfers between devices, on_device(): small = lax.psum(jnp.concatenate([small, ups]), BOTH)  71.4 us
    ppermute x6, waiting for transfers between devices, collect(): arrived = lax.ppermute(pick(total, 1 - high), 'dp', flip[4])  64 us
    ppermute x6, waiting for transfers between devices, collect(): arrived = lax.ppermute(pick(grad, 1 - near_y, 2), 'dp', flip[1])  60.8 us
    ppermute x5, waiting for transfers between devices, spread(): far = lax.ppermute(pair, 'dp', flip[4])  59.6 us
    ppermute x17, waiting for transfers between devices, swap_low(): return lax.ppermute(values, 'dp', flip[2])  59.6 us
    unnamed x355, local copies, waits for them, and re-layouts  49.8 us
  transfers between devices with their start and end apart: 121, of which 50 were waited for; matrix products, arithmetic and copies ran while one was open for 33% of the time, Pallas kernels for 3%

profile of v1, /device:TPU:0, one launch (start us, length us, event | category | flops | bytes accessed | tf_op | source)
XLA Modules:
  0.0 1148.9 jit_solution(4019579951842878573)
XLA Ops:
  19.7 15.0 %collective-permute-done.4 = bf16[256,768]{0,1:T(8,128)(2,1)S(1)} collective-permute-done((bf16[256,768]{0,1:T(8,128)(2,1)}, bf16[256,768]{0,1:T(8,128)(2,1)S(1)}, u32[]{:S(2)}, u32[]{:S(2)}) %collective-permute-start.4) | collective-permute-done | bytes 393248 | tf_op jit(solution)/shard_map/ppermute | solution.py:169
  38.3 16.1 %collective-permute-done = bf16[2,64,2048]{2,1,0:T(8,128)(2,1)S(1)} collective-permute-done((bf16[2,64,2048]{2,1,0:T(8,128)(2,1)S(1)}, bf16[2,64,2048]{2,1,0:T(8,128)(2,1)S(1)}, u32[]{:S(2)}, u32[]{:S(2)}) %collective-permute-start) | collective-permute-done | bytes 524320 | tf_op jit(solution)/shard_map/ppermute | solution.py:169
  72.6 17.7 %collective-permute-done.5 = bf16[2,256,768]{1,2,0:T(8,128)(2,1)} collective-permute-done((bf16[2,256,768]{1,2,0:T(8,128)(2,1)}, bf16[2,256,768]{1,2,0:T(8,128)(2,1)}, u32[]{:S(2)}, u32[]{:S(2)}) %collective-permute-start.5) | collective-permute-done | bytes 786464 | tf_op jit(solution)/shard_map/ppermute | solution.py:175
  121.0 10.8 collective-permute-done.12
  134.2 5.1 convolution_convert_fusion.14.q_ref.k_ref.v_ref
  146.7 5.0 convolution_convert_fusion.15.q_ref.k_ref.v_ref
  178.7 26.8 %collective-permute-done.45 = bf16[128,2048]{1,0:T(8,128)(2,1)} collective-permute-done((bf16[128,2048]{1,0:T(8,128)(2,1)}, bf16[128,2048]{1,0:T(8,128)(2,1)}, u32[]{:S(2)}, u32[]{:S(2)}) %collective-permute-start.45) | collective-permute-done | bytes 524320 | tf_op jit(solution)/shard_map/ppermute | solution.py:132
  208.5 10.1 collective-permute-done.14
  223.7 5.3 collective-permute-done.15
  284.6 4.8 fusion.30.k_ref.v_ref
  325.0 5.4 collective-permute-done.30
  332.3 27.8 %collective-permute-done.25 = bf16[128,2048]{1,0:T(8,128)(2,1)S(1)} collective-permute-done((bf16[128,2048]{1,0:T(8,128)(2,1)S(1)}, bf16[128,2048]{1,0:T(8,128)(2,1)S(1)}, u32[]{:S(2)}, u32[]{:S(2)}) %collective-permute-start.25) | collective-permute-done | bytes 524320 | tf_op jit(solution)/shard_map/ppermute | solution.py:132
  361.6 9.7 collective-permute-done.51
  377.0 14.4 %collective-permute-done.35 = bf16[2,256,1024]{2,1,0:T(8,128)(2,1)S(1)} collective-permute-done((bf16[2,256,1024]{2,1,0:T(8,128)(2,1)S(1)}, bf16[2,256,1024]{2,1,0:T(8,128)(2,1)S(1)}, u32[]{:S(2)}, u32[]{:S(2)}) %collective-permute-start.35) | collective-permute-done | bytes 1048608 | tf_op jit(solution)/shard_map/ppermute | solution.py:175
  391.9 21.2 %collective-permute-done.31 = bf16[2,256,1024]{2,1,0:T(8,128)(2,1)S(1)} collective-permute-done((bf16[2,256,1024]{2,1,0:T(8,128)(2,1)S(1)}, bf16[2,256,1024]{2,1,0:T(8,128)(2,1)S(1)}, u32[]{:S(2)}, u32[]{:S(2)}) %collective-permute-start.31) | collective-permute-done | bytes 1048608 | tf_op jit(solution)/shard_map/ppermute | solution.py:175
  417.7 4.9 collective-permute-done.53
  424.4 8.7 collective-permute-done.54
  433.8 5.4 collective-permute-done.37
  439.3 20.8 %collective-permute-done.33 = bf16[2,256,1024]{2,1,0:T(8,128)(2,1)S(1)} collective-permute-done((bf16[2,256,1024]{2,1,0:T(8,128)(2,1)S(1)}, bf16[2,256,1024]{2,1,0:T(8,128)(2,1)S(1)}, u32[]{:S(2)}, u32[]{:S(2)}) %collective-permute-start.33) | collective-permute-done | bytes 1048608 | tf_op jit(solution)/shard_map/ppermute | solution.py:177
  474.8 6.6 collective-permute-done.57
  483.0 6.8 collective-permute-done.39
  491.4 5.0 collective-permute-done.40
  499.9 6.5 collective-permute-done.60
  508.1 7.6 collective-permute-done.61
  520.1 12.7 %collective-permute-done.59 = bf16[64,2048]{1,0:T(8,128)(2,1)S(1)} collective-permute-done((bf16[64,2048]{1,0:T(8,128)(2,1)S(1)}, bf16[64,2048]{1,0:T(8,128)(2,1)S(1)}, u32[]{:S(2)}, u32[]{:S(2)}) %collective-permute-start.59) | collective-permute-done | bytes 262176 | tf_op jit(solution)/shard_map/ppermute | solution.py:169
  535.1 7.3 convert_reduce_fusion.1
  545.8 5.0 convert_reduce_fusion
  554.0 7.2 fusion.101
  561.2 6.3 add_convert_fusion
  579.4 6.9 collective-permute-done.82
  597.8 18.5 %collective-permute-done.113 = bf16[2,2,256,1024]{3,2,1,0:T(8,128)(2,1)S(1)} collective-permute-done((bf16[2,2,256,1024]{3,2,1,0:T(8,128)(2,1)S(1)}, bf16[2,2,256,1024]{3,2,1,0:T(8,128)(2,1)S(1)}, u32[]{:S(2)}, u32[]{:S(2)}) %collective-permute-start.113) | collective-permute-done | bytes 2097184 | tf_op jit(solution)/shard_map/ppermute | solution.py:197
  618.4 42.2 %collective-permute-done.110 = bf16[2,2,256,1024]{3,2,1,0:T(8,128)(2,1)S(1)} collective-permute-done((bf16[2,2,256,1024]{3,2,1,0:T(8,128)(2,1)S(1)}, bf16[2,2,256,1024]{3,2,1,0:T(8,128)(2,1)S(1)}, u32[]{:S(2)}, u32[]{:S(2)}) %collective-permute-start.110) | collective-permute-done | bytes 2097184 | tf_op jit(solution)/shard_map/ppermute | solution.py:197
  667.3 8.6 collective-permute-done.85
  681.7 31.0 %collective-permute-done.111 = bf16[2,256,1024]{2,1,0:T(8,128)(2,1)} collective-permute-done((bf16[2,256,1024]{2,1,0:T(8,128)(2,1)}, bf16[2,256,1024]{2,1,0:T(8,128)(2,1)}, u32[]{:S(2)}, u32[]{:S(2)}) %collective-permute-start.111) | collective-permute-done | bytes 1048608 | tf_op jit(solution)/shard_map/ppermute | solution.py:200
  777.4 6.4 constant_dynamic-slice_fusion.5
  783.8 6.0 copy.200
  801.7 5.1 fusion
  825.5 4.7 collective-permute-done.70
  830.9 20.3 %collective-permute-done.88 = bf16[128,2048]{1,0:T(8,128)(2,1)S(1)} collective-permute-done((bf16[128,2048]{1,0:T(8,128)(2,1)S(1)}, bf16[128,2048]{1,0:T(8,128)(2,1)S(1)}, u32[]{:S(2)}, u32[]{:S(2)}) %collective-permute-start.88) | collective-permute-done | bytes 524320 | tf_op jit(solution)/shard_map/ppermute | solution.py:132
  862.4 5.1 collective-permute-done.72
  903.0 5.4 convolution_convert_fusion.13
  911.5 4.9 shard_map.288
  935.4 5.6 collective-permute-done.76
  943.4 8.1 collective-permute-done.94
  975.1 5.0 collective-permute-done.96
  997.8 33.0 %collective-permute-done.102 = bf16[2,256,256]{2,1,0:T(8,128)(2,1)S(1)} collective-permute-done((bf16[2,256,256]{2,1,0:T(8,128)(2,1)S(1)}, bf16[2,256,256]{2,1,0:T(8,128)(2,1)S(1)}, u32[]{:S(2)}, u32[]{:S(2)}) %collective-permute-start.102) | collective-permute-done | bytes 262176 | tf_op jit(solution)/shard_map/ppermute | solution.py:200
  1040.7 71.4 %all-reduce.2.cloned.1.call-done = f32[30720]{0:T(1024)} async-done(((f32[30720]{0:T(1024)}), f32[30720]{0:T(1024)}) %all-reduce.2.cloned.1.call-update) | async-done | bytes 122896 | tf_op jit(solution)/shard_map/psum | solution.py:397
  1120.0 16.4 %all-gather.8.cloned.1.call-done = bf16[2,4,64,2048]{3,2,1,0:T(8,128)(2,1)} async-done(((bf16[2,1,64,2048]{3,2,1,0:T(8,128)(2,1)}), bf16[2,4,64,2048]{3,2,1,0:T(8,128)(2,1)}) %all-gather.8.cloned.1.call-update) | async-done | bytes 2097168 | tf_op jit(solution)/shard_map/all_gather | solution.py:387
  (914 shorter events, 520.5 us)
Async XLA Ops:
  7.2 277.4 %all-gather.4.cloned.1.call-start = ((), (), s32[]{:S(2)}) async-start(), calls=%async_computation.1 | async-start | bytes 5242880 | tf_op jit(solution)/shard_map/all_gather | solution.py:246
  14.1 51.6 %collective-permute-start.9 = (bf16[256,768]{0,1:T(8,128)(2,1)}, bf16[256,768]{0,1:T(8,128)(2,1)S(1)}, u32[]{:S(2)}, u32[]{:S(2)}) collective-permute-start(bf16[256,768]{0,1:T(8,128)(2,1)} %get-tuple-element.186), channel_id=1, source_target_pairs={{0,8},{4,12},{8,0},{12,4},{16,24},{20,28},{24,16},{28,20},{1,9},{5... | collective-permute-start | bytes 1179656 | tf_op jit(solution)/shard_map/ppermute | solution.py:169
  18.5 35.9 %collective-permute-start = (bf16[2,64,2048]{2,1,0:T(8,128)(2,1)S(1)}, bf16[2,64,2048]{2,1,0:T(8,128)(2,1)S(1)}, u32[]{:S(2)}, u32[]{:S(2)}) collective-permute-start(bf16[2,64,2048]{2,1,0:T(8,128)(2,1)S(1)} %get-tuple-element.156), channel_id=1, source_target_pairs={{0,8},{4,12},{8,0},{12,4},{16,24},{20,28},{24,16},{28,20},{1,9},{5... | collective-permute-start | bytes 1572872 | tf_op jit(solution)/shard_map/ppermute | solution.py:169
  35.7 54.6 %collective-permute-start.5 = (bf16[2,256,768]{1,2,0:T(8,128)(2,1)}, bf16[2,256,768]{1,2,0:T(8,128)(2,1)}, u32[]{:S(2)}, u32[]{:S(2)}) collective-permute-start(bf16[2,256,768]{1,2,0:T(8,128)(2,1)} %maximum_select_fusion.12), channel_id=1, source_target_pairs={{0,16},{4,20},{8,24},{12,28},{16,0},{20,4},{24,8},{28,12},{1,17},{... | collective-permute-start | bytes 2359304 | tf_op jit(solution)/shard_map/ppermute | solution.py:175
  64.1 36.4 %collective-permute-start.6 = (bf16[2,256,768]{1,2,0:T(8,128)(2,1)}, bf16[2,256,768]{1,2,0:T(8,128)(2,1)}, u32[]{:S(2)}, u32[]{:S(2)}) collective-permute-start(bf16[2,256,768]{1,2,0:T(8,128)(2,1)} %maximum_select_fusion.12), channel_id=1, source_target_pairs={{0,4},{4,0},{8,12},{12,8},{16,20},{20,16},{24,28},{28,24},{1,5},{5... | collective-permute-start | bytes 2359304 | tf_op jit(solution)/shard_map/ppermute | solution.py:176
  66.7 41.6 %collective-permute-start.11 = (bf16[2,256,768]{1,2,0:T(8,128)(2,1)}, bf16[2,256,768]{1,2,0:T(8,128)(2,1)}, u32[]{:S(2)}, u32[]{:S(2)}) collective-permute-start(bf16[2,256,768]{1,2,0:T(8,128)(2,1)} %maximum_select_fusion.14), channel_id=1, source_target_pairs={{0,4},{4,0},{8,12},{12,8},{16,20},{20,16},{24,28},{28,24},{1,5},{5... | collective-permute-start | bytes 2359304 | tf_op jit(solution)/shard_map/ppermute | solution.py:176
  67.2 37.1 %collective-permute-start.10 = (bf16[2,256,768]{1,2,0:T(8,128)(2,1)}, bf16[2,256,768]{1,2,0:T(8,128)(2,1)}, u32[]{:S(2)}, u32[]{:S(2)}) collective-permute-start(bf16[2,256,768]{1,2,0:T(8,128)(2,1)} %maximum_select_fusion.14), channel_id=1, source_target_pairs={{0,16},{4,20},{8,24},{12,28},{16,0},{20,4},{24,8},{28,12},{1,17},{... | collective-permute-start | bytes 2359304 | tf_op jit(solution)/shard_map/ppermute | solution.py:175
  98.2 35.9 %collective-permute-start.43 = (bf16[256,2048]{1,0:T(8,128)(2,1)}, bf16[256,2048]{1,0:T(8,128)(2,1)}, u32[]{:S(2)}, u32[]{:S(2)}) collective-permute-start(bf16[256,2048]{1,0:T(8,128)(2,1)} %pad_maximum_fusion.17), channel_id=1, source_target_pairs={{0,1},{1,0},{2,3},{3,2},{4,5},{5,4},{6,7},{7,6},{8,9},{9,8},{10,11... | collective-permute-start | bytes 3145736 | tf_op jit(solution)/shard_map/ppermute | solution.py:126
  116.1 30.6 %collective-permute-start.3 = (bf16[256,2048]{1,0:T(8,128)(2,1)}, bf16[256,2048]{1,0:T(8,128)(2,1)}, u32[]{:S(2)}, u32[]{:S(2)}) collective-permute-start(bf16[256,2048]{1,0:T(8,128)(2,1)} %pad_maximum_fusion.14), channel_id=1, source_target_pairs={{0,1},{1,0},{2,3},{3,2},{4,5},{5,4},{6,7},{7,6},{8,9},{9,8},{10,11... | collective-permute-start | bytes 3145736 | tf_op jit(solution)/shard_map/ppermute | solution.py:126
  167.0 54.3 %collective-permute-start.20 = (bf16[512,512]{0,1:T(8,128)(2,1)}, bf16[512,512]{0,1:T(8,128)(2,1)}, u32[]{:S(2)}, u32[]{:S(2)}) collective-permute-start(bf16[512,512]{0,1:T(8,128)(2,1)} %get-tuple-element.182), channel_id=1, source_target_pairs={{0,8},{4,12},{8,0},{12,4},{16,24},{20,28},{24,16},{28,20},{1,9},{5... | collective-permute-start | bytes 1572872 | tf_op jit(solution)/shard_map/ppermute | solution.py:169
  170.0 35.4 %collective-permute-start.45 = (bf16[128,2048]{1,0:T(8,128)(2,1)}, bf16[128,2048]{1,0:T(8,128)(2,1)}, u32[]{:S(2)}, u32[]{:S(2)}) collective-permute-start(bf16[128,2048]{1,0:T(8,128)(2,1)} %slice.778), channel_id=1, source_target_pairs={{0,8},{1,3},{2,10},{3,1},{4,12},{5,7},{6,14},{7,5},{8,0},{9,11},{1... | collective-permute-start | bytes 1572872 | tf_op jit(solution)/shard_map/ppermute | solution.py:132
  174.7 43.9 %collective-permute-start.14 = (bf16[128,2048]{1,0:T(8,128)(2,1)}, bf16[128,2048]{1,0:T(8,128)(2,1)}, u32[]{:S(2)}, u32[]{:S(2)}) collective-permute-start(bf16[128,2048]{1,0:T(8,128)(2,1)} %slice.781), channel_id=1, source_target_pairs={{0,8},{1,3},{2,10},{3,1},{4,12},{5,7},{6,14},{7,5},{8,0},{9,11},{1... | collective-permute-start | bytes 1572872 | tf_op jit(solution)/shard_map/ppermute | solution.py:132
  178.6 540.7 %all-gather.6.cloned.1.call-start = ((), (), s32[]{:S(2)}) async-start(), calls=%async_computation.2 | async-start | bytes 2621440 | tf_op jit(solution)/shard_map/all_gather | solution.py:387
  239.8 28.8 %collective-permute-start.22 = (bf16[2,512,512]{1,2,0:T(8,128)(2,1)}, bf16[2,512,512]{1,2,0:T(8,128)(2,1)}, u32[]{:S(2)}, u32[]{:S(2)}) collective-permute-start(bf16[2,512,512]{1,2,0:T(8,128)(2,1)} %maximum_select_fusion.3), channel_id=1, source_target_pairs={{0,4},{4,0},{8,12},{12,8},{16,20},{20,16},{24,28},{28,24},{1,5},{5... | collective-permute-start | bytes 3145736 | tf_op jit(solution)/shard_map/ppermute | solution.py:176
  245.7 70.7 %collective-permute-start.34 = (bf16[256,1024]{1,0:T(8,128)(2,1)}, bf16[256,1024]{1,0:T(8,128)(2,1)}, u32[]{:S(2)}, u32[]{:S(2)}) collective-permute-start(bf16[256,1024]{1,0:T(8,128)(2,1)} %bitcast.473), channel_id=1, source_target_pairs={{0,8},{4,12},{8,0},{12,4},{16,24},{20,28},{24,16},{28,20},{1,9},{5... | collective-permute-start | bytes 1572872 | tf_op jit(solution)/shard_map/ppermute | solution.py:169
  317.9 105.0 %collective-permute-start.36 = (bf16[2,256,1024]{2,1,0:T(8,128)(2,1)S(1)}, bf16[2,256,1024]{2,1,0:T(8,128)(2,1)S(1)}, u32[]{:S(2)}, u32[]{:S(2)}) collective-permute-start(bf16[2,256,1024]{2,1,0:T(8,128)(2,1)S(1)} %maximum_select_fusion.7), channel_id=1, source_target_pairs={{0,4},{4,0},{8,12},{12,8},{16,20},{20,16},{24,28},{28,24},{1,5},{5... | collective-permute-start | bytes 3145736 | tf_op jit(solution)/shard_map/ppermute | solution.py:176
  319.5 71.9 %collective-permute-start.35 = (bf16[2,256,1024]{2,1,0:T(8,128)(2,1)S(1)}, bf16[2,256,1024]{2,1,0:T(8,128)(2,1)S(1)}, u32[]{:S(2)}, u32[]{:S(2)}) collective-permute-start(bf16[2,256,1024]{2,1,0:T(8,128)(2,1)S(1)} %maximum_select_fusion.7), channel_id=1, source_target_pairs={{0,16},{4,20},{8,24},{12,28},{16,0},{20,4},{24,8},{28,12},{1,17},{... | collective-permute-start | bytes 3145736 | tf_op jit(solution)/shard_map/ppermute | solution.py:175
  321.2 39.0 %collective-permute-start.25 = (bf16[128,2048]{1,0:T(8,128)(2,1)S(1)}, bf16[128,2048]{1,0:T(8,128)(2,1)S(1)}, u32[]{:S(2)}, u32[]{:S(2)}) collective-permute-start(bf16[128,2048]{1,0:T(8,128)(2,1)S(1)} %slice.780), channel_id=1, source_target_pairs={{0,8},{1,3},{2,10},{3,1},{4,12},{5,7},{6,14},{7,5},{8,0},{9,11},{1... | collective-permute-start | bytes 1572872 | tf_op jit(solution)/shard_map/ppermute | solution.py:132
  324.9 46.5 %collective-permute-start.51 = (bf16[128,2048]{1,0:T(8,128)(2,1)S(1)}, bf16[128,2048]{1,0:T(8,128)(2,1)S(1)}, u32[]{:S(2)}, u32[]{:S(2)}) collective-permute-start(bf16[128,2048]{1,0:T(8,128)(2,1)S(1)} %slice.777), channel_id=1, source_target_pairs={{0,8},{1,3},{2,10},{3,1},{4,12},{5,7},{6,14},{7,5},{8,0},{9,11},{1... | collective-permute-start | bytes 1572872 | tf_op jit(solution)/shard_map/ppermute | solution.py:132
  331.8 81.4 %collective-permute-start.31 = (bf16[2,256,1024]{2,1,0:T(8,128)(2,1)S(1)}, bf16[2,256,1024]{2,1,0:T(8,128)(2,1)S(1)}, u32[]{:S(2)}, u32[]{:S(2)}) collective-permute-start(bf16[2,256,1024]{2,1,0:T(8,128)(2,1)S(1)} %maximum_select_fusion.5), channel_id=1, source_target_pairs={{0,16},{4,20},{8,24},{12,28},{16,0},{20,4},{24,8},{28,12},{1,17},{... | collective-permute-start | bytes 3145736 | tf_op jit(solution)/shard_map/ppermute | solution.py:175
  360.3 53.4 %collective-permute-start.26 = (bf16[64,2048]{1,0:T(8,128)(2,1)S(1)}, bf16[64,2048]{1,0:T(8,128)(2,1)S(1)}, u32[]{:S(2)}, u32[]{:S(2)}) collective-permute-start(bf16[64,2048]{1,0:T(8,128)(2,1)S(1)} %slice.792), channel_id=1, source_target_pairs={{0,2},{1,9},{2,0},{3,11},{4,6},{5,13},{6,4},{7,15},{8,10},{9,1},{1... | collective-permute-start | bytes 786440 | tf_op jit(solution)/shard_map/ppermute | solution.py:134
  371.5 43.7 %collective-permute-start.52 = (bf16[64,2048]{1,0:T(8,128)(2,1)S(1)}, bf16[64,2048]{1,0:T(8,128)(2,1)S(1)}, u32[]{:S(2)}, u32[]{:S(2)}) collective-permute-start(bf16[64,2048]{1,0:T(8,128)(2,1)S(1)} %slice.789), channel_id=1, source_target_pairs={{0,2},{1,9},{2,0},{3,11},{4,6},{5,13},{6,4},{7,15},{8,10},{9,1},{1... | collective-permute-start | bytes 786440 | tf_op jit(solution)/shard_map/ppermute | solution.py:134
  391.4 41.9 %collective-permute-start.32 = (bf16[2,256,1024]{2,1,0:T(8,128)(2,1)S(1)}, bf16[2,256,1024]{2,1,0:T(8,128)(2,1)S(1)}, u32[]{:S(2)}, u32[]{:S(2)}) collective-permute-start(bf16[2,256,1024]{2,1,0:T(8,128)(2,1)S(1)} %maximum_select_fusion.5), channel_id=1, source_target_pairs={{0,4},{4,0},{8,12},{12,8},{16,20},{20,16},{24,28},{28,24},{1,5},{5... | collective-permute-start | bytes 3145736 | tf_op jit(solution)/shard_map/ppermute | solution.py:176
  413.7 46.4 %collective-permute-start.33 = (bf16[2,256,1024]{2,1,0:T(8,128)(2,1)S(1)}, bf16[2,256,1024]{2,1,0:T(8,128)(2,1)S(1)}, u32[]{:S(2)}, u32[]{:S(2)}) collective-permute-start(bf16[2,256,1024]{2,1,0:T(8,128)(2,1)S(1)} %collective-permute-done.31), channel_id=1, source_target_pairs={{0,4},{4,0},{8,12},{12,8},{16,20},{20,16},{24,28},{28,24},{1,5},{5... | collective-permute-start | bytes 3145736 | tf_op jit(solution)/shard_map/ppermute | solution.py:177
  533.7 500.9 %reduce-scatter.2.cloned.1.call-start = ((), (), s32[]{:S(2)}) async-start(), calls=%async_computation.4 | async-start | bytes 5242880 | tf_op jit(solution)/shard_map/reduce_scatter | solution.py:358
  567.7 48.6 %collective-permute-start.113 = (bf16[2,2,256,1024]{3,2,1,0:T(8,128)(2,1)S(1)}, bf16[2,2,256,1024]{3,2,1,0:T(8,128)(2,1)S(1)}, u32[]{:S(2)}, u32[]{:S(2)}) collective-permute-start(bf16[2,2,256,1024]{3,2,1,0:T(8,128)(2,1)S(1)} %dynamic-slice_bitcast_fusion), channel_id=1, source_target_pairs={{0,4},{4,0},{8,12},{12,8},{16,20},{20,16},{24,28},{28,24},{1,5},{5... | collective-permute-start | bytes 6291464 | tf_op jit(solution)/shard_map/ppermute | solution.py:197
  592.1 68.5 %collective-permute-start.110 = (bf16[2,2,256,1024]{3,2,1,0:T(8,128)(2,1)S(1)}, bf16[2,2,256,1024]{3,2,1,0:T(8,128)(2,1)S(1)}, u32[]{:S(2)}, u32[]{:S(2)}) collective-permute-start(bf16[2,2,256,1024]{3,2,1,0:T(8,128)(2,1)S(1)} %dynamic-slice_bitcast_fusion.1), channel_id=1, source_target_pairs={{0,4},{4,0},{8,12},{12,8},{16,20},{20,16},{24,28},{28,24},{1,5},{5... | collective-permute-start | bytes 6291464 | tf_op jit(solution)/shard_map/ppermute | solution.py:197
  595.7 65.9 %collective-permute-start.84 = (bf16[64,2048]{1,0:T(8,128)(2,1)S(1)}, bf16[64,2048]{1,0:T(8,128)(2,1)S(1)}, u32[]{:S(2)}, u32[]{:S(2)}) collective-permute-start(bf16[64,2048]{1,0:T(8,128)(2,1)S(1)} %convert_element_type.616), channel_id=1, source_target_pairs={{0,2},{1,9},{2,0},{3,11},{4,6},{5,13},{6,4},{7,15},{8,10},{9,1},{1... | collective-permute-start | bytes 786440 | tf_op jit(solution)/shard_map/ppermute | solution.py:123
  596.5 69.5 %collective-permute-start.66 = (bf16[64,2048]{1,0:T(8,128)(2,1)S(1)}, bf16[64,2048]{1,0:T(8,128)(2,1)}, u32[]{:S(2)}, u32[]{:S(2)}) collective-permute-start(bf16[64,2048]{1,0:T(8,128)(2,1)S(1)} %convert_element_type.592), channel_id=1, source_target_pairs={{0,2},{1,9},{2,0},{3,11},{4,6},{5,13},{6,4},{7,15},{8,10},{9,1},{1... | collective-permute-start | bytes 786440 | tf_op jit(solution)/shard_map/ppermute | solution.py:123
  618.4 59.7 %collective-permute-start.114 = (bf16[2,256,1024]{2,1,0:T(8,128)(2,1)}, bf16[2,256,1024]{2,1,0:T(8,128)(2,1)}, u32[]{:S(2)}, u32[]{:S(2)}) collective-permute-start(bf16[2,256,1024]{2,1,0:T(8,128)(2,1)} %dynamic-slice_bitcast_fusion.2), channel_id=1, source_target_pairs={{0,16},{4,20},{8,24},{12,28},{16,0},{20,4},{24,8},{28,12},{1,17},{... | collective-permute-start | bytes 3145736 | tf_op jit(solution)/shard_map/ppermute | solution.py:200
  663.6 49.1 %collective-permute-start.111 = (bf16[2,256,1024]{2,1,0:T(8,128)(2,1)}, bf16[2,256,1024]{2,1,0:T(8,128)(2,1)}, u32[]{:S(2)}, u32[]{:S(2)}) collective-permute-start(bf16[2,256,1024]{2,1,0:T(8,128)(2,1)} %dynamic-slice_bitcast_fusion.3), channel_id=1, source_target_pairs={{0,16},{4,20},{8,24},{12,28},{16,0},{20,4},{24,8},{28,12},{1,17},{... | collective-permute-start | bytes 3145736 | tf_op jit(solution)/shard_map/ppermute | solution.py:200
  667.1 48.2 %collective-permute-start.67 = (bf16[128,2048]{1,0:T(8,128)(2,1)S(1)}, bf16[128,2048]{1,0:T(8,128)(2,1)S(1)}, u32[]{:S(2)}, u32[]{:S(2)}) collective-permute-start(bf16[128,2048]{1,0:T(8,128)(2,1)S(1)} %pad_maximum_fusion.34), channel_id=1, source_target_pairs={{0,8},{1,3},{2,10},{3,1},{4,12},{5,7},{6,14},{7,5},{8,0},{9,11},{1... | collective-permute-start | bytes 1572872 | tf_op jit(solution)/shard_map/ppermute | solution.py:125
  678.1 57.7 %collective-permute-start.86 = (bf16[256,2048]{1,0:T(8,128)(2,1)}, bf16[256,2048]{1,0:T(8,128)(2,1)}, u32[]{:S(2)}, u32[]{:S(2)}) collective-permute-start(bf16[256,2048]{1,0:T(8,128)(2,1)} %pad_maximum_fusion.24), channel_id=1, source_target_pairs={{0,1},{1,0},{2,3},{3,2},{4,5},{5,4},{6,7},{7,6},{8,9},{9,8},{10,11... | collective-permute-start | bytes 3145736 | tf_op jit(solution)/shard_map/ppermute | solution.py:126
  680.8 40.3 %collective-permute-start.115 = (bf16[256,1024]{1,0:T(8,128)(2,1)}, bf16[256,1024]{1,0:T(8,128)(2,1)}, u32[]{:S(2)}, u32[]{:S(2)}) collective-permute-start(bf16[256,1024]{1,0:T(8,128)(2,1)} %get-tuple-element.170), channel_id=1, source_target_pairs={{0,8},{4,12},{8,0},{12,4},{16,24},{20,28},{24,16},{28,20},{1,9},{5... | collective-permute-start | bytes 1572872 | tf_op jit(solution)/shard_map/ppermute | solution.py:169
  775.8 41.9 %collective-permute-start.69 = (bf16[256,2048]{1,0:T(8,128)(2,1)}, bf16[256,2048]{1,0:T(8,128)(2,1)}, u32[]{:S(2)}, u32[]{:S(2)}) collective-permute-start(bf16[256,2048]{1,0:T(8,128)(2,1)} %slice.549), channel_id=1, source_target_pairs={{0,1},{1,0},{2,3},{3,2},{4,5},{5,4},{6,7},{7,6},{8,9},{9,8},{10,11... | collective-permute-start | bytes 3145736 | tf_op jit(solution)/shard_map/ppermute | solution.py:130
  776.9 43.0 %collective-permute-start.87 = (bf16[256,2048]{1,0:T(8,128)(2,1)}, bf16[256,2048]{1,0:T(8,128)(2,1)}, u32[]{:S(2)}, u32[]{:S(2)}) collective-permute-start(bf16[256,2048]{1,0:T(8,128)(2,1)} %slice.568), channel_id=1, source_target_pairs={{0,1},{1,0},{2,3},{3,2},{4,5},{5,4},{6,7},{7,6},{8,9},{9,8},{10,11... | collective-permute-start | bytes 3145736 | tf_op jit(solution)/shard_map/ppermute | solution.py:130
  789.8 33.5 %collective-permute-start.104 = (bf16[2,2,256,512]{3,2,1,0:T(8,128)(2,1)}, bf16[2,2,256,512]{3,2,1,0:T(8,128)(2,1)}, u32[]{:S(2)}, u32[]{:S(2)}) collective-permute-start(bf16[2,2,256,512]{3,2,1,0:T(8,128)(2,1)} %bitcast.129), channel_id=1, source_target_pairs={{0,4},{4,0},{8,12},{12,8},{16,20},{20,16},{24,28},{28,24},{1,5},{5... | collective-permute-start | bytes 3145736 | tf_op jit(solution)/shard_map/ppermute | solution.py:197
  812.6 70.7 %collective-permute-start.107 = (bf16[2,2,512,512]{2,3,1,0:T(8,128)(2,1)}, bf16[2,2,512,512]{2,3,1,0:T(8,128)(2,1)}, u32[]{:S(2)}, u32[]{:S(2)}) collective-permute-start(bf16[2,2,512,512]{2,3,1,0:T(8,128)(2,1)} %bitcast.457), channel_id=1, source_target_pairs={{0,4},{4,0},{8,12},{12,8},{16,20},{20,16},{24,28},{28,24},{1,5},{5... | collective-permute-start | bytes 6291464 | tf_op jit(solution)/shard_map/ppermute | solution.py:197
  821.5 29.7 %collective-permute-start.88 = (bf16[128,2048]{1,0:T(8,128)(2,1)S(1)}, bf16[128,2048]{1,0:T(8,128)(2,1)S(1)}, u32[]{:S(2)}, u32[]{:S(2)}) collective-permute-start(bf16[128,2048]{1,0:T(8,128)(2,1)S(1)} %slice.771), channel_id=1, source_target_pairs={{0,8},{1,3},{2,10},{3,1},{4,12},{5,7},{6,14},{7,5},{8,0},{9,11},{1... | collective-permute-start | bytes 1572872 | tf_op jit(solution)/shard_map/ppermute | solution.py:132
  870.7 241.4 %all-reduce.2.cloned.1.call-start = ((), (), s32[]{:S(2)}) async-start(), calls=%async_computation.5 | async-start | bytes 245760 | tf_op jit(solution)/shard_map/psum | solution.py:397
  886.5 108.1 %collective-permute-start.108 = (bf16[2,512,512]{1,2,0:T(8,128)(2,1)}, bf16[2,512,512]{1,2,0:T(8,128)(2,1)}, u32[]{:S(2)}, u32[]{:S(2)}) collective-permute-start(bf16[2,512,512]{1,2,0:T(8,128)(2,1)} %dynamic-slice_bitcast_fusion.4), channel_id=1, source_target_pairs={{0,16},{4,20},{8,24},{12,28},{16,0},{20,4},{24,8},{28,12},{1,17},{... | collective-permute-start | bytes 3145736 | tf_op jit(solution)/shard_map/ppermute | solution.py:200
  928.2 59.8 %collective-permute-start.101 = (bf16[2,2,256,256]{3,2,1,0:T(8,128)(2,1)}, bf16[2,2,256,256]{3,2,1,0:T(8,128)(2,1)}, u32[]{:S(2)}, u32[]{:S(2)}) collective-permute-start(bf16[2,2,256,256]{3,2,1,0:T(8,128)(2,1)} %dynamic-slice_bitcast_fusion.12), channel_id=1, source_target_pairs={{0,4},{4,0},{8,12},{12,8},{16,20},{20,16},{24,28},{28,24},{1,5},{5... | collective-permute-start | bytes 1572872 | tf_op jit(solution)/shard_map/ppermute | solution.py:197
  975.0 161.3 %all-gather.8.cloned.1.call-start = ((), (), s32[]{:S(2)}) async-start(), calls=%async_computation.3 | async-start | bytes 2621440 | tf_op jit(solution)/shard_map/all_gather | solution.py:387
  991.5 40.1 %collective-permute-start.99 = (bf16[2,256,768]{1,2,0:T(8,128)(2,1)S(1)}, bf16[2,256,768]{1,2,0:T(8,128)(2,1)S(1)}, u32[]{:S(2)}, u32[]{:S(2)}) collective-permute-start(bf16[2,256,768]{1,2,0:T(8,128)(2,1)S(1)} %dynamic-slice_bitcast_fusion.5), channel_id=1, source_target_pairs={{0,16},{4,20},{8,24},{12,28},{16,0},{20,4},{24,8},{28,12},{1,17},{... | collective-permute-start | bytes 2359304 | tf_op jit(solution)/shard_map/ppermute | solution.py:200
  993.3 37.5 %collective-permute-start.102 = (bf16[2,256,256]{2,1,0:T(8,128)(2,1)S(1)}, bf16[2,256,256]{2,1,0:T(8,128)(2,1)S(1)}, u32[]{:S(2)}, u32[]{:S(2)}) collective-permute-start(bf16[2,256,256]{2,1,0:T(8,128)(2,1)S(1)} %dynamic-slice_bitcast_fusion.19), channel_id=1, source_target_pairs={{0,16},{4,20},{8,24},{12,28},{16,0},{20,4},{24,8},{28,12},{1,17},{... | collective-permute-start | bytes 786440 | tf_op jit(solution)/shard_map/ppermute | solution.py:200
  996.2 40.3 %collective-permute-start.109 = (bf16[512,512]{0,1:T(8,128)(2,1)S(1)}, bf16[512,512]{0,1:T(8,128)(2,1)S(1)}, u32[]{:S(2)}, u32[]{:S(2)}) collective-permute-start(bf16[512,512]{0,1:T(8,128)(2,1)S(1)} %get-tuple-element.176), channel_id=1, source_target_pairs={{0,8},{4,12},{8,0},{12,4},{16,24},{20,28},{24,16},{28,20},{1,9},{5... | collective-permute-start | bytes 1572872 | tf_op jit(solution)/shard_map/ppermute | solution.py:169
  1032.6 84.3 %collective-permute-start.100 = (bf16[256,768]{0,1:T(8,128)(2,1)}, bf16[256,768]{0,1:T(8,128)(2,1)S(1)}, u32[]{:S(2)}, u32[]{:S(2)}) collective-permute-start(bf16[256,768]{0,1:T(8,128)(2,1)} %get-tuple-element.184), channel_id=1, source_target_pairs={{0,8},{4,12},{8,0},{12,4},{16,24},{20,28},{24,16},{28,20},{1,9},{5... | collective-permute-start | bytes 1179656 | tf_op jit(solution)/shard_map/ppermute | solution.py:169
  1036.5 82.3 %collective-permute-start.97 = (bf16[256,1024]{1,0:T(8,128)(2,1)}, bf16[256,1024]{1,0:T(8,128)(2,1)S(1)}, u32[]{:S(2)}, u32[]{:S(2)}) collective-permute-start(bf16[256,1024]{1,0:T(8,128)(2,1)} %dynamic-slice_bitcast_fusion.13), channel_id=1, source_target_pairs={{0,8},{4,12},{8,0},{12,4},{16,24},{20,28},{24,16},{28,20},{1,9},{5... | collective-permute-start | bytes 1572872 | tf_op jit(solution)/shard_map/ppermute | solution.py:169
  (240 other events, 3271.5 us)
Sparse Core Ops, SparseCore 0:
  178.7 34.2 all-gather.3
  533.8 20.5 all-gather.5
  870.9 43.8 reduce-scatter.1
  975.2 136.9 all-reduce.1
  1113.6 22.7 all-gather.7

commit v2 on v1

v2 whole, which is shorter than its diff:
```python
import functools

import jax
import jax.numpy as jnp
from jax import lax
from jax.experimental import pallas as pl
from jax.experimental.pallas import tpu as pltpu
from jax.sharding import PartitionSpec as P

HD = 128
BOTH = ("dp", "mp")

eps = 1e-05
masked = -1e30
f32 = jnp.float32
bf16 = jnp.bfloat16


def normalize(values, gain, shift):
    center = values - jnp.mean(values, axis=-1, keepdims=True)
    spread = jnp.mean(center * center, axis=-1, keepdims=True)
    return center * lax.rsqrt(spread + eps) * gain + shift


def gelu_tanh(values):
    return (
        0.5
        * values
        * (1.0 + jnp.tanh(0.7978845608028654 * (values + 0.044715 * values * values * values)))
    )


def dot(left, right, contract):
    return lax.dot_general(left, right, (contract, ((), ())), preferred_element_type=f32)


def softmax_of(q, k, q_seg, k_seg):
    scores = dot(q, k, ((1,), (1,))) * HD ** (-0.5)
    scores = jnp.where(q_seg == k_seg, scores, masked)
    top = jnp.max(scores, axis=-1, keepdims=True)
    expo = jnp.exp(scores - top)
    return expo / jnp.sum(expo, axis=-1, keepdims=True)


def head_at(ref, index):
    return ref[:, index * HD : (index + 1) * HD]


def forward_kernel(heads, at, q_ref, kv_ref, qs_ref, ks_ref, o_ref):
    for h in range(heads):
        probs = softmax_of(
            head_at(q_ref, h), head_at(kv_ref, at + h), qs_ref[...], ks_ref[...]
        ).astype(bf16)
        out = dot(probs, head_at(kv_ref, at + heads + h), ((1,), (0,)))
        o_ref[:, h * HD : (h + 1) * HD] = out.astype(bf16)


def backward_kernel(heads, at, q_ref, kv_ref, g_ref, qs_ref, ks_ref, *outs):
    dq_ref, dkv_ref = outs[0], outs[-1]
    for h in range(heads):
        q, k = head_at(q_ref, h), head_at(kv_ref, at + h)
        v, g = head_at(kv_ref, at + heads + h), head_at(g_ref, h)
        probs = softmax_of(q, k, qs_ref[...], ks_ref[...])
        dv = dot(probs.astype(bf16), g, ((0,), (0,)))
        grad_probs = dot(g, v, ((1,), (1,)))
        shift = jnp.sum(probs * grad_probs, axis=-1, keepdims=True)
        grad_scores = (probs * (grad_probs - shift)).astype(bf16)
        dq = dot(grad_scores, k, ((1,), (0,))) * HD ** (-0.5)
        dk = dot(grad_scores, q, ((0,), (0,))) * HD ** (-0.5)
        for ref, index, value in (
            (dq_ref, h, dq),
            (dkv_ref, at + h, dk),
            (dkv_ref, at + heads + h, dv),
        ):
            ref[:, index * HD : (index + 1) * HD] = value.astype(bf16)


def row_block(shape, row):
    return pl.BlockSpec(shape, lambda i: (row, 0))


def attend(q, kv, row, at, q_seg, k_seg, heads):
    nq, nk = q_seg.shape[0], k_seg.shape[1]
    return pl.pallas_call(
        functools.partial(forward_kernel, heads, at),
        grid=(1,),
        in_specs=[
            row_block((nq, q.shape[1]), 0),
            row_block((nk, kv.shape[1]), row),
            row_block((nq, 1), 0),
            row_block((1, nk), 0),
        ],
        out_specs=row_block((nq, heads * HD), 0),
        out_shape=jax.ShapeDtypeStruct((nq, heads * HD), bf16),
    )(q, kv, q_seg, k_seg)


def attend_back(q, kv, row, at, grad, q_seg, k_seg, heads):
    nq, nk = q_seg.shape[0], k_seg.shape[1]
    wide = heads * HD
    shapes = [(nq, 3 * wide)] if at else [(nq, wide), (nk, 2 * wide)]
    return pl.pallas_call(
        functools.partial(backward_kernel, heads, at),
        grid=(1,),
        in_specs=[
            row_block((nq, q.shape[1]), 0),
            row_block((nk, kv.shape[1]), row),
            row_block((nq, wide), 0),
            row_block((nq, 1), 0),
            row_block((1, nk), 0),
        ],
        out_specs=[row_block(shape, 0) for shape in shapes],
        out_shape=[jax.ShapeDtypeStruct(shape, bf16) for shape in shapes],
    )(q, kv, grad, q_seg, k_seg)


def assemble_kernel(kinds, order, *refs):
    step = pl.program_id(0)
    pieces, outs = refs[:4], refs[4:]
    for index, piece in enumerate(pieces):

        @pl.when(step // 2 == index)
        def _(piece=piece):
            for unit, (which, _, column) in enumerate(kinds):
                value = piece[0, unit] if len(kinds) > 1 else piece[0]
                cols = value.shape[1]
                outs[which][:, column * cols : (column + 1) * cols] = value


def assembled(order, pieces, kinds, shapes, n_blocks):
    lead = pieces[0].shape[1:]
    zeros = (0,) * len(lead)
    in_specs = [
        pl.BlockSpec(
            (1,) + lead, lambda i, o, first=2 * index: (jnp.clip(i - first, 0, 1),) + zeros
        )
        for index in range(4)
    ]
    out_specs = []
    for index, (rows, cols) in enumerate(shapes):
        kind = [kind for which, kind, _ in kinds if which == index][0]
        if kind == "row":
            out_specs.append(pl.BlockSpec((rows // n_blocks, cols), lambda i, o: (o[i], 0)))
        else:
            out_specs.append(pl.BlockSpec((rows, cols // n_blocks), lambda i, o: (0, o[i])))
    return pl.pallas_call(
        functools.partial(assemble_kernel, kinds),
        grid_spec=pltpu.PrefetchScalarGridSpec(
            num_scalar_prefetch=1, grid=(8,), in_specs=in_specs, out_specs=out_specs
        ),
        out_shape=[jax.ShapeDtypeStruct(shape, bf16) for shape in shapes],
    )(order, *pieces)


def grad_kernel(kinds, extra, splits, order, *refs):
    step = pl.program_id(0)
    refs = list(refs)
    pairs = []
    for kind, count in kinds:
        lefts = [refs.pop(0) for _ in range(count)]
        pairs.append((kind, lefts, [refs.pop(0) for _ in range(count)]))
    added = refs.pop(0) if extra else None
    outs = [refs.pop(0) for _ in splits]
    pieces = []
    for kind, lefts, rights in pairs:
        total = 0.0
        for left, right in zip(lefts, rights):
            if kind == "row":
                total = total + dot(left[...], right[...], ((0,), (0,)))
            else:
                turned = refs.pop(0)

                @pl.when(step == 0)
                def _(turned=turned, left=left):
                    turned[...] = left[...].T

                total = total + dot(turned[...], right[...], ((1,), (0,)))
        pieces.append(total)
    value = pieces[0] if len(pieces) == 1 else jnp.concatenate(pieces, axis=1)
    if extra:
        value = value + added[0].astype(f32)
    value = value.astype(bf16)
    start = 0
    for out, size in zip(outs, splits):

        @pl.when((step >= start) & (step < start + size))
        def _(out=out):
            out[0] = value

        start += size


def grad_blocks(order, terms, n_blocks, splits, added=None):
    operands, specs, kinds, scratch, wide, high = [], [], [], [], 0, 0

    def fixed(rows, cols, row):
        return pl.BlockSpec((rows, cols), lambda i, o: (row, 0))

    def moving(rows, cols, row):
        return pl.BlockSpec((rows, cols), lambda i, o: (row, o[i]))

    for kind, lefts, rights in terms:
        kinds.append((kind, len(lefts)))
        for array, rows, row in lefts:
            cols = array.shape[1] // (n_blocks if kind == "row" else 1)
            specs.append((moving if kind == "row" else fixed)(rows, cols, row))
            operands.append(array)
            if kind == "col":
                scratch.append(pltpu.VMEM((cols, rows), bf16))
            high = cols
        for index, (array, rows, row) in enumerate(rights):
            cols = array.shape[1] // (n_blocks if kind == "col" else 1)
            specs.append((moving if kind == "col" else fixed)(rows, cols, row))
            operands.append(array)
            if index == 0:
                wide += cols
    if added is not None:
        operands.append(added)
        specs.append(pl.BlockSpec((1, high, wide), lambda i, o: (i, 0, 0)))
    outs, start = [], 0
    for size in splits:
        place = lambda i, o, a=start, n=size: (jnp.clip(i - a, 0, n - 1), 0, 0)
        outs.append(pl.BlockSpec((1, high, wide), place))
        start += size
    return pl.pallas_call(
        functools.partial(grad_kernel, kinds, added is not None, splits),
        grid_spec=pltpu.PrefetchScalarGridSpec(
            num_scalar_prefetch=1,
            grid=(sum(splits),),
            in_specs=specs,
            out_specs=outs,
            scratch_shapes=scratch,
        ),
        out_shape=[jax.ShapeDtypeStruct((size, high, wide), bf16) for size in splits],
    )(order, *operands)


def pick(values, index, axis=0):
    return lax.dynamic_index_in_dim(values, index, axis, keepdims=False)


def after(value, *others):
    return lax.optimization_barrier((value,) + others)[0]


def build(n_dp, n_mp):
    n_hi = n_dp // 4
    flip = {bit: [(i, i ^ bit) for i in range(n_dp)] for bit in (1, 2, 4)}
    core_swap = [(i, i ^ 1) for i in range(n_mp)]
    side_swap = [(i, i ^ 2) for i in range(n_mp)]
    side = lambda i, m: i * n_mp + (m ^ 2)
    lower = lambda i, m: (i ^ 2) * n_mp + m
    pairs = [(i, m) for i in range(n_dp) for m in range(n_mp)]
    first_hop = [(i * n_mp + m, side(i, m) if m % 2 == 0 else lower(i, m)) for i, m in pairs]
    second_hop = [(i * n_mp + m, lower(i, m) if m % 2 == 0 else side(i, m)) for i, m in pairs]
    high_groups = [[h * 4 + low for h in range(n_hi)] for low in range(4)]

    def gather_tokens(own):
        near = lax.ppermute(own, BOTH, first_hop)
        two = jnp.concatenate([own, near], axis=0)
        four = jnp.concatenate([two, lax.ppermute(two, BOTH, second_hop)], axis=0)
        return jnp.concatenate([four, lax.ppermute(four, "mp", core_swap)], axis=0)

    def scatter_tokens(left, right, contract):
        half = left.shape[0] // 2
        part = half // 4
        arrived = lax.ppermute(
            dot(left[half:], right, contract).astype(bf16), "mp", core_swap
        )
        four = dot(left[:half], right, contract) + arrived.astype(f32)
        arrived = lax.ppermute(four[2 * part :].astype(bf16), BOTH, second_hop)
        two = four[: 2 * part] + arrived.astype(f32)
        arrived = lax.ppermute(two[part:].astype(bf16), BOTH, first_hop)
        return two[:part] + arrived.astype(f32)

    def on_device(
        tokens,
        text,
        image_seg,
        text_seg,
        w_qkv,
        w_out,
        c_q,
        c_kv,
        c_out,
        w_up,
        w_down,
        norm_gain,
        norm_bias,
        out_bias,
        up_bias,
        cotangent,
    ):
        d, m = lax.axis_index("dp"), lax.axis_index("mp")
        high, low, near_y = d // 4, (d // 2) % 2, d % 2
        core = m % 2
        seq, dim = tokens.shape
        text_len, text_dim = text_seg.shape[1], text.shape[1] * n_mp
        block = seq // 8
        place = low * 4 + m
        slice_dim = dim // n_dp
        slice_text = text_dim // n_dp
        mine = w_qkv.shape[2] // 2
        hidden = w_up.shape[1] // 2
        heads = mine // HD

        def xor_order(masks):
            return (d ^ jnp.array(masks, jnp.int32)).astype(jnp.int32)

        def ordered(own, theirs, axis=0):
            return jnp.where(
                low == 0, jnp.stack([own, theirs], axis), jnp.stack([theirs, own], axis)
            )

        def swap_low(values):
            return lax.ppermute(values, "dp", flip[2])

        def cut(parts, shape):
            def side_of(g):
                pieces = []
                for weight, kind in parts:
                    axis = 0 if kind == "col" else weight.ndim - 1
                    width = weight.shape[axis] // 2
                    pieces.append(lax.dynamic_slice_in_dim(weight, g * width, width, axis))
                return (jnp.stack(pieces) if len(pieces) > 1 else pieces[0]).reshape(shape)

            return side_of(low), side_of(1 - low)

        def spread(keep, recv):
            pair = jnp.stack([keep, recv])
            if n_hi == 2:
                far = lax.all_gather(pair, "dp", axis=0, axis_index_groups=high_groups)
                far = pick(far, 1 - high)
                return [
                    pair,
                    far,
                    lax.ppermute(pair, "dp", flip[1]),
                    lax.ppermute(far, "dp", flip[1]),
                ]
            pair = jnp.where(low == 0, pair, pair[::-1])
            own = lax.all_gather(pair, "dp", axis=0, axis_index_groups=high_groups)
            theirs = lax.ppermute(own, "dp", flip[1])
            full = jnp.where(
                near_y == 0, jnp.stack([own, theirs], 2), jnp.stack([theirs, own], 2)
            )
            return full.reshape((n_dp,) + keep.shape)

        def assemble(pieces, kinds, shapes):
            units = len(kinds)
            if n_hi != 2:
                outs = [[] for _ in shapes]
                for unit, (which, kind, _) in enumerate(kinds):
                    value = pieces[:, unit] if units > 1 else pieces
                    if kind == "col":
                        value = jnp.moveaxis(value, 0, 1)
                    outs[which].append(value.reshape(shapes[which][0], -1))
                return [jnp.concatenate(out, axis=1) for out in outs]

            return assembled(xor_order([0, 2, 4, 6, 1, 3, 5, 7]), pieces, kinds, shapes, n_dp)

        def first_blocks(terms):
            if n_hi != 2:
                return ()
            return (grad_blocks(xor_order([5, 7, 1, 3]), terms, n_dp, [4])[0],)

        def second_blocks(terms, away, *gates):
            if n_hi != 2:
                return ()
            arrived = after(lax.ppermute(away[0], "dp", flip[1]), *gates)
            return tuple(grad_blocks(xor_order([4, 6, 0, 2]), terms, n_dp, [2, 2], arrived))

        def across_high(second, *gates):
            if n_hi != 2:
                return ()
            return (after(lax.ppermute(second[0], "dp", flip[4]), *gates),)

        def collected(terms, second, arrived, axis):
            if n_hi == 2:
                total = second[1].astype(f32) + arrived[0].astype(f32)
                own, theirs = total[0], swap_low(total[1].astype(bf16))
            else:
                grads = []
                for kind, lefts, rights in terms:
                    cut_of = lambda v: v[0][v[1] * v[2] : v[1] * (v[2] + 1)]
                    grad = sum(
                        dot(cut_of(left), cut_of(right), ((0,), (0,)))
                        for left, right in zip(lefts, rights)
                    ).astype(bf16)
                    if kind == "row":
                        grads.append(grad.reshape(n_dp, -1, grad.shape[1]))
                    else:
                        grads.append(
                            jnp.moveaxis(grad.reshape(grad.shape[0], n_dp, -1), 1, 0)
                        )
                grad = jnp.concatenate(grads, axis=2)
                grad = grad.reshape((n_hi, 2, 2) + grad.shape[1:])
                arrived = lax.ppermute(pick(grad, 1 - near_y, 2), "dp", flip[1])
                total = (pick(grad, near_y, 2).astype(f32) + arrived.astype(f32)).astype(bf16)
                total = lax.psum_scatter(
                    total, "dp", scatter_dimension=0, axis_index_groups=high_groups
                )
                theirs = swap_low(pick(total, 1 - low))
                own = pick(total, low).astype(f32)
            return ordered(own, theirs.astype(f32), axis)

        qkv_shape = (3, slice_dim, mine)
        stay_qkv, go_qkv = cut([(w_qkv, "row")], qkv_shape)
        got_qkv = swap_low(go_qkv)
        packed = slice_dim == mine
        if packed:
            stay_proj, go_proj = cut(
                [(w_out, "col"), (c_q, "row"), (c_out, "col")], (3, slice_dim, mine)
            )
        else:
            singles = [
                cut([(w_out, "col")], (mine, slice_dim)),
                cut([(c_q, "row")], (slice_dim, mine)),
                cut([(c_out, "col")], (mine, slice_dim)),
            ]
        stay_kv, go_kv = cut([(c_kv, "row")], (2, slice_text, mine))
        stay_up, go_up = cut([(w_up, "row")], (slice_dim, hidden))
        stay_down, go_down = cut([(w_down, "col")], (hidden, slice_dim))
        pieces_qkv = spread(stay_qkv, got_qkv)
        far = lambda pieces, *which: tuple(pieces[i] for i in which) if n_hi == 2 else ()
        full_qkv = assemble(pieces_qkv, [(0, "row", j) for j in range(3)], [(dim, 3 * mine)])[0]
        kinds, shapes = ("col", "row", "col"), [(mine, dim), (dim, mine), (mine, dim)]
        if packed:
            got_proj = swap_low(after(go_proj, got_qkv))
            pieces_proj = spread(stay_proj, got_proj)
            full_out, full_cq, full_cout = assemble(
                pieces_proj, [(i, kind, 0) for i, kind in enumerate(kinds)], shapes
            )
        else:
            got_proj = got_qkv
            pieces_proj = [got_qkv] * 2
            full_out, full_cq, full_cout = [
                assemble(spread(stay, swap_low(go)), [(0, kind, 0)], [shape])[0]
                for (stay, go), kind, shape in zip(singles, kinds, shapes)
            ]
        got_kv = swap_low(after(go_kv, got_proj))
        pieces_kv = spread(stay_kv, got_kv)
        full_kv = assemble(pieces_kv, [(0, "row", 0), (0, "row", 1)], [(text_dim, 2 * mine)])[0]
        bias_up = lax.dynamic_slice(up_bias, (low * hidden,), (hidden,))

        local = after(jnp.stack([tokens, cotangent]), got_qkv)
        own = lax.dynamic_slice(local, (0, place * block, 0), (2, block, dim))
        away = lax.dynamic_slice(
            local, (0, ((1 - low) * 4 + m) * block, 0), (2, block, dim)
        )
        both = ordered(own, swap_low(away))
        segs = jnp.concatenate([image_seg[0], text_seg[0]])
        segs = ordered(segs, swap_low(segs))
        order = jnp.where(
            core == 0,
            jnp.array([0, 2, 4, 6, 1, 5, 3, 7], jnp.int32),
            jnp.array([0, 4, 2, 6, 1, 3, 5, 7], jnp.int32),
        )
        image_ids = jnp.take(segs[:, :seq].reshape(2, 8, block), place ^ order, axis=1)
        image_ids = image_ids.reshape(2, seq)
        text_ids = segs[:, seq:]
        words = lax.all_gather(ordered(text, swap_low(text)), "mp", axis=2, tiled=True)
        words = words.reshape(2 * text_len, text_dim)

        rows = (0, 1)
        residual = [both[r, 0].astype(f32) for r in rows]
        upstream = [both[r, 1].astype(f32) for r in rows]
        q_ids = [image_ids[r].reshape(seq, 1) for r in rows]
        i_ids = [image_ids[r].reshape(1, seq) for r in rows]
        t_ids = [text_ids[r].reshape(1, text_len) for r in rows]

        def norm(values, which):
            out, pull = jax.vjp(normalize, values, norm_gain[which], norm_bias[which])
            return out.astype(bf16), pull

        straight, across = ((1,), (0,)), ((1,), (1,))
        pulls = [[None] * 2 for _ in range(4)]
        hid_one, qkv, mixed, after_self = [], [], [], []
        for r in rows:
            normed, pulls[0][r] = norm(residual[r], 0)
            hid_one.append(gather_tokens(normed))
        hid_one[0] = after(hid_one[0], got_kv)
        got_up = swap_low(after(go_up, hid_one[1]))
        got_down = swap_low(after(go_down, hid_one[1]))
        pieces_up = spread(stay_up, got_up)
        full_up = assemble(pieces_up, [(0, "row", 0)], [(dim, hidden)])[0]
        pieces_down = spread(stay_down, got_down)
        full_down = assemble(pieces_down, [(0, "col", 0)], [(hidden, dim)])[0]
        for r in rows:
            qkv.append(dot(hid_one[r], full_qkv, straight).astype(bf16))
            mixed.append(attend(qkv[r], qkv[r], 0, heads, q_ids[r], i_ids[r], heads))
            ready = after(mixed[r], got_up, got_down, *far(pieces_kv, 1)) if r == 0 else mixed[r]
            after_self.append(
                residual[r] + scatter_tokens(ready, full_out, straight) + out_bias[0]
            )
        hid_two, cross_q, cross_mixed, after_cross = [], [], [], []
        cross_kv = dot(after(words, *far(pieces_up, 1, 2)), full_kv, straight).astype(bf16)
        for r in rows:
            normed, pulls[1][r] = norm(after_self[r], 1)
            hid_two.append(gather_tokens(after(normed, words) if r else normed))
        for r in rows:
            cross_q.append(dot(hid_two[r], full_cq, straight).astype(bf16))
            cross_mixed.append(attend(cross_q[r], cross_kv, r, 0, q_ids[r], t_ids[r], heads))
            after_cross.append(
                after_self[r] + scatter_tokens(cross_mixed[r], full_cout, straight) + out_bias[1]
            )
        hid_three, pre_act, act, after_mlp = [], [], [], []
        for r in rows:
            normed, pulls[2][r] = norm(after_cross[r], 2)
            gates = far(pieces_down, 2) if r else far(pieces_up, 3) + far(pieces_down, 1)
            hid_three.append(gather_tokens(after(normed, *gates)))
        for r in rows:
            pre_act.append(dot(hid_three[r], full_up, straight) + bias_up)
            act.append(gelu_tanh(pre_act[r]).astype(bf16))
            after_mlp.append(
                after_cross[r] + scatter_tokens(act[r], full_down, straight) + out_bias[2]
            )

        gains, shifts, biases = [0.0] * 4, [0.0] * 4, [0.0] * 3

        def back_norm(which, r, grad):
            out, gain, shift = pulls[which][r](grad)
            gains[which] = gains[which] + gain
            shifts[which] = shifts[which] + shift
            return out

        outs, grad_mlp, low_mlp = [], [], []
        for r in rows:
            final, pulls[3][r] = norm(after_mlp[r], 3)
            outs.append(final)
            grad_mlp.append(back_norm(3, r, upstream[r]))
            biases[2] = biases[2] + jnp.sum(grad_mlp[r], axis=0)
            low_mlp.append(gather_tokens(grad_mlp[r].astype(bf16)))
        def streams(values):
            return [(value, value.shape[0], 0) for value in values]

        down_term = [("col", streams(act), streams(low_mlp))]
        down = first_blocks(down_term)
        grad_pre, grad_in = [], []
        for r in rows:
            ready = low_mlp[r] if r == 0 else after(low_mlp[r], *down)
            grad_act = dot(ready, full_down, across)
            grad_pre.append(jax.vjp(gelu_tanh, pre_act[r])[1](grad_act)[0].astype(bf16))
            grad_in.append(scatter_tokens(grad_pre[r], full_up, across))
        up_term = [("row", streams(hid_three), streams(grad_pre))]
        up = first_blocks(up_term)
        grad_after_cross, low_cross = [], []
        for r in rows:
            grad_after_cross.append(grad_mlp[r] + back_norm(2, r, grad_in[r]))
            biases[1] = biases[1] + jnp.sum(grad_after_cross[r], axis=0)
            ready = grad_after_cross[r].astype(bf16)
            low_cross.append(gather_tokens(ready if r == 0 else after(ready, *up)))
        up_grad = jnp.sum(grad_pre[0].astype(f32), axis=0) + jnp.sum(
            grad_pre[1].astype(f32), axis=0
        )

        down_second = second_blocks(down_term, down, *grad_in)
        cq_low, ckv_low, grad_in = [], [], []
        for r in rows:
            ready = after(low_cross[r], *down_second) if r == 0 else low_cross[r]
            grad_mixed = dot(ready, full_cout, across).astype(bf16)
            dq, dkv = attend_back(
                cross_q[r], cross_kv, r, 0, grad_mixed, q_ids[r], t_ids[r], heads
            )
            cq_low.append(dq)
            ckv_low.append(dkv)
            grad_in.append(scatter_tokens(dq, full_cq, across))
        cq_term = ("row", streams(hid_two), streams(cq_low))
        cout_term = ("col", streams(cross_mixed), streams(low_cross))
        kv_term = [("row", [(words, text_len, r) for r in rows], streams(ckv_low))]
        both_term = [cq_term, cout_term]
        both_first, kv_first = first_blocks(both_term), first_blocks(kv_term)
        grad_after_self, low_self = [], []
        for r in rows:
            grad_after_self.append(grad_after_cross[r] + back_norm(1, r, grad_in[r]))
            biases[0] = biases[0] + jnp.sum(grad_after_self[r], axis=0)
            ready = grad_after_self[r].astype(bf16)
            if r == 1:
                up_second = second_blocks(up_term, up, *cq_low)
            gates = kv_first + up_second if r else both_first
            low_self.append(gather_tokens(after(ready, *gates)))
        text_term = dot(jnp.concatenate(ckv_low), full_kv, across).astype(bf16)

        down_far = across_high(down_second, *cq_low)
        out_term = [("col", streams(mixed), streams(low_self))]
        out_first = first_blocks(out_term)
        both_second = second_blocks(both_term, both_first, *grad_after_self)
        qkv_low = []
        for r in rows:
            gates = (*down_far, text_term, *out_first) if r else both_second
            grad_mixed = dot(after(low_self[r], *gates), full_out, across).astype(bf16)
            qkv_low.append(
                attend_back(qkv[r], qkv[r], 0, heads, grad_mixed, q_ids[r], i_ids[r], heads)[0]
            )
        qkv_term = [("row", streams(hid_one), streams(qkv_low))]
        qkv_first = first_blocks(qkv_term)
        up_far = across_high(up_second, *qkv_first)
        kv_second = second_blocks(kv_term, kv_first, *qkv_first)
        out_second = second_blocks(out_term, out_first, *kv_second)
        qkv_second = second_blocks(qkv_term, qkv_first, *out_second)
        both_far = across_high(both_second, *kv_second)
        kv_far = across_high(kv_second, *qkv_second)
        out_far = across_high(out_second, *qkv_second)
        grad_tokens = []
        for r in rows:
            grad_in = scatter_tokens(after(qkv_low[r], *qkv_first), full_qkv, across)
            piece = grad_after_self[r] + back_norm(0, r, grad_in)
            grad_tokens.append(piece)
        text_term = lax.psum_scatter(
            text_term.reshape(2, text_len, text_dim), "mp", scatter_dimension=2, tiled=True
        )
        grad_text = pick(text_term, low).astype(f32) + swap_low(
            pick(text_term, 1 - low)
        ).astype(f32)

        sum_down = collected(down_term, down_second, down_far, 0)
        sum_up = collected(up_term, up_second, up_far, 1)
        if packed:
            sum_both = collected(both_term, both_second, both_far, 0)
            sum_cq = jnp.moveaxis(sum_both[:, :, :mine], 0, 1)
            sum_cout = sum_both[:, :, mine:]
        else:
            sum_cq, sum_cout = collected([cq_term], (), (), 1), collected([cout_term], (), (), 0)
        sum_kv = collected(kv_term, kv_second, kv_far, 1)
        sum_out = collected(out_term, out_second, out_far, 0)
        sum_qkv = collected(qkv_term, qkv_second, across_high(qkv_second), 1)

        small = jnp.stack(gains + shifts + biases)
        small = small + lax.ppermute(small, "mp", core_swap)
        small = small + lax.ppermute(small, "mp", side_swap)
        wide = jnp.concatenate([small.reshape(-1), up_grad])
        if n_hi == 2:
            for bit in (1, 4):
                wide = wide + lax.ppermute(wide, "dp", flip[bit])
        else:
            wide = wide + lax.ppermute(wide, "dp", flip[1])
            wide = lax.psum(wide, "dp", axis_index_groups=high_groups)
        theirs = swap_low(wide)
        parts = (wide + theirs)[: 11 * dim].reshape(11, dim)
        up_total = ordered(wide[11 * dim :], theirs[11 * dim :]).reshape(-1)

        def whole_row(pieces):
            pieces = jnp.stack(pieces)
            pieces = ordered(pick(pieces, low), swap_low(pick(pieces, 1 - low)))
            pieces = lax.all_gather(pieces, "mp", axis=1)
            return pieces.reshape(seq, dim)

        output = whole_row(outs)
        grad_tokens = [piece.astype(bf16) for piece in grad_tokens]
        grad_tokens = whole_row([after(piece, *qkv_second) for piece in grad_tokens]).astype(f32)
        gain_total, shift_total, bias_total = parts[:4], parts[4:8], parts[8:]

        apart = lambda v, n: v.reshape(v.shape[0], 2, n, -1).transpose(2, 0, 1, 3)
        return (
            output,
            grad_tokens,
            grad_text,
            apart(sum_qkv, 3).reshape(w_qkv.shape),
            sum_out.reshape(w_out.shape),
            sum_cq.reshape(c_q.shape),
            apart(sum_kv, 2).reshape(c_kv.shape),
            sum_cout.reshape(c_out.shape),
            sum_up.reshape(w_up.shape),
            sum_down.reshape(w_down.shape),
            gain_total,
            shift_total,
            bias_total,
            up_total,
        )

    return on_device


def solution(mesh):
    in_specs = (
        P("dp", None),
        P("dp", "mp"),
        P("dp", None),
        P("dp", None),
        P(None, "dp", "mp"),
        P("mp", "dp"),
        P("dp", "mp"),
        P(None, "dp", "mp"),
        P("mp", "dp"),
        P("dp", "mp"),
        P("mp", "dp"),
        P(),
        P(),
        P(),
        P("mp"),
        P("dp", None),
    )
    out_specs = (
        P("dp", None),
        P("dp", None),
        P("dp", "mp"),
        P(None, "dp", "mp"),
        P("mp", "dp"),
        P("dp", "mp"),
        P(None, "dp", "mp"),
        P("mp", "dp"),
        P("dp", "mp"),
        P("mp", "dp"),
        P(),
        P(),
        P(),
        P("mp"),
    )
    return jax.shard_map(
        build(mesh.shape["dp"], mesh.shape["mp"]),
        mesh=mesh,
        in_specs=in_specs,
        out_specs=out_specs,
        check_vma=False,
    )
```

time: 1160 us -> 1010 us (0.87)
  waiting for transfers between devices: 579 us -> 397 us
  Pallas kernels: 34.1 us -> 154 us
  local copies, waits for them, and re-layouts: 161 us -> 100 us
  matrix products: 143 us -> 98.6 us
  starting transfers between devices: 96.1 us -> 126 us
    pallas_call x8 -> x25, Pallas kernels: 34.1 us -> 154 us  [the longest x12 82.6 us: grad_blocks(): pl.pallas_call(functools.partial(grad_kernel, kinds, added is not None, s...]
    ppermute x39 -> x38, waiting for transfers between devices: 226 us -> 115 us  [the longest x5 70.3 us: spread(): lax.ppermute(far, 'dp', flip[1])]
    psum x1 -> x0, waiting for transfers between devices: 71.4 us -> none  [on_device(): small = lax.psum(jnp.concatenate([small, ups]), BOTH)]
    ppermute x12, waiting for transfers between devices: 138 us -> 75.6 us  [scatter_tokens(): arrived = lax.ppermute(four[2 * part:].astype(bf16), BOTH, second_hop)]
    dot_general x42 -> x38, matrix products: 143 us -> 98.6 us  [dot(): lax.dot_general(left, right, (contract, ((), ())), preferred_element_type...]
    ppermute x17 -> x18, waiting for transfers between devices: 59.6 us -> 88.4 us  [swap_low(): return lax.ppermute(values, 'dp', flip[2])]
    all_gather x0 -> x5, waiting for transfers between devices: none -> 26.3 us  [spread(): far = lax.all_gather(pair, 'dp', axis=0, axis_index_groups=high_groups)]
    dynamic_slice x13 -> x0, local copies, waits for them, and re-layouts: 22.5 us -> none  [the longest x12 21.2 us: pick(): return lax.dynamic_index_in_dim(values, index, axis, keepdims=False)]
  transfers between devices with their start and end apart: 121 -> 125, of which waited for: 50 -> 55; matrix products, arithmetic and copies ran while one was open for 33% -> 27% of each run, Pallas kernels for 3% -> 15%
where the time goes in v2:
time: 1010 us; the launch traced here: 1000 us
  waiting for transfers between devices  397 us (39%)
  Pallas kernels  154 us (15%)
  starting transfers between devices  126 us (12%)
  other arithmetic  111 us (11%)
  local copies, waits for them, and re-layouts  100 us (10%)
  matrix products  98.6 us (10%)
  between operations  17.2 us (2%)
    dot_general x38, matrix products, dot(): lax.dot_general(left, right, (contract, ((), ())), preferred_element_type...  98.6 us
    ppermute x18, waiting for transfers between devices, swap_low(): return lax.ppermute(values, 'dp', flip[2])  88.4 us
    pallas_call x12, Pallas kernels, grad_blocks(): pl.pallas_call(functools.partial(grad_kernel, kinds, added is not None, s...  82.6 us
    ppermute x12, waiting for transfers between devices, scatter_tokens(): arrived = lax.ppermute(four[2 * part:].astype(bf16), BOTH, second_hop)  75.6 us
    ppermute x5, waiting for transfers between devices, spread(): lax.ppermute(far, 'dp', flip[1])  70.3 us
    ppermute x12, waiting for transfers between devices, gather_tokens(): four = jnp.concatenate([two, lax.ppermute(two, BOTH, second_hop)], axis=0)  52.3 us
    pallas_call x5, Pallas kernels, assembled(): pl.pallas_call(functools.partial(assemble_kernel, kinds), grid_spec=pltpu...  39.6 us
    unnamed x365, local copies, waits for them, and re-layouts  33.9 us
  transfers between devices with their start and end apart: 125, of which 55 were waited for; matrix products, arithmetic and copies ran while one was open for 27% of the time, Pallas kernels for 15%

profile of v2, /device:TPU:0, one launch (start us, length us, event | category | flops | bytes accessed | tf_op | source)
XLA Modules:
  0.0 1004.7 jit_solution(16483212389035041542)
XLA Ops:
  34.7 14.4 %collective-permute-done.5 = bf16[3,256,256]{2,1,0:T(8,128)(2,1)} collective-permute-done((bf16[3,256,256]{2,1,0:T(8,128)(2,1)S(1)}, bf16[3,256,256]{2,1,0:T(8,128)(2,1)}, u32[]{:S(2)}, u32[]{:S(2)}) %collective-permute-start.5) | collective-permute-done | bytes 393248 | tf_op jit(solution)/shard_map/ppermute | solution.py:316
  53.8 16.4 %collective-permute-done.1 = bf16[2,64,2048]{2,1,0:T(8,128)(2,1)S(1)} collective-permute-done((bf16[2,64,2048]{2,1,0:T(8,128)(2,1)S(1)}, bf16[2,64,2048]{2,1,0:T(8,128)(2,1)S(1)}, u32[]{:S(2)}, u32[]{:S(2)}) %collective-permute-start.1) | collective-permute-done | bytes 524320 | tf_op jit(solution)/shard_map/ppermute | solution.py:316
  71.0 9.6 collective-permute-done.6
  99.6 9.2 collective-permute-done.11
  111.5 6.6 collective-permute-done.3
  140.8 16.8 %collective-permute-done.8.refs_3_ = bf16[2,3,256,256]{3,2,1,0:T(8,128)(2,1)} collective-permute-done((bf16[2,3,256,256]{3,2,1,0:T(8,128)(2,1)}, bf16[2,3,256,256]{3,2,1,0:T(8,128)(2,1)}, u32[]{:S(2)}, u32[]{:S(2)}) %collective-permute-start.8) | collective-permute-done | bytes 786464 | tf_op jit(solution)/shard_map/ppermute | solution.py:338
  157.6 7.4 shard_map.434
  174.5 16.4 %collective-permute-done.16.refs_3_ = bf16[2,3,256,256]{3,2,1,0:T(8,128)(2,1)} collective-permute-done((bf16[2,3,256,256]{3,2,1,0:T(8,128)(2,1)}, bf16[2,3,256,256]{3,2,1,0:T(8,128)(2,1)}, u32[]{:S(2)}, u32[]{:S(2)}) %collective-permute-start.16) | collective-permute-done | bytes 786464 | tf_op jit(solution)/shard_map/ppermute | solution.py:338
  190.9 7.4 shard_map.436
  217.3 6.6 collective-permute-done.40
  226.4 5.8 collective-permute-done.18
  252.4 8.6 collective-permute-done.25.refs_2_
  261.0 22.5 %collective-permute-done.26.refs_3_ = bf16[2,2,512,256]{3,2,1,0:T(8,128)(2,1)} collective-permute-done((bf16[2,2,512,256]{3,2,1,0:T(8,128)(2,1)}, bf16[2,2,512,256]{3,2,1,0:T(8,128)(2,1)}, u32[]{:S(2)}, u32[]{:S(2)}) %collective-permute-start.26) | collective-permute-done | bytes 1048608 | tf_op jit(solution)/shard_map/ppermute | solution.py:338
  283.5 8.1 shard_map.437
  342.2 17.7 %collective-permute-done.46 = bf16[128,2048]{1,0:T(8,128)(2,1)S(1)} collective-permute-done((bf16[128,2048]{1,0:T(8,128)(2,1)S(1)}, bf16[128,2048]{1,0:T(8,128)(2,1)S(1)}, u32[]{:S(2)}, u32[]{:S(2)}) %collective-permute-start.46) | collective-permute-done | bytes 524320 | tf_op jit(solution)/shard_map/ppermute | solution.py:271
  364.0 23.5 %all-gather.28.cloned.1.call-done = bf16[4,1024,256]{2,1,0:T(8,128)(2,1)} async-done(((bf16[2,1024,256]{2,1,0:T(8,128)(2,1)}), bf16[4,1024,256]{2,1,0:T(8,128)(2,1)}) %all-gather.28.cloned.1.call-update) | async-done | bytes 2097168 | tf_op jit(solution)/shard_map/all_gather | solution.py:332
  394.9 6.0 collective-permute-done.30.refs_3_
  402.5 8.1 shard_map.439
  410.6 8.6 collective-permute-done.35.refs_3_
  419.2 8.6 shard_map.440
  429.8 7.2 collective-permute-done.48
  438.9 7.4 collective-permute-done.49
  464.8 5.7 collective-permute-done.37
  472.3 6.6 collective-permute-done.52
  490.6 7.0 collective-permute-done.55
  499.6 7.2 collective-permute-done.56
  508.0 8.4 collective-permute-done.65
  526.2 7.8 shard_map.443
  534.1 6.9 convert_reduce_fusion
  548.9 5.7 collective-permute-done.59
  578.8 7.0 shard_map.446
  592.0 5.8 collective-permute-done.74
  602.9 11.9 %collective-permute-done.67.refs_4_ = bf16[4,1024,256]{2,1,0:T(8,128)(2,1)} collective-permute-done((bf16[4,1024,256]{2,1,0:T(8,128)(2,1)}, bf16[4,1024,256]{2,1,0:T(8,128)(2,1)}, u32[]{:S(2)}, u32[]{:S(2)}) %collective-permute-start.67) | collective-permute-done | bytes 2097184 | tf_op jit(solution)/shard_map/ppermute | solution.py:369
  614.8 8.6 shard_map.444
  656.5 8.1 collective-permute-done.88
  676.3 7.4 shard_map.448
  683.7 7.5 shard_map.452
  694.2 5.9 shard_map.451
  706.8 6.8 convolution_convert_fusion
  730.2 8.3 shard_map.449
  744.6 11.9 %collective-permute-done.86 = bf16[128,2048]{1,0:T(8,128)(2,1)} collective-permute-done((bf16[128,2048]{1,0:T(8,128)(2,1)}, bf16[128,2048]{1,0:T(8,128)(2,1)}, u32[]{:S(2)}, u32[]{:S(2)}) %collective-permute-start.86) | collective-permute-done | bytes 524320 | tf_op jit(solution)/shard_map/ppermute | solution.py:261
  757.8 17.3 %collective-permute-start.87 = (bf16[256,2048]{1,0:T(8,128)(2,1)S(1)}, bf16[256,2048]{1,0:T(8,128)(2,1)S(1)}, u32[]{:S(2)}, u32[]{:S(2)}) collective-permute-start(bf16[256,2048]{1,0:T(8,128)(2,1)S(1)} %pad_maximum_fusion.21), channel_id=1, source_target_pairs={{0,1},{1,0},{2,3},{3,2},{4,5},{5,4},{6,7},{7,6},{8,9},{9,8},{10,11... | collective-permute-start | bytes 3145736 | tf_op jit(solution)/shard_map/ppermute | solution.py:262
  803.6 6.3 shard_map.455
  818.4 6.5 shard_map.456
  838.4 9.7 collective-permute-done.109
  872.8 11.9 %collective-permute-done.96 = bf16[128,2048]{1,0:T(8,128)(2,1)} collective-permute-done((bf16[128,2048]{1,0:T(8,128)(2,1)}, bf16[128,2048]{1,0:T(8,128)(2,1)}, u32[]{:S(2)}, u32[]{:S(2)}) %collective-permute-start.96) | collective-permute-done | bytes 524320 | tf_op jit(solution)/shard_map/ppermute | solution.py:271
  894.7 6.7 shard_map.458
  934.2 23.9 %collective-permute-done.103 = bf16[256,256]{1,0:T(8,128)(2,1)S(1)} collective-permute-done((bf16[256,256]{1,0:T(8,128)(2,1)S(1)}, bf16[256,256]{1,0:T(8,128)(2,1)S(1)}, u32[]{:S(2)}, u32[]{:S(2)}) %collective-permute-start.103) | collective-permute-done | bytes 131104 | tf_op jit(solution)/shard_map/ppermute | solution.py:316
  (900 shorter events, 517.8 us)
Async XLA Ops:
  7.2 114.5 %all-gather.20.cloned.1.call-start = ((), (), s32[]{:S(2)}) async-start(), calls=%async_computation.5 | async-start | bytes 2359296 | tf_op jit(solution)/shard_map/all_gather | solution.py:332
  13.5 82.4 %collective-permute-start.9 = (s32[768]{0:T(1024)}, s32[768]{0:T(1024)}, u32[]{:S(2)}, u32[]{:S(2)}) collective-permute-start(s32[768]{0:T(1024)} %pad_add_fusion), channel_id=1, source_target_pairs={{0,8},{4,12},{8,0},{12,4},{16,24},{20,28},{24,16},{28,20},{1,9},{5... | collective-permute-start | bytes 9224 | tf_op jit(solution)/shard_map/ppermute | solution.py:316
  13.5 83.1 %collective-permute-start.23 = (bf16[256,1024]{1,0:T(8,128)(2,1)}, bf16[256,1024]{1,0:T(8,128)(2,1)}, u32[]{:S(2)}, u32[]{:S(2)}) collective-permute-start(bf16[256,1024]{1,0:T(8,128)(2,1)} %param.36), channel_id=1, source_target_pairs={{0,8},{4,12},{8,0},{12,4},{16,24},{20,28},{24,16},{28,20},{1,9},{5... | collective-permute-start | bytes 1572872 | tf_op jit(solution)/shard_map/ppermute | solution.py:316
  24.5 104.4 %all-gather.24.cloned.1.call-start = ((), (), s32[]{:S(2)}) async-start(), calls=%async_computation.7 | async-start | bytes 2359296 | tf_op jit(solution)/shard_map/all_gather | solution.py:332
  34.6 35.7 %collective-permute-start.1 = (bf16[2,64,2048]{2,1,0:T(8,128)(2,1)S(1)}, bf16[2,64,2048]{2,1,0:T(8,128)(2,1)S(1)}, u32[]{:S(2)}, u32[]{:S(2)}) collective-permute-start(bf16[2,64,2048]{2,1,0:T(8,128)(2,1)S(1)} %get-tuple-element.238), channel_id=1, source_target_pairs={{0,8},{4,12},{8,0},{12,4},{16,24},{20,28},{24,16},{28,20},{1,9},{5... | collective-permute-start | bytes 1572872 | tf_op jit(solution)/shard_map/ppermute | solution.py:316
  51.1 158.5 %all-gather.22.cloned.1.call-start = ((), (), s32[]{:S(2)}) async-start(), calls=%async_computation.6 | async-start | bytes 3145728 | tf_op jit(solution)/shard_map/all_gather | solution.py:332
  51.2 29.5 %collective-permute-start.6 = (bf16[2,512,256]{2,1,0:T(8,128)(2,1)S(1)}, bf16[2,512,256]{2,1,0:T(8,128)(2,1)S(1)}, u32[]{:S(2)}, u32[]{:S(2)}) collective-permute-start(bf16[2,512,256]{2,1,0:T(8,128)(2,1)S(1)} %get-tuple-element.68), channel_id=1, source_target_pairs={{0,8},{4,12},{8,0},{12,4},{16,24},{20,28},{24,16},{28,20},{1,9},{5... | collective-permute-start | bytes 1572872 | tf_op jit(solution)/shard_map/ppermute | solution.py:316
  81.7 209.9 %all-gather.14.cloned.1.call-start = ((), (), s32[]{:S(2)}) async-start(), calls=%async_computation.1 | async-start | bytes 5242880 | tf_op jit(solution)/shard_map/all_gather | solution.py:461
  99.4 195.5 %all-gather.26.cloned.1.call-start = ((), (), s32[]{:S(2)}) async-start(), calls=%async_computation.8 | async-start | bytes 3145728 | tf_op jit(solution)/shard_map/all_gather | solution.py:332
  123.8 33.9 %collective-permute-start.8 = (bf16[2,3,256,256]{3,2,1,0:T(8,128)(2,1)}, bf16[2,3,256,256]{3,2,1,0:T(8,128)(2,1)}, u32[]{:S(2)}, u32[]{:S(2)}) collective-permute-start(bf16[2,3,256,256]{3,2,1,0:T(8,128)(2,1)} %dynamic-slice_bitcast_fusion.4.refs_1_), channel_id=1, source_target_pairs={{0,4},{4,0},{8,12},{12,8},{16,20},{20,16},{24,28},{28,24},{1,5},{5... | collective-permute-start | bytes 2359304 | tf_op jit(solution)/shard_map/ppermute | solution.py:338
  127.3 47.2 %collective-permute-start.15 = (bf16[2,3,256,256]{3,2,1,0:T(8,128)(2,1)}, bf16[2,3,256,256]{3,2,1,0:T(8,128)(2,1)}, u32[]{:S(2)}, u32[]{:S(2)}) collective-permute-start(bf16[2,3,256,256]{3,2,1,0:T(8,128)(2,1)} %pad_maximum_fusion.23.refs_0_), channel_id=1, source_target_pairs={{0,4},{4,0},{8,12},{12,8},{16,20},{20,16},{24,28},{28,24},{1,5},{5... | collective-permute-start | bytes 2359304 | tf_op jit(solution)/shard_map/ppermute | solution.py:337
  131.0 59.9 %collective-permute-start.16 = (bf16[2,3,256,256]{3,2,1,0:T(8,128)(2,1)}, bf16[2,3,256,256]{3,2,1,0:T(8,128)(2,1)}, u32[]{:S(2)}, u32[]{:S(2)}) collective-permute-start(bf16[2,3,256,256]{3,2,1,0:T(8,128)(2,1)} %dynamic-slice_bitcast_fusion.3.refs_1_), channel_id=1, source_target_pairs={{0,4},{4,0},{8,12},{12,8},{16,20},{20,16},{24,28},{28,24},{1,5},{5... | collective-permute-start | bytes 2359304 | tf_op jit(solution)/shard_map/ppermute | solution.py:338
  134.3 77.6 %collective-permute-start.14 = (bf16[1024,256]{1,0:T(8,128)(2,1)}, bf16[1024,256]{1,0:T(8,128)(2,1)}, u32[]{:S(2)}, u32[]{:S(2)}) collective-permute-start(bf16[1024,256]{1,0:T(8,128)(2,1)} %get-tuple-element.71), channel_id=1, source_target_pairs={{0,8},{4,12},{8,0},{12,4},{16,24},{20,28},{24,16},{28,20},{1,9},{5... | collective-permute-start | bytes 1572872 | tf_op jit(solution)/shard_map/ppermute | solution.py:316
  140.8 71.1 %collective-permute-start.13 = (bf16[256,1024]{1,0:T(8,128)(2,1)}, bf16[256,1024]{1,0:T(8,128)(2,1)}, u32[]{:S(2)}, u32[]{:S(2)}) collective-permute-start(bf16[256,1024]{1,0:T(8,128)(2,1)} %get-tuple-element.70), channel_id=1, source_target_pairs={{0,8},{4,12},{8,0},{12,4},{16,24},{20,28},{24,16},{28,20},{1,9},{5... | collective-permute-start | bytes 1572872 | tf_op jit(solution)/shard_map/ppermute | solution.py:316
  238.5 149.0 %all-gather.28.cloned.1.call-start = ((), (), s32[]{:S(2)}) async-start(), calls=%async_computation.9 | async-start | bytes 3145728 | tf_op jit(solution)/shard_map/all_gather | solution.py:332
  238.8 44.7 %collective-permute-start.26 = (bf16[2,2,512,256]{3,2,1,0:T(8,128)(2,1)}, bf16[2,2,512,256]{3,2,1,0:T(8,128)(2,1)}, u32[]{:S(2)}, u32[]{:S(2)}) collective-permute-start(bf16[2,2,512,256]{3,2,1,0:T(8,128)(2,1)} %dynamic-slice_bitcast_fusion.2.refs_1_), channel_id=1, source_target_pairs={{0,4},{4,0},{8,12},{12,8},{16,20},{20,16},{24,28},{28,24},{1,5},{5... | collective-permute-start | bytes 3145736 | tf_op jit(solution)/shard_map/ppermute | solution.py:338
  244.6 55.3 %collective-permute-start.24 = (bf16[2,256,1024]{2,1,0:T(8,128)(2,1)S(1)}, bf16[2,256,1024]{2,1,0:T(8,128)(2,1)}, u32[]{:S(2)}, u32[]{:S(2)}) collective-permute-start(bf16[2,256,1024]{2,1,0:T(8,128)(2,1)S(1)} %copy-done.35), channel_id=1, source_target_pairs={{0,4},{4,0},{8,12},{12,8},{16,20},{20,16},{24,28},{28,24},{1,5},{5... | collective-permute-start | bytes 3145736 | tf_op jit(solution)/shard_map/ppermute | solution.py:337
  251.8 45.4 %collective-permute-start.21 = (bf16[128,2048]{1,0:T(8,128)(2,1)}, bf16[128,2048]{1,0:T(8,128)(2,1)}, u32[]{:S(2)}, u32[]{:S(2)}) collective-permute-start(bf16[128,2048]{1,0:T(8,128)(2,1)} %pad_maximum_fusion.26), channel_id=1, source_target_pairs={{0,8},{1,3},{2,10},{3,1},{4,12},{5,7},{6,14},{7,5},{8,0},{9,11},{1... | collective-permute-start | bytes 1572872 | tf_op jit(solution)/shard_map/ppermute | solution.py:261
  329.3 325.3 %all-gather.16.cloned.1.call-start = ((), (), s32[]{:S(2)}) async-start(), calls=%async_computation.2 | async-start | bytes 2621440 | tf_op jit(solution)/shard_map/all_gather | solution.py:644
  340.6 50.9 %collective-permute-start.29 = (bf16[64,2048]{1,0:T(8,128)(2,1)S(1)}, bf16[64,2048]{1,0:T(8,128)(2,1)S(1)}, u32[]{:S(2)}, u32[]{:S(2)}) collective-permute-start(bf16[64,2048]{1,0:T(8,128)(2,1)S(1)} %slice.826), channel_id=1, source_target_pairs={{0,2},{1,9},{2,0},{3,11},{4,6},{5,13},{6,4},{7,15},{8,10},{9,1},{1... | collective-permute-start | bytes 786440 | tf_op jit(solution)/shard_map/ppermute | solution.py:273
  361.0 30.5 %collective-permute-start.47 = (bf16[64,2048]{1,0:T(8,128)(2,1)S(1)}, bf16[64,2048]{1,0:T(8,128)(2,1)S(1)}, u32[]{:S(2)}, u32[]{:S(2)}) collective-permute-start(bf16[64,2048]{1,0:T(8,128)(2,1)S(1)} %slice.823), channel_id=1, source_target_pairs={{0,2},{1,9},{2,0},{3,11},{4,6},{5,13},{6,4},{7,15},{8,10},{9,1},{1... | collective-permute-start | bytes 786440 | tf_op jit(solution)/shard_map/ppermute | solution.py:273
  362.0 48.6 %collective-permute-start.34 = (bf16[2,1024,256]{2,1,0:T(8,128)(2,1)}, bf16[2,1024,256]{2,1,0:T(8,128)(2,1)}, u32[]{:S(2)}, u32[]{:S(2)}) collective-permute-start(bf16[2,1024,256]{2,1,0:T(8,128)(2,1)} %pad_maximum_fusion.12.refs_0_), channel_id=1, source_target_pairs={{0,4},{4,0},{8,12},{12,8},{16,20},{20,16},{24,28},{28,24},{1,5},{5... | collective-permute-start | bytes 3145736 | tf_op jit(solution)/shard_map/ppermute | solution.py:337
  363.6 37.3 %collective-permute-start.30 = (bf16[2,256,1024]{2,1,0:T(8,128)(2,1)}, bf16[2,256,1024]{2,1,0:T(8,128)(2,1)}, u32[]{:S(2)}, u32[]{:S(2)}) collective-permute-start(bf16[2,256,1024]{2,1,0:T(8,128)(2,1)} %dynamic-slice_bitcast_fusion.1.refs_1_), channel_id=1, source_target_pairs={{0,4},{4,0},{8,12},{12,8},{16,20},{20,16},{24,28},{28,24},{1,5},{5... | collective-permute-start | bytes 3145736 | tf_op jit(solution)/shard_map/ppermute | solution.py:338
  390.0 29.2 %collective-permute-start.35 = (bf16[2,1024,256]{2,1,0:T(8,128)(2,1)}, bf16[2,1024,256]{2,1,0:T(8,128)(2,1)}, u32[]{:S(2)}, u32[]{:S(2)}) collective-permute-start(bf16[2,1024,256]{2,1,0:T(8,128)(2,1)} %dynamic-slice_bitcast_fusion.refs_1_), channel_id=1, source_target_pairs={{0,4},{4,0},{8,12},{12,8},{16,20},{20,16},{24,28},{28,24},{1,5},{5... | collective-permute-start | bytes 3145736 | tf_op jit(solution)/shard_map/ppermute | solution.py:338
  566.0 48.8 %collective-permute-start.67 = (bf16[4,1024,256]{2,1,0:T(8,128)(2,1)}, bf16[4,1024,256]{2,1,0:T(8,128)(2,1)}, u32[]{:S(2)}, u32[]{:S(2)}) collective-permute-start(bf16[4,1024,256]{2,1,0:T(8,128)(2,1)} %shard_map.443), channel_id=1, source_target_pairs={{0,4},{4,0},{8,12},{12,8},{16,20},{20,16},{24,28},{28,24},{1,5},{5... | collective-permute-start | bytes 6291464 | tf_op jit(solution)/shard_map/ppermute | solution.py:369
  592.0 379.0 %reduce-scatter.2.cloned.1.call-start = ((), (), s32[]{:S(2)}) async-start(), calls=%async_computation.4 | async-start | bytes 5242880 | tf_op jit(solution)/shard_map/reduce_scatter | solution.py:608
  599.8 31.9 %collective-permute-start.63 = (bf16[256,2048]{1,0:T(8,128)(2,1)}, bf16[256,2048]{1,0:T(8,128)(2,1)}, u32[]{:S(2)}, u32[]{:S(2)}) collective-permute-start(bf16[256,2048]{1,0:T(8,128)(2,1)} %pad_maximum_fusion.17), channel_id=1, source_target_pairs={{0,1},{1,0},{2,3},{3,2},{4,5},{5,4},{6,7},{7,6},{8,9},{9,8},{10,11... | collective-permute-start | bytes 3145736 | tf_op jit(solution)/shard_map/ppermute | solution.py:262
  600.3 83.3 %collective-permute-start.84 = (bf16[4,256,1024]{2,1,0:T(8,128)(2,1)}, bf16[4,256,1024]{2,1,0:T(8,128)(2,1)}, u32[]{:S(2)}, u32[]{:S(2)}) collective-permute-start(bf16[4,256,1024]{2,1,0:T(8,128)(2,1)} %shard_map.446), channel_id=1, source_target_pairs={{0,4},{4,0},{8,12},{12,8},{16,20},{20,16},{24,28},{28,24},{1,5},{5... | collective-permute-start | bytes 6291464 | tf_op jit(solution)/shard_map/ppermute | solution.py:369
  623.4 41.2 %collective-permute-start.88 = (bf16[2,1024,256]{2,1,0:T(8,128)(2,1)}, bf16[2,1024,256]{2,1,0:T(8,128)(2,1)}, u32[]{:S(2)}, u32[]{:S(2)}) collective-permute-start(bf16[2,1024,256]{2,1,0:T(8,128)(2,1)} %get-tuple-element.82), channel_id=1, source_target_pairs={{0,16},{4,20},{8,24},{12,28},{16,0},{20,4},{24,8},{28,12},{1,17},{... | collective-permute-start | bytes 3145736 | tf_op jit(solution)/shard_map/ppermute | solution.py:375
  669.5 30.6 %collective-permute-start.72 = (bf16[128,2048]{1,0:T(8,128)(2,1)}, bf16[128,2048]{1,0:T(8,128)(2,1)}, u32[]{:S(2)}, u32[]{:S(2)}) collective-permute-start(bf16[128,2048]{1,0:T(8,128)(2,1)} %slice.807), channel_id=1, source_target_pairs={{0,8},{1,3},{2,10},{3,1},{4,12},{5,7},{6,14},{7,5},{8,0},{9,11},{1... | collective-permute-start | bytes 1572872 | tf_op jit(solution)/shard_map/ppermute | solution.py:271
  673.9 30.6 %collective-permute-start.82 = (bf16[128,2048]{1,0:T(8,128)(2,1)}, bf16[128,2048]{1,0:T(8,128)(2,1)}, u32[]{:S(2)}, u32[]{:S(2)}) collective-permute-start(bf16[128,2048]{1,0:T(8,128)(2,1)} %slice.806), channel_id=1, source_target_pairs={{0,8},{1,3},{2,10},{3,1},{4,12},{5,7},{6,14},{7,5},{8,0},{9,11},{1... | collective-permute-start | bytes 1572872 | tf_op jit(solution)/shard_map/ppermute | solution.py:271
  691.1 39.1 %collective-permute-start.80 = (bf16[4,256,512]{2,1,0:T(8,128)(2,1)}, bf16[4,256,512]{2,1,0:T(8,128)(2,1)}, u32[]{:S(2)}, u32[]{:S(2)}) collective-permute-start(bf16[4,256,512]{2,1,0:T(8,128)(2,1)} %shard_map.448), channel_id=1, source_target_pairs={{0,4},{4,0},{8,12},{12,8},{16,20},{20,16},{24,28},{28,24},{1,5},{5... | collective-permute-start | bytes 3145736 | tf_op jit(solution)/shard_map/ppermute | solution.py:369
  693.1 124.9 %collective-permute-start.108 = (bf16[2,256,1024]{2,1,0:T(8,128)(2,1)}, bf16[2,256,1024]{2,1,0:T(8,128)(2,1)}, u32[]{:S(2)}, u32[]{:S(2)}) collective-permute-start(bf16[2,256,1024]{2,1,0:T(8,128)(2,1)} %get-tuple-element.96), channel_id=1, source_target_pairs={{0,16},{4,20},{8,24},{12,28},{16,0},{20,4},{24,8},{28,12},{1,17},{... | collective-permute-start | bytes 3145736 | tf_op jit(solution)/shard_map/ppermute | solution.py:375
  713.6 278.7 %all-gather.18.cloned.1.call-start = ((), (), s32[]{:S(2)}) async-start(), calls=%async_computation.3 | async-start | bytes 2621440 | tf_op jit(solution)/shard_map/all_gather | solution.py:644
  713.7 104.3 %collective-permute-start.94 = (bf16[4,512,512]{2,1,0:T(8,128)(2,1)}, bf16[4,512,512]{2,1,0:T(8,128)(2,1)}, u32[]{:S(2)}, u32[]{:S(2)}) collective-permute-start(bf16[4,512,512]{2,1,0:T(8,128)(2,1)} %shard_map.451), channel_id=1, source_target_pairs={{0,4},{4,0},{8,12},{12,8},{16,20},{20,16},{24,28},{28,24},{1,5},{5... | collective-permute-start | bytes 6291464 | tf_op jit(solution)/shard_map/ppermute | solution.py:369
  726.4 30.2 %collective-permute-start.86 = (bf16[128,2048]{1,0:T(8,128)(2,1)}, bf16[128,2048]{1,0:T(8,128)(2,1)}, u32[]{:S(2)}, u32[]{:S(2)}) collective-permute-start(bf16[128,2048]{1,0:T(8,128)(2,1)} %pad_maximum_fusion.35), channel_id=1, source_target_pairs={{0,8},{1,3},{2,10},{3,1},{4,12},{5,7},{6,14},{7,5},{8,0},{9,11},{1... | collective-permute-start | bytes 1572872 | tf_op jit(solution)/shard_map/ppermute | solution.py:261
  729.8 45.3 %collective-permute-start.78 = (bf16[128,2048]{1,0:T(8,128)(2,1)}, bf16[128,2048]{1,0:T(8,128)(2,1)}, u32[]{:S(2)}, u32[]{:S(2)}) collective-permute-start(bf16[128,2048]{1,0:T(8,128)(2,1)} %pad_maximum_fusion.34), channel_id=1, source_target_pairs={{0,8},{1,3},{2,10},{3,1},{4,12},{5,7},{6,14},{7,5},{8,0},{9,11},{1... | collective-permute-start | bytes 1572872 | tf_op jit(solution)/shard_map/ppermute | solution.py:261
  738.5 86.4 %collective-permute-start.104 = (bf16[2,256,512]{2,1,0:T(8,128)(2,1)}, bf16[2,256,512]{2,1,0:T(8,128)(2,1)}, u32[]{:S(2)}, u32[]{:S(2)}) collective-permute-start(bf16[2,256,512]{2,1,0:T(8,128)(2,1)} %get-tuple-element.90), channel_id=1, source_target_pairs={{0,16},{4,20},{8,24},{12,28},{16,0},{20,4},{24,8},{28,12},{1,17},{... | collective-permute-start | bytes 1572872 | tf_op jit(solution)/shard_map/ppermute | solution.py:375
  809.9 57.0 %collective-permute-start.93 = (bf16[4,256,256]{2,1,0:T(8,128)(2,1)}, bf16[4,256,256]{2,1,0:T(8,128)(2,1)}, u32[]{:S(2)}, u32[]{:S(2)}) collective-permute-start(bf16[4,256,256]{2,1,0:T(8,128)(2,1)} %shard_map.453), channel_id=1, source_target_pairs={{0,4},{4,0},{8,12},{12,8},{16,20},{20,16},{24,28},{28,24},{1,5},{5... | collective-permute-start | bytes 1572872 | tf_op jit(solution)/shard_map/ppermute | solution.py:369
  810.5 84.3 %collective-permute-start.92 = (bf16[4,256,768]{2,1,0:T(8,128)(2,1)}, bf16[4,256,768]{2,1,0:T(8,128)(2,1)}, u32[]{:S(2)}, u32[]{:S(2)}) collective-permute-start(bf16[4,256,768]{2,1,0:T(8,128)(2,1)} %shard_map.455), channel_id=1, source_target_pairs={{0,4},{4,0},{8,12},{12,8},{16,20},{20,16},{24,28},{28,24},{1,5},{5... | collective-permute-start | bytes 4718600 | tf_op jit(solution)/shard_map/ppermute | solution.py:369
  817.9 34.0 %collective-permute-start.95 = (bf16[256,2048]{1,0:T(8,128)(2,1)}, bf16[256,2048]{1,0:T(8,128)(2,1)}, u32[]{:S(2)}, u32[]{:S(2)}) collective-permute-start(bf16[256,2048]{1,0:T(8,128)(2,1)} %convolution_convert_fusion.11), channel_id=1, source_target_pairs={{0,1},{1,0},{2,3},{3,2},{4,5},{5,4},{6,7},{7,6},{8,9},{9,8},{10,11... | collective-permute-start | bytes 3145736 | tf_op jit(solution)/shard_map/ppermute | solution.py:267
  817.9 38.8 %collective-permute-start.89 = (bf16[256,2048]{1,0:T(8,128)(2,1)}, bf16[256,2048]{1,0:T(8,128)(2,1)}, u32[]{:S(2)}, u32[]{:S(2)}) collective-permute-start(bf16[256,2048]{1,0:T(8,128)(2,1)} %convolution_convert_fusion.12), channel_id=1, source_target_pairs={{0,1},{1,0},{2,3},{3,2},{4,5},{5,4},{6,7},{7,6},{8,9},{9,8},{10,11... | collective-permute-start | bytes 3145736 | tf_op jit(solution)/shard_map/ppermute | solution.py:267
  848.1 53.4 %collective-permute-start.106 = (bf16[2,512,512]{2,1,0:T(8,128)(2,1)}, bf16[2,512,512]{2,1,0:T(8,128)(2,1)}, u32[]{:S(2)}, u32[]{:S(2)}) collective-permute-start(bf16[2,512,512]{2,1,0:T(8,128)(2,1)} %get-tuple-element.103), channel_id=1, source_target_pairs={{0,16},{4,20},{8,24},{12,28},{16,0},{20,4},{24,8},{28,12},{1,17},{... | collective-permute-start | bytes 3145736 | tf_op jit(solution)/shard_map/ppermute | solution.py:375
  860.6 31.3 %collective-permute-start.90 = (bf16[128,2048]{1,0:T(8,128)(2,1)}, bf16[128,2048]{1,0:T(8,128)(2,1)}, u32[]{:S(2)}, u32[]{:S(2)}) collective-permute-start(bf16[128,2048]{1,0:T(8,128)(2,1)} %slice.805), channel_id=1, source_target_pairs={{0,8},{1,3},{2,10},{3,1},{4,12},{5,7},{6,14},{7,5},{8,0},{9,11},{1... | collective-permute-start | bytes 1572872 | tf_op jit(solution)/shard_map/ppermute | solution.py:271
  872.5 34.2 %collective-permute-start.102 = (bf16[2,256,256]{2,1,0:T(8,128)(2,1)}, bf16[2,256,256]{2,1,0:T(8,128)(2,1)}, u32[]{:S(2)}, u32[]{:S(2)}) collective-permute-start(bf16[2,256,256]{2,1,0:T(8,128)(2,1)} %get-tuple-element.106), channel_id=1, source_target_pairs={{0,16},{4,20},{8,24},{12,28},{16,0},{20,4},{24,8},{28,12},{1,17},{... | collective-permute-start | bytes 786440 | tf_op jit(solution)/shard_map/ppermute | solution.py:375
  923.5 42.8 %collective-permute-start.100 = (bf16[2,256,768]{2,1,0:T(8,128)(2,1)}, bf16[2,256,768]{2,1,0:T(8,128)(2,1)}, u32[]{:S(2)}, u32[]{:S(2)}) collective-permute-start(bf16[2,256,768]{2,1,0:T(8,128)(2,1)} %get-tuple-element.109), channel_id=1, source_target_pairs={{0,16},{4,20},{8,24},{12,28},{16,0},{20,4},{24,8},{28,12},{1,17},{... | collective-permute-start | bytes 2359304 | tf_op jit(solution)/shard_map/ppermute | solution.py:375
  926.9 34.9 %collective-permute-start.107 = (bf16[512,512]{1,0:T(8,128)(2,1)}, bf16[512,512]{1,0:T(8,128)(2,1)}, u32[]{:S(2)}, u32[]{:S(2)}) collective-permute-start(bf16[512,512]{1,0:T(8,128)(2,1)} %fusion.54), channel_id=1, source_target_pairs={{0,8},{4,12},{8,0},{12,4},{16,24},{20,28},{24,16},{28,20},{1,9},{5... | collective-permute-start | bytes 1572872 | tf_op jit(solution)/shard_map/ppermute | solution.py:316
  928.9 29.2 %collective-permute-start.103 = (bf16[256,256]{1,0:T(8,128)(2,1)S(1)}, bf16[256,256]{1,0:T(8,128)(2,1)S(1)}, u32[]{:S(2)}, u32[]{:S(2)}) collective-permute-start(bf16[256,256]{1,0:T(8,128)(2,1)S(1)} %copy-done.137), channel_id=1, source_target_pairs={{0,8},{4,12},{8,0},{12,4},{16,24},{20,28},{24,16},{28,20},{1,9},{5... | collective-permute-start | bytes 393224 | tf_op jit(solution)/shard_map/ppermute | solution.py:316
  (252 other events, 2752.3 us)
Sparse Core Ops, SparseCore 0:
  24.6 45.7 all-gather.19
  72.5 45.0 all-gather.23
  119.8 55.4 all-gather.21
  177.3 33.4 all-gather.13
  238.6 56.1 all-gather.25
  329.5 57.9 all-gather.27
  592.1 23.9 all-gather.15
  713.7 44.5 reduce-scatter.1
  934.0 20.0 all-gather.17

commit v3 on v2

--- a/solution.py
+++ b/solution.py
@@ -3,6 +3,7 @@
 import jax
 import jax.numpy as jnp
 from jax import lax
+from jax.experimental.layout import Layout, with_layout_constraint
 from jax.experimental import pallas as pl
 from jax.experimental.pallas import tpu as pltpu
 from jax.sharding import PartitionSpec as P
@@ -254,6 +255,9 @@
     first_hop = [(i * n_mp + m, side(i, m) if m % 2 == 0 else lower(i, m)) for i, m in pairs]
     second_hop = [(i * n_mp + m, lower(i, m) if m % 2 == 0 else side(i, m)) for i, m in pairs]
     high_groups = [[h * 4 + low for h in range(n_hi)] for low in range(4)]
+    data_groups = [
+        [h * 4 + low * 2 + y for h in range(n_hi) for y in range(2)] for low in range(2)
+    ]
 
     def gather_tokens(own):
         near = lax.ppermute(own, BOTH, first_hop)
@@ -358,6 +362,25 @@
 
             return assembled(xor_order([0, 2, 4, 6, 1, 3, 5, 7]), pieces, kinds, shapes, n_dp)
 
+        def all_blocks(terms):
+            if n_hi != 2:
+                return ()
+            j = jnp.arange(8, dtype=jnp.int32)
+            order = (j // 4 * 4 + (low ^ (j % 2)) * 2 + j // 2 % 2).astype(jnp.int32)
+            return (grad_blocks(order, terms, n_dp, [8])[0],)
+
+        def scattered(terms, blocks, axis, *gates):
+            if n_hi != 2:
+                return collected(terms, (), (), axis)
+            total = lax.psum_scatter(
+                blocks[0].reshape((4, 2) + blocks[0].shape[1:]),
+                "dp",
+                scatter_dimension=0,
+                axis_index_groups=data_groups,
+            )
+            total = after(with_layout_constraint(total, Layout((0, 1, 2))), *gates)
+            return ordered(total[0].astype(f32), swap_low(total[1]).astype(f32), axis)
+
         def first_blocks(terms):
             if n_hi != 2:
                 return ()
@@ -534,7 +557,7 @@
             return [(value, value.shape[0], 0) for value in values]
 
         down_term = [("col", streams(act), streams(low_mlp))]
-        down = first_blocks(down_term)
+        down = all_blocks(down_term)
         grad_pre, grad_in = [], []
         for r in rows:
             ready = low_mlp[r] if r == 0 else after(low_mlp[r], *down)
@@ -542,7 +565,7 @@
             grad_pre.append(jax.vjp(gelu_tanh, pre_act[r])[1](grad_act)[0].astype(bf16))
             grad_in.append(scatter_tokens(grad_pre[r], full_up, across))
         up_term = [("row", streams(hid_three), streams(grad_pre))]
-        up = first_blocks(up_term)
+        up = all_blocks(up_term)
         grad_after_cross, low_cross = [], []
         for r in rows:
             grad_after_cross.append(grad_mlp[r] + back_norm(2, r, grad_in[r]))
@@ -553,11 +576,9 @@
             grad_pre[1].astype(f32), axis=0
         )
 
-        down_second = second_blocks(down_term, down, *grad_in)
         cq_low, ckv_low, grad_in = [], [], []
         for r in rows:
-            ready = after(low_cross[r], *down_second) if r == 0 else low_cross[r]
-            grad_mixed = dot(ready, full_cout, across).astype(bf16)
+            grad_mixed = dot(low_cross[r], full_cout, across).astype(bf16)
             dq, dkv = attend_back(
                 cross_q[r], cross_kv, r, 0, grad_mixed, q_ids[r], t_ids[r], heads
             )
@@ -568,61 +589,64 @@
         cout_term = ("col", streams(cross_mixed), streams(low_cross))
         kv_term = [("row", [(words, text_len, r) for r in rows], streams(ckv_low))]
         both_term = [cq_term, cout_term]
-        both_first, kv_first = first_blocks(both_term), first_blocks(kv_term)
+        both_first, kv_first = first_blocks(both_term), all_blocks(kv_term)
         grad_after_self, low_self = [], []
         for r in rows:
             grad_after_self.append(grad_after_cross[r] + back_norm(1, r, grad_in[r]))
             biases[0] = biases[0] + jnp.sum(grad_after_self[r], axis=0)
             ready = grad_after_self[r].astype(bf16)
-            if r == 1:
-                up_second = second_blocks(up_term, up, *cq_low)
-            gates = kv_first + up_second if r else both_first
+            gates = kv_first if r else both_first
             low_self.append(gather_tokens(after(ready, *gates)))
-        text_term = dot(jnp.concatenate(ckv_low), full_kv, across).astype(bf16)
-
-        down_far = across_high(down_second, *cq_low)
-        out_term = [("col", streams(mixed), streams(low_self))]
-        out_first = first_blocks(out_term)
+
+        keys_low = jnp.concatenate(ckv_low)
+        width, x_at = text_dim // n_mp, m // 2
+
+        def text_part(owner):
+            rows_of = lax.dynamic_slice_in_dim(full_kv, owner * width, width, 0)
+            return dot(keys_low, rows_of, across)
+
+        def text_sum(side):
+            away = text_part(side * 2 + 1 - core).astype(bf16)
+            return text_part(side * 2 + core) + lax.ppermute(away, "mp", core_swap).astype(f32)
+
+        arrived = lax.ppermute(text_sum(1 - x_at).astype(bf16), "mp", side_swap)
+        text_total = (text_sum(x_at) + arrived.astype(f32)).reshape(2, text_len, width)
         both_second = second_blocks(both_term, both_first, *grad_after_self)
         qkv_low = []
         for r in rows:
-            gates = (*down_far, text_term, *out_first) if r else both_second
-            grad_mixed = dot(after(low_self[r], *gates), full_out, across).astype(bf16)
+            ready = after(low_self[r], *((text_total,) if r else both_second))
+            grad_mixed = dot(ready, full_out, across).astype(bf16)
             qkv_low.append(
                 attend_back(qkv[r], qkv[r], 0, heads, grad_mixed, q_ids[r], i_ids[r], heads)[0]
             )
         qkv_term = [("row", streams(hid_one), streams(qkv_low))]
-        qkv_first = first_blocks(qkv_term)
-        up_far = across_high(up_second, *qkv_first)
-        kv_second = second_blocks(kv_term, kv_first, *qkv_first)
-        out_second = second_blocks(out_term, out_first, *kv_second)
-        qkv_second = second_blocks(qkv_term, qkv_first, *out_second)
-        both_far = across_high(both_second, *kv_second)
-        kv_far = across_high(kv_second, *qkv_second)
-        out_far = across_high(out_second, *qkv_second)
-        grad_tokens = []
-        for r in rows:
-            grad_in = scatter_tokens(after(qkv_low[r], *qkv_first), full_qkv, across)
-            piece = grad_after_self[r] + back_norm(0, r, grad_in)
-            grad_tokens.append(piece)
-        text_term = lax.psum_scatter(
-            text_term.reshape(2, text_len, text_dim), "mp", scatter_dimension=2, tiled=True
-        )
-        grad_text = pick(text_term, low).astype(f32) + swap_low(
-            pick(text_term, 1 - low)
-        ).astype(f32)
-
-        sum_down = collected(down_term, down_second, down_far, 0)
-        sum_up = collected(up_term, up_second, up_far, 1)
+        qkv_first = all_blocks(qkv_term)
+        last_low = [after(low_self[0], *qkv_first), low_self[1]]
+        out_term = [("col", streams(mixed), streams(last_low))]
+        out_first = first_blocks(out_term)
+        grad_in = []
+        for r in rows:
+            gates = out_first if r else qkv_first
+            grad_in.append(scatter_tokens(after(qkv_low[r], *gates), full_qkv, across))
+        out_second = second_blocks(out_term, out_first, grad_in[0])
+        sum_down = scattered(down_term, down, 0, *grad_in)
+        sum_up = scattered(up_term, up, 1, *grad_in)
+        sum_kv = scattered(kv_term, kv_first, 1, *grad_in)
+        grad_tokens = [grad_after_self[r] + back_norm(0, r, grad_in[r]) for r in rows]
+        both_far = across_high(both_second, *grad_in)
+        out_far = across_high(out_second, *grad_tokens)
+        text_total = after(text_total, *grad_in)
+        arrived = swap_low(pick(text_total, 1 - low).astype(bf16))
+        grad_text = pick(text_total, low) + arrived.astype(f32)
+
         if packed:
             sum_both = collected(both_term, both_second, both_far, 0)
             sum_cq = jnp.moveaxis(sum_both[:, :, :mine], 0, 1)
             sum_cout = sum_both[:, :, mine:]
         else:
             sum_cq, sum_cout = collected([cq_term], (), (), 1), collected([cout_term], (), (), 0)
-        sum_kv = collected(kv_term, kv_second, kv_far, 1)
         sum_out = collected(out_term, out_second, out_far, 0)
-        sum_qkv = collected(qkv_term, qkv_second, across_high(qkv_second), 1)
+        sum_qkv = scattered(qkv_term, qkv_first, 1)
 
         small = jnp.stack(gains + shifts + biases)
         small = small + lax.ppermute(small, "mp", core_swap)
@@ -646,7 +670,7 @@
 
         output = whole_row(outs)
         grad_tokens = [piece.astype(bf16) for piece in grad_tokens]
-        grad_tokens = whole_row([after(piece, *qkv_second) for piece in grad_tokens]).astype(f32)
+        grad_tokens = whole_row([piece for piece in grad_tokens]).astype(f32)
         gain_total, shift_total, bias_total = parts[:4], parts[4:8], parts[8:]
 
         apart = lambda v, n: v.reshape(v.shape[0], 2, n, -1).transpose(2, 0, 1, 3)

time: 1010 us -> 1020 us (level)
  waiting for transfers between devices: 397 us -> 464 us
  starting transfers between devices: 126 us -> 104 us
  local copies, waits for them, and re-layouts: 100 us -> 83 us
  Pallas kernels: 154 us -> 140 us
    ppermute x12, waiting for transfers between devices: 75.6 us -> 123 us  [scatter_tokens(): arrived = lax.ppermute(four[2 * part:].astype(bf16), BOTH, second_hop)]
    ppermute x18, waiting for transfers between devices: 88.4 us -> 71.7 us  [swap_low(): return lax.ppermute(values, 'dp', flip[2])]
    ppermute x12, waiting for transfers between devices: 31 us -> 47.7 us  [gather_tokens(): near = lax.ppermute(own, BOTH, first_hop)]
    ppermute x12, starting transfers between devices: 19.2 us -> 5.11 us  [gather_tokens(): return jnp.concatenate([four, lax.ppermute(four, 'mp', core_swap)], axis=0)]
    pallas_call x12 -> x8, Pallas kernels: 82.6 us -> 68.8 us  [grad_blocks(): pl.pallas_call(functools.partial(grad_kernel, kinds, added is not None, s...]
    ppermute x6 -> x2, waiting for transfers between devices: 11.9 us -> 0.01 us  [second_blocks(): arrived = after(lax.ppermute(away[0], 'dp', flip[1]), *gates)]
    ppermute x6 -> x2, waiting for transfers between devices: 13.4 us -> 22 us  [across_high(): return (after(lax.ppermute(second[0], 'dp', flip[4]), *gates),)]
    dot_general x38 -> x41, matrix products: 98.6 us -> 105 us  [dot(): lax.dot_general(left, right, (contract, ((), ())), preferred_element_type...]
  transfers between devices with their start and end apart: 125 -> 123, of which waited for: 55 -> 65; matrix products, arithmetic and copies ran while one was open for 27% -> 25% of each run, Pallas kernels for 15% -> 14%
where the time goes in v3:
time: 1020 us
  waiting for transfers between devices  464 us (45%)
  Pallas kernels  140 us (14%)
  matrix products  105 us (10%)
  starting transfers between devices  104 us (10%)
  other arithmetic  103 us (10%)
  local copies, waits for them, and re-layouts  83 us (8%)
  between operations  17.1 us (2%)
    ppermute x12, waiting for transfers between devices, scatter_tokens(): arrived = lax.ppermute(four[2 * part:].astype(bf16), BOTH, second_hop)  123 us
    dot_general x41, matrix products, dot(): lax.dot_general(left, right, (contract, ((), ())), preferred_element_type...  105 us
    ppermute x18, waiting for transfers between devices, swap_low(): return lax.ppermute(values, 'dp', flip[2])  71.7 us
    ppermute x5, waiting for transfers between devices, spread(): lax.ppermute(far, 'dp', flip[1])  71.3 us
    pallas_call x8, Pallas kernels, grad_blocks(): pl.pallas_call(functools.partial(grad_kernel, kinds, added is not None, s...  68.8 us
    ppermute x12, waiting for transfers between devices, gather_tokens(): four = jnp.concatenate([two, lax.ppermute(two, BOTH, second_hop)], axis=0)  62.3 us
    ppermute x12, waiting for transfers between devices, gather_tokens(): near = lax.ppermute(own, BOTH, first_hop)  47.7 us
    pallas_call x5, Pallas kernels, assembled(): pl.pallas_call(functools.partial(assemble_kernel, kinds), grid_spec=pltpu...  39.7 us
  transfers between devices with their start and end apart: 123, of which 65 were waited for; matrix products, arithmetic and copies ran while one was open for 25% of the time, Pallas kernels for 14%

profile of v3, /device:TPU:0, one launch (start us, length us, event | category | flops | bytes accessed | tf_op | source)
XLA Modules:
  0.0 1015.6 jit_solution(5177086618697236180)
XLA Ops:
  34.4 14.9 %collective-permute-done.5 = bf16[3,256,256]{2,1,0:T(8,128)(2,1)} collective-permute-done((bf16[3,256,256]{2,1,0:T(8,128)(2,1)}, bf16[3,256,256]{2,1,0:T(8,128)(2,1)}, u32[]{:S(2)}, u32[]{:S(2)}) %collective-permute-start.5) | collective-permute-done | bytes 393248 | tf_op jit(solution)/shard_map/ppermute | solution.py:320
  53.8 16.4 %collective-permute-done.1 = bf16[2,64,2048]{2,1,0:T(8,128)(2,1)S(1)} collective-permute-done((bf16[2,64,2048]{2,1,0:T(8,128)(2,1)S(1)}, bf16[2,64,2048]{2,1,0:T(8,128)(2,1)S(1)}, u32[]{:S(2)}, u32[]{:S(2)}) %collective-permute-start.1) | collective-permute-done | bytes 524320 | tf_op jit(solution)/shard_map/ppermute | solution.py:320
  71.6 9.1 collective-permute-done.6
  99.7 9.2 collective-permute-done.11
  111.5 6.6 collective-permute-done.3
  140.8 16.8 %collective-permute-done.8.refs_3_ = bf16[2,3,256,256]{3,2,1,0:T(8,128)(2,1)} collective-permute-done((bf16[2,3,256,256]{3,2,1,0:T(8,128)(2,1)}, bf16[2,3,256,256]{3,2,1,0:T(8,128)(2,1)}, u32[]{:S(2)}, u32[]{:S(2)}) %collective-permute-start.8) | collective-permute-done | bytes 786464 | tf_op jit(solution)/shard_map/ppermute | solution.py:342
  157.7 7.4 shard_map.362
  174.5 16.4 %collective-permute-done.16.refs_3_ = bf16[2,3,256,256]{3,2,1,0:T(8,128)(2,1)} collective-permute-done((bf16[2,3,256,256]{3,2,1,0:T(8,128)(2,1)}, bf16[2,3,256,256]{3,2,1,0:T(8,128)(2,1)}, u32[]{:S(2)}, u32[]{:S(2)}) %collective-permute-start.16) | collective-permute-done | bytes 786464 | tf_op jit(solution)/shard_map/ppermute | solution.py:342
  190.9 7.5 shard_map.364
  217.3 6.6 collective-permute-done.40
  226.3 5.9 collective-permute-done.18
  252.6 8.4 collective-permute-done.25.refs_2_
  261.0 22.5 %collective-permute-done.26.refs_3_ = bf16[2,2,512,256]{3,2,1,0:T(8,128)(2,1)} collective-permute-done((bf16[2,2,512,256]{3,2,1,0:T(8,128)(2,1)}, bf16[2,2,512,256]{3,2,1,0:T(8,128)(2,1)}, u32[]{:S(2)}, u32[]{:S(2)}) %collective-permute-start.26) | collective-permute-done | bytes 1048608 | tf_op jit(solution)/shard_map/ppermute | solution.py:342
  283.4 8.1 shard_map.365
  342.2 17.7 %collective-permute-done.46 = bf16[128,2048]{1,0:T(8,128)(2,1)S(1)} collective-permute-done((bf16[128,2048]{1,0:T(8,128)(2,1)S(1)}, bf16[128,2048]{1,0:T(8,128)(2,1)S(1)}, u32[]{:S(2)}, u32[]{:S(2)}) %collective-permute-start.46) | collective-permute-done | bytes 524320 | tf_op jit(solution)/shard_map/ppermute | solution.py:275
  363.9 23.5 %all-gather.28.cloned.1.call-done = bf16[4,1024,256]{2,1,0:T(8,128)(2,1)} async-done(((bf16[2,1024,256]{2,1,0:T(8,128)(2,1)}), bf16[4,1024,256]{2,1,0:T(8,128)(2,1)}) %all-gather.28.cloned.1.call-update) | async-done | bytes 2097168 | tf_op jit(solution)/shard_map/all_gather | solution.py:336
  393.6 7.1 collective-permute-done.30.refs_3_
  402.3 8.1 shard_map.367
  410.4 8.6 collective-permute-done.35.refs_3_
  419.0 8.6 shard_map.368
  429.7 7.2 collective-permute-done.48
  438.7 7.4 collective-permute-done.49
  464.5 5.7 collective-permute-done.37
  472.1 6.6 collective-permute-done.52
  491.1 7.1 collective-permute-done.54
  501.5 6.9 collective-permute-done.55
  508.9 9.2 collective-permute-done.67
  518.4 9.0 collective-permute-done.68
  534.3 11.6 %shard_map.372 = bf16[8,1024,256]{2,1,0:T(8,128)(2,1)} custom-call(s32[8]{0:T(128)} %fusion.109.order, bf16[512,1024]{1,0:T(8,128)(2,1)} %copy-done.100, bf16[512,1024]{1,0:T(8,128)(2,1)} %copy-done.99, bf16[512,2048]{1,0:T(8,128)(2,1)} %pad_maximum_fusion.4.refs_2_, bf16[512,2048]{1,0:T(8,128)(2,1)} %pad_maximum_fusion.6.refs_3_), custom_call_target="tpu_custom_call" | custom-call | tf_op jit(solution)/shard_map/pallas_call | solution.py:226
  546.0 8.1 convert_reduce_fusion.1
  569.0 11.1 %shard_map.373 = bf16[8,256,1024]{2,1,0:T(8,128)(2,1)} custom-call(s32[8]{0:T(128)} %fusion.109.order, bf16[512,2048]{1,0:T(8,128)(2,1)} %copy-done.63, bf16[512,2048]{1,0:T(8,128)(2,1)} %copy-done.64, bf16[512,1024]{1,0:T(8,128)(2,1)} %copy-done.102, bf16[512,1024]{1,0:T(8,128)(2,1)} %copy-done.101), custom_call_target="tpu_custom_call" | custom-call | tf_op jit(solution)/shard_map/pallas_call | solution.py:226
  588.6 20.7 %collective-permute-done.71 = bf16[128,2048]{1,0:T(8,128)(2,1)S(1)} collective-permute-done((bf16[128,2048]{1,0:T(8,128)(2,1)S(1)}, bf16[128,2048]{1,0:T(8,128)(2,1)S(1)}, u32[]{:S(2)}, u32[]{:S(2)}) %collective-permute-start.71) | collective-permute-done | bytes 524320 | tf_op jit(solution)/shard_map/ppermute | solution.py:275
  635.0 6.6 collective-permute-done.62
  671.3 8.0 shard_map.375
  680.9 9.3 shard_map.378
  704.4 12.3 %collective-permute-done.65 = bf16[128,2048]{1,0:T(8,128)(2,1)S(1)} collective-permute-done((bf16[128,2048]{1,0:T(8,128)(2,1)S(1)}, bf16[128,2048]{1,0:T(8,128)(2,1)S(1)}, u32[]{:S(2)}, u32[]{:S(2)}) %collective-permute-start.65) | collective-permute-done | bytes 524320 | tf_op jit(solution)/shard_map/ppermute | solution.py:275
  718.6 11.3 %collective-permute-done.81 = bf16[128,2048]{1,0:T(8,128)(2,1)S(1)} collective-permute-done((bf16[128,2048]{1,0:T(8,128)(2,1)S(1)}, bf16[128,2048]{1,0:T(8,128)(2,1)S(1)}, u32[]{:S(2)}, u32[]{:S(2)}) %collective-permute-start.81) | collective-permute-done | bytes 524320 | tf_op jit(solution)/shard_map/ppermute | solution.py:275
  744.9 8.0 shard_map.376
  766.3 5.6 collective-permute-done.77
  774.2 11.6 %collective-permute-done.84 = bf16[128,2048]{1,0:T(8,128)(2,1)S(1)} collective-permute-done((bf16[128,2048]{1,0:T(8,128)(2,1)S(1)}, bf16[128,2048]{1,0:T(8,128)(2,1)S(1)}, u32[]{:S(2)}, u32[]{:S(2)}) %collective-permute-start.84) | collective-permute-done | bytes 524320 | tf_op jit(solution)/shard_map/ppermute | solution.py:265
  807.4 10.0 shard_map.380
  839.7 15.7 %collective-permute-done.90 = bf16[128,2048]{1,0:T(8,128)(2,1)S(1)} collective-permute-done((bf16[128,2048]{1,0:T(8,128)(2,1)S(1)}, bf16[128,2048]{1,0:T(8,128)(2,1)S(1)}, u32[]{:S(2)}, u32[]{:S(2)}) %collective-permute-start.90) | collective-permute-done | bytes 524320 | tf_op jit(solution)/shard_map/ppermute | solution.py:275
  857.1 15.0 %collective-permute-done.93 = bf16[128,2048]{1,0:T(8,128)(2,1)S(1)} collective-permute-done((bf16[128,2048]{1,0:T(8,128)(2,1)S(1)}, bf16[128,2048]{1,0:T(8,128)(2,1)S(1)}, u32[]{:S(2)}, u32[]{:S(2)}) %collective-permute-start.93) | collective-permute-done | bytes 524320 | tf_op jit(solution)/shard_map/ppermute | solution.py:275
  898.0 5.5 shard_map.382
  914.1 19.8 %collective-permute-done.99 = bf16[2,256,256]{2,1,0:T(8,128)(2,1)} collective-permute-done((bf16[2,256,256]{2,1,0:T(8,128)(2,1)}, bf16[2,256,256]{2,1,0:T(8,128)(2,1)}, u32[]{:S(2)}, u32[]{:S(2)}) %collective-permute-start.99) | collective-permute-done | bytes 262176 | tf_op jit(solution)/shard_map/ppermute | solution.py:398
  935.9 6.7 collective-permute-done.95
  949.6 5.4 collective-permute-done.109
  997.7 5.7 collective-permute-done.97
  (839 shorter events, 502.1 us)
Async XLA Ops:
  7.2 114.5 %all-gather.20.cloned.1.call-start = ((), (), s32[]{:S(2)}) async-start(), calls=%async_computation.11 | async-start | bytes 2359296 | tf_op jit(solution)/shard_map/all_gather | solution.py:336
  13.5 82.4 %collective-permute-start.9 = (s32[768]{0:T(1024)}, s32[768]{0:T(1024)}, u32[]{:S(2)}, u32[]{:S(2)}) collective-permute-start(s32[768]{0:T(1024)} %pad_add_fusion), channel_id=1, source_target_pairs={{0,8},{4,12},{8,0},{12,4},{16,24},{20,28},{24,16},{28,20},{1,9},{5... | collective-permute-start | bytes 9224 | tf_op jit(solution)/shard_map/ppermute | solution.py:320
  13.5 83.1 %collective-permute-start.23 = (bf16[256,1024]{1,0:T(8,128)(2,1)}, bf16[256,1024]{1,0:T(8,128)(2,1)}, u32[]{:S(2)}, u32[]{:S(2)}) collective-permute-start(bf16[256,1024]{1,0:T(8,128)(2,1)} %param.28), channel_id=1, source_target_pairs={{0,8},{4,12},{8,0},{12,4},{16,24},{20,28},{24,16},{28,20},{1,9},{5... | collective-permute-start | bytes 1572872 | tf_op jit(solution)/shard_map/ppermute | solution.py:320
  24.5 104.4 %all-gather.24.cloned.1.call-start = ((), (), s32[]{:S(2)}) async-start(), calls=%async_computation.13 | async-start | bytes 2359296 | tf_op jit(solution)/shard_map/all_gather | solution.py:336
  34.3 36.0 %collective-permute-start.1 = (bf16[2,64,2048]{2,1,0:T(8,128)(2,1)S(1)}, bf16[2,64,2048]{2,1,0:T(8,128)(2,1)S(1)}, u32[]{:S(2)}, u32[]{:S(2)}) collective-permute-start(bf16[2,64,2048]{2,1,0:T(8,128)(2,1)S(1)} %get-tuple-element.209), channel_id=1, source_target_pairs={{0,8},{4,12},{8,0},{12,4},{16,24},{20,28},{24,16},{28,20},{1,9},{5... | collective-permute-start | bytes 1572872 | tf_op jit(solution)/shard_map/ppermute | solution.py:320
  51.2 158.3 %all-gather.22.cloned.1.call-start = ((), (), s32[]{:S(2)}) async-start(), calls=%async_computation.12 | async-start | bytes 3145728 | tf_op jit(solution)/shard_map/all_gather | solution.py:336
  51.3 29.4 %collective-permute-start.6 = (bf16[2,512,256]{2,1,0:T(8,128)(2,1)}, bf16[2,512,256]{2,1,0:T(8,128)(2,1)S(1)}, u32[]{:S(2)}, u32[]{:S(2)}) collective-permute-start(bf16[2,512,256]{2,1,0:T(8,128)(2,1)} %get-tuple-element.55), channel_id=1, source_target_pairs={{0,8},{4,12},{8,0},{12,4},{16,24},{20,28},{24,16},{28,20},{1,9},{5... | collective-permute-start | bytes 1572872 | tf_op jit(solution)/shard_map/ppermute | solution.py:320
  81.7 209.8 %all-gather.14.cloned.1.call-start = ((), (), s32[]{:S(2)}) async-start(), calls=%async_computation.4 | async-start | bytes 5242880 | tf_op jit(solution)/shard_map/all_gather | solution.py:484
  92.4 25.7 %collective-permute-start.3 = (bf16[128,2048]{1,0:T(8,128)(2,1)}, bf16[128,2048]{1,0:T(8,128)(2,1)S(1)}, u32[]{:S(2)}, u32[]{:S(2)}) collective-permute-start(bf16[128,2048]{1,0:T(8,128)(2,1)} %pad_maximum_fusion.24), channel_id=1, source_target_pairs={{0,8},{1,3},{2,10},{3,1},{4,12},{5,7},{6,14},{7,5},{8,0},{9,11},{1... | collective-permute-start | bytes 1572872 | tf_op jit(solution)/shard_map/ppermute | solution.py:265
  99.5 195.4 %all-gather.26.cloned.1.call-start = ((), (), s32[]{:S(2)}) async-start(), calls=%async_computation.14 | async-start | bytes 3145728 | tf_op jit(solution)/shard_map/all_gather | solution.py:336
  123.8 33.9 %collective-permute-start.8 = (bf16[2,3,256,256]{3,2,1,0:T(8,128)(2,1)}, bf16[2,3,256,256]{3,2,1,0:T(8,128)(2,1)}, u32[]{:S(2)}, u32[]{:S(2)}) collective-permute-start(bf16[2,3,256,256]{3,2,1,0:T(8,128)(2,1)} %dynamic-slice_bitcast_fusion.4.refs_1_), channel_id=1, source_target_pairs={{0,4},{4,0},{8,12},{12,8},{16,20},{20,16},{24,28},{28,24},{1,5},{5... | collective-permute-start | bytes 2359304 | tf_op jit(solution)/shard_map/ppermute | solution.py:342
  127.3 47.2 %collective-permute-start.15 = (bf16[2,3,256,256]{3,2,1,0:T(8,128)(2,1)}, bf16[2,3,256,256]{3,2,1,0:T(8,128)(2,1)}, u32[]{:S(2)}, u32[]{:S(2)}) collective-permute-start(bf16[2,3,256,256]{3,2,1,0:T(8,128)(2,1)} %pad_maximum_fusion.23.refs_0_), channel_id=1, source_target_pairs={{0,4},{4,0},{8,12},{12,8},{16,20},{20,16},{24,28},{28,24},{1,5},{5... | collective-permute-start | bytes 2359304 | tf_op jit(solution)/shard_map/ppermute | solution.py:341
  131.0 59.9 %collective-permute-start.16 = (bf16[2,3,256,256]{3,2,1,0:T(8,128)(2,1)}, bf16[2,3,256,256]{3,2,1,0:T(8,128)(2,1)}, u32[]{:S(2)}, u32[]{:S(2)}) collective-permute-start(bf16[2,3,256,256]{3,2,1,0:T(8,128)(2,1)} %dynamic-slice_bitcast_fusion.3.refs_1_), channel_id=1, source_target_pairs={{0,4},{4,0},{8,12},{12,8},{16,20},{20,16},{24,28},{28,24},{1,5},{5... | collective-permute-start | bytes 2359304 | tf_op jit(solution)/shard_map/ppermute | solution.py:342
  134.3 77.6 %collective-permute-start.14 = (bf16[1024,256]{1,0:T(8,128)(2,1)}, bf16[1024,256]{1,0:T(8,128)(2,1)}, u32[]{:S(2)}, u32[]{:S(2)}) collective-permute-start(bf16[1024,256]{1,0:T(8,128)(2,1)} %get-tuple-element.58), channel_id=1, source_target_pairs={{0,8},{4,12},{8,0},{12,4},{16,24},{20,28},{24,16},{28,20},{1,9},{5... | collective-permute-start | bytes 1572872 | tf_op jit(solution)/shard_map/ppermute | solution.py:320
  140.8 71.1 %collective-permute-start.13 = (bf16[256,1024]{1,0:T(8,128)(2,1)}, bf16[256,1024]{1,0:T(8,128)(2,1)}, u32[]{:S(2)}, u32[]{:S(2)}) collective-permute-start(bf16[256,1024]{1,0:T(8,128)(2,1)} %get-tuple-element.57), channel_id=1, source_target_pairs={{0,8},{4,12},{8,0},{12,4},{16,24},{20,28},{24,16},{28,20},{1,9},{5... | collective-permute-start | bytes 1572872 | tf_op jit(solution)/shard_map/ppermute | solution.py:320
  234.8 26.2 %collective-permute-start.25 = (bf16[2,2,512,256]{3,2,1,0:T(8,128)(2,1)S(1)}, bf16[2,2,512,256]{3,2,1,0:T(8,128)(2,1)}, u32[]{:S(2)}, u32[]{:S(2)}) collective-permute-start(bf16[2,2,512,256]{3,2,1,0:T(8,128)(2,1)S(1)} %copy-done.24), channel_id=1, source_target_pairs={{0,4},{4,0},{8,12},{12,8},{16,20},{20,16},{24,28},{28,24},{1,5},{5... | collective-permute-start | bytes 3145736 | tf_op jit(solution)/shard_map/ppermute | solution.py:341
  238.5 148.9 %all-gather.28.cloned.1.call-start = ((), (), s32[]{:S(2)}) async-start(), calls=%async_computation.15 | async-start | bytes 3145728 | tf_op jit(solution)/shard_map/all_gather | solution.py:336
  238.8 44.7 %collective-permute-start.26 = (bf16[2,2,512,256]{3,2,1,0:T(8,128)(2,1)}, bf16[2,2,512,256]{3,2,1,0:T(8,128)(2,1)}, u32[]{:S(2)}, u32[]{:S(2)}) collective-permute-start(bf16[2,2,512,256]{3,2,1,0:T(8,128)(2,1)} %dynamic-slice_bitcast_fusion.2.refs_1_), channel_id=1, source_target_pairs={{0,4},{4,0},{8,12},{12,8},{16,20},{20,16},{24,28},{28,24},{1,5},{5... | collective-permute-start | bytes 3145736 | tf_op jit(solution)/shard_map/ppermute | solution.py:342
  244.6 55.2 %collective-permute-start.24 = (bf16[2,256,1024]{2,1,0:T(8,128)(2,1)S(1)}, bf16[2,256,1024]{2,1,0:T(8,128)(2,1)}, u32[]{:S(2)}, u32[]{:S(2)}) collective-permute-start(bf16[2,256,1024]{2,1,0:T(8,128)(2,1)S(1)} %copy-done.25), channel_id=1, source_target_pairs={{0,4},{4,0},{8,12},{12,8},{16,20},{20,16},{24,28},{28,24},{1,5},{5... | collective-permute-start | bytes 3145736 | tf_op jit(solution)/shard_map/ppermute | solution.py:341
  252.0 45.3 %collective-permute-start.21 = (bf16[128,2048]{1,0:T(8,128)(2,1)}, bf16[128,2048]{1,0:T(8,128)(2,1)}, u32[]{:S(2)}, u32[]{:S(2)}) collective-permute-start(bf16[128,2048]{1,0:T(8,128)(2,1)} %pad_maximum_fusion.26), channel_id=1, source_target_pairs={{0,8},{1,3},{2,10},{3,1},{4,12},{5,7},{6,14},{7,5},{8,0},{9,11},{1... | collective-permute-start | bytes 1572872 | tf_op jit(solution)/shard_map/ppermute | solution.py:265
  329.3 546.1 %all-gather.16.cloned.1.call-start = ((), (), s32[]{:S(2)}) async-start(), calls=%async_computation.5 | async-start | bytes 2621440 | tf_op jit(solution)/shard_map/all_gather | solution.py:668
  334.0 25.9 %collective-permute-start.46 = (bf16[128,2048]{1,0:T(8,128)(2,1)S(1)}, bf16[128,2048]{1,0:T(8,128)(2,1)S(1)}, u32[]{:S(2)}, u32[]{:S(2)}) collective-permute-start(bf16[128,2048]{1,0:T(8,128)(2,1)S(1)} %slice.804), channel_id=1, source_target_pairs={{0,8},{1,3},{2,10},{3,1},{4,12},{5,7},{6,14},{7,5},{8,0},{9,11},{1... | collective-permute-start | bytes 1572872 | tf_op jit(solution)/shard_map/ppermute | solution.py:275
  340.5 50.7 %collective-permute-start.29 = (bf16[64,2048]{1,0:T(8,128)(2,1)S(1)}, bf16[64,2048]{1,0:T(8,128)(2,1)}, u32[]{:S(2)}, u32[]{:S(2)}) collective-permute-start(bf16[64,2048]{1,0:T(8,128)(2,1)S(1)} %slice.819), channel_id=1, source_target_pairs={{0,2},{1,9},{2,0},{3,11},{4,6},{5,13},{6,4},{7,15},{8,10},{9,1},{1... | collective-permute-start | bytes 786440 | tf_op jit(solution)/shard_map/ppermute | solution.py:277
  360.8 30.5 %collective-permute-start.47 = (bf16[64,2048]{1,0:T(8,128)(2,1)}, bf16[64,2048]{1,0:T(8,128)(2,1)}, u32[]{:S(2)}, u32[]{:S(2)}) collective-permute-start(bf16[64,2048]{1,0:T(8,128)(2,1)} %slice.816), channel_id=1, source_target_pairs={{0,2},{1,9},{2,0},{3,11},{4,6},{5,13},{6,4},{7,15},{8,10},{9,1},{1... | collective-permute-start | bytes 786440 | tf_op jit(solution)/shard_map/ppermute | solution.py:277
  361.9 48.5 %collective-permute-start.34 = (bf16[2,1024,256]{2,1,0:T(8,128)(2,1)}, bf16[2,1024,256]{2,1,0:T(8,128)(2,1)}, u32[]{:S(2)}, u32[]{:S(2)}) collective-permute-start(bf16[2,1024,256]{2,1,0:T(8,128)(2,1)} %pad_maximum_fusion.12.refs_0_), channel_id=1, source_target_pairs={{0,4},{4,0},{8,12},{12,8},{16,20},{20,16},{24,28},{28,24},{1,5},{5... | collective-permute-start | bytes 3145736 | tf_op jit(solution)/shard_map/ppermute | solution.py:341
  363.6 37.1 %collective-permute-start.30 = (bf16[2,256,1024]{2,1,0:T(8,128)(2,1)}, bf16[2,256,1024]{2,1,0:T(8,128)(2,1)}, u32[]{:S(2)}, u32[]{:S(2)}) collective-permute-start(bf16[2,256,1024]{2,1,0:T(8,128)(2,1)} %dynamic-slice_bitcast_fusion.1.refs_1_), channel_id=1, source_target_pairs={{0,4},{4,0},{8,12},{12,8},{16,20},{20,16},{24,28},{28,24},{1,5},{5... | collective-permute-start | bytes 3145736 | tf_op jit(solution)/shard_map/ppermute | solution.py:342
  389.8 29.2 %collective-permute-start.35 = (bf16[2,1024,256]{2,1,0:T(8,128)(2,1)}, bf16[2,1024,256]{2,1,0:T(8,128)(2,1)}, u32[]{:S(2)}, u32[]{:S(2)}) collective-permute-start(bf16[2,1024,256]{2,1,0:T(8,128)(2,1)} %dynamic-slice_bitcast_fusion.refs_1_), channel_id=1, source_target_pairs={{0,4},{4,0},{8,12},{12,8},{16,20},{20,16},{24,28},{28,24},{1,5},{5... | collective-permute-start | bytes 3145736 | tf_op jit(solution)/shard_map/ppermute | solution.py:342
  400.6 28.6 %collective-permute-start.31 = (bf16[64,2048]{1,0:T(8,128)(2,1)S(1)}, bf16[64,2048]{1,0:T(8,128)(2,1)S(1)}, u32[]{:S(2)}, u32[]{:S(2)}) collective-permute-start(bf16[64,2048]{1,0:T(8,128)(2,1)S(1)} %get-tuple-element.64), channel_id=1, source_target_pairs={{0,2},{1,9},{2,0},{3,11},{4,6},{5,13},{6,4},{7,15},{8,10},{9,1},{1... | collective-permute-start | bytes 786440 | tf_op jit(solution)/shard_map/ppermute | solution.py:263
  499.1 386.3 %reduce-scatter.11.cloned.1.call-start = ((), (), s32[]{:S(2)}) async-start(), calls=%async_computation.10 | async-start | bytes 5242880 | tf_op jit(solution)/shard_map/reduce_scatter | solution.py:375
  545.9 344.4 %reduce-scatter.9.cloned.1.call-start = ((), (), s32[]{:S(2)}) async-start(), calls=%async_computation.9 | async-start | bytes 5242880 | tf_op jit(solution)/shard_map/reduce_scatter | solution.py:375
  580.1 387.5 %reduce-scatter.7.cloned.1.call-start = ((), (), s32[]{:S(2)}) async-start(), calls=%async_computation.8 | async-start | bytes 5242880 | tf_op jit(solution)/shard_map/reduce_scatter | solution.py:375
  587.0 25.1 %collective-permute-start.60 = (bf16[64,2048]{1,0:T(8,128)(2,1)S(1)}, bf16[64,2048]{1,0:T(8,128)(2,1)S(1)}, u32[]{:S(2)}, u32[]{:S(2)}) collective-permute-start(bf16[64,2048]{1,0:T(8,128)(2,1)S(1)} %slice.814), channel_id=1, source_target_pairs={{0,2},{1,9},{2,0},{3,11},{4,6},{5,13},{6,4},{7,15},{8,10},{9,1},{1... | collective-permute-start | bytes 786440 | tf_op jit(solution)/shard_map/ppermute | solution.py:277
  660.3 36.7 %collective-permute-start.64 = (bf16[256,2048]{1,0:T(8,128)(2,1)}, bf16[256,2048]{1,0:T(8,128)(2,1)}, u32[]{:S(2)}, u32[]{:S(2)}) collective-permute-start(bf16[256,2048]{1,0:T(8,128)(2,1)} %convolution_convert_fusion.2), channel_id=1, source_target_pairs={{0,1},{1,0},{2,3},{3,2},{4,5},{5,4},{6,7},{7,6},{8,9},{9,8},{10,11... | collective-permute-start | bytes 3145736 | tf_op jit(solution)/shard_map/ppermute | solution.py:271
  671.1 28.7 %collective-permute-start.80 = (bf16[256,2048]{1,0:T(8,128)(2,1)}, bf16[256,2048]{1,0:T(8,128)(2,1)}, u32[]{:S(2)}, u32[]{:S(2)}) collective-permute-start(bf16[256,2048]{1,0:T(8,128)(2,1)} %convolution_convert_fusion), channel_id=1, source_target_pairs={{0,1},{1,0},{2,3},{3,2},{4,5},{5,4},{6,7},{7,6},{8,9},{9,8},{10,11... | collective-permute-start | bytes 3145736 | tf_op jit(solution)/shard_map/ppermute | solution.py:271
  679.3 65.6 %collective-permute-start.79 = (bf16[4,256,512]{2,1,0:T(8,128)(2,1)}, bf16[4,256,512]{2,1,0:T(8,128)(2,1)}, u32[]{:S(2)}, u32[]{:S(2)}) collective-permute-start(bf16[4,256,512]{2,1,0:T(8,128)(2,1)} %shard_map.375), channel_id=1, source_target_pairs={{0,4},{4,0},{8,12},{12,8},{16,20},{20,16},{24,28},{28,24},{1,5},{5... | collective-permute-start | bytes 3145736 | tf_op jit(solution)/shard_map/ppermute | solution.py:392
  693.5 69.5 %collective-permute-start.86 = (bf16[512,1024]{1,0:T(8,128)(2,1)}, bf16[512,1024]{1,0:T(8,128)(2,1)}, u32[]{:S(2)}, u32[]{:S(2)}) collective-permute-start(bf16[512,1024]{1,0:T(8,128)(2,1)} %convolution_convert_fusion.13), channel_id=1, source_target_pairs={{0,1},{1,0},{2,3},{3,2},{4,5},{5,4},{6,7},{7,6},{8,9},{9,8},{10,11... | collective-permute-start | bytes 3145736 | tf_op jit(solution)/shard_map/ppermute | solution.py:610
  696.4 34.8 %collective-permute-start.87 = (bf16[512,1024]{1,0:T(8,128)(2,1)}, bf16[512,1024]{1,0:T(8,128)(2,1)}, u32[]{:S(2)}, u32[]{:S(2)}) collective-permute-start(bf16[512,1024]{1,0:T(8,128)(2,1)} %convolution_convert_fusion.12), channel_id=1, source_target_pairs={{0,1},{1,0},{2,3},{3,2},{4,5},{5,4},{6,7},{7,6},{8,9},{9,8},{10,11... | collective-permute-start | bytes 3145736 | tf_op jit(solution)/shard_map/ppermute | solution.py:610
  697.0 294.8 %reduce-scatter.5.cloned.1.call-start = ((), (), s32[]{:S(2)}) async-start(), calls=%async_computation.7 | async-start | bytes 3932160 | tf_op jit(solution)/shard_map/reduce_scatter | solution.py:375
  701.7 28.1 %collective-permute-start.81 = (bf16[128,2048]{1,0:T(8,128)(2,1)S(1)}, bf16[128,2048]{1,0:T(8,128)(2,1)S(1)}, u32[]{:S(2)}, u32[]{:S(2)}) collective-permute-start(bf16[128,2048]{1,0:T(8,128)(2,1)S(1)} %slice.799), channel_id=1, source_target_pairs={{0,8},{1,3},{2,10},{3,1},{4,12},{5,7},{6,14},{7,5},{8,0},{9,11},{1... | collective-permute-start | bytes 1572872 | tf_op jit(solution)/shard_map/ppermute | solution.py:275
  734.4 28.6 %collective-permute-start.88 = (bf16[512,1024]{1,0:T(8,128)(2,1)}, bf16[512,1024]{1,0:T(8,128)(2,1)}, u32[]{:S(2)}, u32[]{:S(2)}) collective-permute-start(bf16[512,1024]{1,0:T(8,128)(2,1)} %add_convert_fusion), channel_id=1, source_target_pairs={{0,2},{1,3},{2,0},{3,1},{4,6},{5,7},{6,4},{7,5},{8,10},{9,11},{10,... | collective-permute-start | bytes 3145736 | tf_op jit(solution)/shard_map/ppermute | solution.py:612
  831.2 162.1 %all-gather.18.cloned.1.call-start = ((), (), s32[]{:S(2)}) async-start(), calls=%async_computation.6 | async-start | bytes 2621440 | tf_op jit(solution)/shard_map/all_gather | solution.py:668
  837.6 34.5 %collective-permute-start.93 = (bf16[128,2048]{1,0:T(8,128)(2,1)S(1)}, bf16[128,2048]{1,0:T(8,128)(2,1)S(1)}, u32[]{:S(2)}, u32[]{:S(2)}) collective-permute-start(bf16[128,2048]{1,0:T(8,128)(2,1)S(1)} %slice.797), channel_id=1, source_target_pairs={{0,8},{1,3},{2,10},{3,1},{4,12},{5,7},{6,14},{7,5},{8,0},{9,11},{1... | collective-permute-start | bytes 1572872 | tf_op jit(solution)/shard_map/ppermute | solution.py:275
  887.9 75.4 %collective-permute-start.105 = (bf16[1024,256]{1,0:T(8,128)(2,1)}, bf16[1024,256]{1,0:T(8,128)(2,1)}, u32[]{:S(2)}, u32[]{:S(2)}) collective-permute-start(bf16[1024,256]{1,0:T(8,128)(2,1)} %get-tuple-element.219), channel_id=1, source_target_pairs={{0,8},{4,12},{8,0},{12,4},{16,24},{20,28},{24,16},{28,20},{1,9},{5... | collective-permute-start | bytes 1572872 | tf_op jit(solution)/shard_map/ppermute | solution.py:320
  892.8 72.6 %collective-permute-start.104 = (bf16[256,1024]{1,0:T(8,128)(2,1)}, bf16[256,1024]{1,0:T(8,128)(2,1)}, u32[]{:S(2)}, u32[]{:S(2)}) collective-permute-start(bf16[256,1024]{1,0:T(8,128)(2,1)} %get-tuple-element.221), channel_id=1, source_target_pairs={{0,8},{4,12},{8,0},{12,4},{16,24},{20,28},{24,16},{28,20},{1,9},{5... | collective-permute-start | bytes 1572872 | tf_op jit(solution)/shard_map/ppermute | solution.py:320
  898.0 47.0 %collective-permute-start.102 = (bf16[256,512]{1,0:T(8,128)(2,1)}, bf16[256,512]{1,0:T(8,128)(2,1)S(1)}, u32[]{:S(2)}, u32[]{:S(2)}) collective-permute-start(bf16[256,512]{1,0:T(8,128)(2,1)} %fusion.82), channel_id=1, source_target_pairs={{0,8},{4,12},{8,0},{12,4},{16,24},{20,28},{24,16},{28,20},{1,9},{5... | collective-permute-start | bytes 786440 | tf_op jit(solution)/shard_map/ppermute | solution.py:320
  903.5 30.3 %collective-permute-start.99 = (bf16[2,256,256]{2,1,0:T(8,128)(2,1)}, bf16[2,256,256]{2,1,0:T(8,128)(2,1)}, u32[]{:S(2)}, u32[]{:S(2)}) collective-permute-start(bf16[2,256,256]{2,1,0:T(8,128)(2,1)} %get-tuple-element.86), channel_id=1, source_target_pairs={{0,16},{4,20},{8,24},{12,28},{16,0},{20,4},{24,8},{28,12},{1,17},{... | collective-permute-start | bytes 786440 | tf_op jit(solution)/shard_map/ppermute | solution.py:398
  913.8 28.9 %collective-permute-start.95 = (bf16[64,2048]{1,0:T(8,128)(2,1)S(1)}, bf16[64,2048]{1,0:T(8,128)(2,1)S(1)}, u32[]{:S(2)}, u32[]{:S(2)}) collective-permute-start(bf16[64,2048]{1,0:T(8,128)(2,1)S(1)} %get-tuple-element.243), channel_id=1, source_target_pairs={{0,8},{4,12},{8,0},{12,4},{16,24},{20,28},{24,16},{28,20},{1,9},{5... | collective-permute-start | bytes 786440 | tf_op jit(solution)/shard_map/ppermute | solution.py:320
  933.9 43.0 %collective-permute-start.96 = (bf16[256,1024]{1,0:T(8,128)(2,1)}, bf16[256,1024]{1,0:T(8,128)(2,1)}, u32[]{:S(2)}, u32[]{:S(2)}) collective-permute-start(bf16[256,1024]{1,0:T(8,128)(2,1)} %fusion.59), channel_id=1, source_target_pairs={{0,8},{4,12},{8,0},{12,4},{16,24},{20,28},{24,16},{28,20},{1,9},{5... | collective-permute-start | bytes 1572872 | tf_op jit(solution)/shard_map/ppermute | solution.py:320
  (222 other events, 2396.3 us)
Sparse Core Ops, SparseCore 0:
  24.6 45.7 all-gather.19
  72.5 45.0 all-gather.23
  119.7 55.4 all-gather.21
  177.3 33.4 all-gather.13
  238.6 56.2 all-gather.25
  329.4 57.9 all-gather.27
  499.2 31.4 all-gather.15
  546.1 88.6 reduce-scatter.10
  637.7 86.1 reduce-scatter.8
  726.7 86.1 reduce-scatter.6
  831.3 90.8 reduce-scatter.4
  945.1 20.6 all-gather.17

commit v4 on v2

--- a/solution.py
+++ b/solution.py
@@ -3,6 +3,7 @@
 import jax
 import jax.numpy as jnp
 from jax import lax
+from jax.experimental.layout import Layout, with_layout_constraint
 from jax.experimental import pallas as pl
 from jax.experimental.pallas import tpu as pltpu
 from jax.sharding import PartitionSpec as P
@@ -254,6 +255,9 @@
     first_hop = [(i * n_mp + m, side(i, m) if m % 2 == 0 else lower(i, m)) for i, m in pairs]
     second_hop = [(i * n_mp + m, lower(i, m) if m % 2 == 0 else side(i, m)) for i, m in pairs]
     high_groups = [[h * 4 + low for h in range(n_hi)] for low in range(4)]
+    data_groups = [
+        [h * 4 + low * 2 + y for h in range(n_hi) for y in range(2)] for low in range(2)
+    ]
 
     def gather_tokens(own):
         near = lax.ppermute(own, BOTH, first_hop)
@@ -358,6 +362,25 @@
 
             return assembled(xor_order([0, 2, 4, 6, 1, 3, 5, 7]), pieces, kinds, shapes, n_dp)
 
+        def all_blocks(terms):
+            if n_hi != 2:
+                return ()
+            j = jnp.arange(8, dtype=jnp.int32)
+            order = (j // 4 * 4 + (low ^ (j % 2)) * 2 + j // 2 % 2).astype(jnp.int32)
+            return (grad_blocks(order, terms, n_dp, [8])[0],)
+
+        def scattered(terms, blocks, axis):
+            if n_hi != 2:
+                return collected(terms, (), (), axis)
+            total = lax.psum_scatter(
+                blocks[0].reshape((4, 2) + blocks[0].shape[1:]),
+                "dp",
+                scatter_dimension=0,
+                axis_index_groups=data_groups,
+            )
+            total = with_layout_constraint(total, Layout((0, 1, 2)))
+            return ordered(total[0].astype(f32), swap_low(total[1]).astype(f32), axis)
+
         def first_blocks(terms):
             if n_hi != 2:
                 return ()
@@ -592,14 +615,13 @@
                 attend_back(qkv[r], qkv[r], 0, heads, grad_mixed, q_ids[r], i_ids[r], heads)[0]
             )
         qkv_term = [("row", streams(hid_one), streams(qkv_low))]
-        qkv_first = first_blocks(qkv_term)
+        qkv_first = all_blocks(qkv_term)
         up_far = across_high(up_second, *qkv_first)
         kv_second = second_blocks(kv_term, kv_first, *qkv_first)
         out_second = second_blocks(out_term, out_first, *kv_second)
-        qkv_second = second_blocks(qkv_term, qkv_first, *out_second)
         both_far = across_high(both_second, *kv_second)
-        kv_far = across_high(kv_second, *qkv_second)
-        out_far = across_high(out_second, *qkv_second)
+        kv_far = across_high(kv_second, *out_second)
+        out_far = across_high(out_second)
         grad_tokens = []
         for r in rows:
             grad_in = scatter_tokens(after(qkv_low[r], *qkv_first), full_qkv, across)
@@ -622,7 +644,7 @@
             sum_cq, sum_cout = collected([cq_term], (), (), 1), collected([cout_term], (), (), 0)
         sum_kv = collected(kv_term, kv_second, kv_far, 1)
         sum_out = collected(out_term, out_second, out_far, 0)
-        sum_qkv = collected(qkv_term, qkv_second, across_high(qkv_second), 1)
+        sum_qkv = scattered(qkv_term, qkv_first, 1)
 
         small = jnp.stack(gains + shifts + biases)
         small = small + lax.ppermute(small, "mp", core_swap)
@@ -646,7 +668,7 @@
 
         output = whole_row(outs)
         grad_tokens = [piece.astype(bf16) for piece in grad_tokens]
-        grad_tokens = whole_row([after(piece, *qkv_second) for piece in grad_tokens]).astype(f32)
+        grad_tokens = whole_row([piece for piece in grad_tokens]).astype(f32)
         gain_total, shift_total, bias_total = parts[:4], parts[4:8], parts[8:]
 
         apart = lambda v, n: v.reshape(v.shape[0], 2, n, -1).transpose(2, 0, 1, 3)

time: 1010 us -> 1010 us (level)
  waiting for transfers between devices: 397 us -> 423 us
  other arithmetic: 111 us -> 93.4 us
    ppermute x12, waiting for transfers between devices: 75.6 us -> 102 us  [scatter_tokens(): arrived = lax.ppermute(four[2 * part:].astype(bf16), BOTH, second_hop)]
    ppermute x12, waiting for transfers between devices: 52.3 us -> 40 us  [gather_tokens(): four = jnp.concatenate([two, lax.ppermute(two, BOTH, second_hop)], axis=0)]
    ppermute x12, starting transfers between devices: 19.2 us -> 8.46 us  [gather_tokens(): return jnp.concatenate([four, lax.ppermute(four, 'mp', core_swap)], axis=0)]
    unnamed x365 -> x353, local copies, waits for them, and re-layouts: 33.9 us -> 38.4 us
    pallas_call x12 -> x11, Pallas kernels: 82.6 us -> 79.1 us  [grad_blocks(): pl.pallas_call(functools.partial(grad_kernel, kinds, added is not None, s...]
  transfers between devices with their start and end apart: 125 -> 124, of which waited for: 55 -> 58; matrix products, arithmetic and copies ran while one was open for 27% -> 25% of each run, Pallas kernels for 15% -> 15%
where the time goes in v4:
time: 1010 us; the launch traced here: 998 us
  waiting for transfers between devices  423 us (42%)
  Pallas kernels  151 us (15%)
  starting transfers between devices  117 us (12%)
  local copies, waits for them, and re-layouts  99.8 us (10%)
  matrix products  96.9 us (10%)
  other arithmetic  93.4 us (9%)
  between operations  17.5 us (2%)
    ppermute x12, waiting for transfers between devices, scatter_tokens(): arrived = lax.ppermute(four[2 * part:].astype(bf16), BOTH, second_hop)  102 us
    dot_general x38, matrix products, dot(): lax.dot_general(left, right, (contract, ((), ())), preferred_element_type...  96.9 us
    ppermute x18, waiting for transfers between devices, swap_low(): return lax.ppermute(values, 'dp', flip[2])  92.9 us
    pallas_call x11, Pallas kernels, grad_blocks(): pl.pallas_call(functools.partial(grad_kernel, kinds, added is not None, s...  79.1 us
    ppermute x5, waiting for transfers between devices, spread(): lax.ppermute(far, 'dp', flip[1])  70.9 us
    ppermute x12, waiting for transfers between devices, gather_tokens(): four = jnp.concatenate([two, lax.ppermute(two, BOTH, second_hop)], axis=0)  40 us
    pallas_call x5, Pallas kernels, assembled(): pl.pallas_call(functools.partial(assemble_kernel, kinds), grid_spec=pltpu...  39.6 us
    unnamed x353, local copies, waits for them, and re-layouts  38.4 us
  transfers between devices with their start and end apart: 124, of which 58 were waited for; matrix products, arithmetic and copies ran while one was open for 25% of the time, Pallas kernels for 15%

profile of v4, /device:TPU:0, one launch (start us, length us, event | category | flops | bytes accessed | tf_op | source)
XLA Modules:
  0.0 998.2 jit_solution(266696279778343120)
XLA Ops:
  34.7 14.4 %collective-permute-done.5 = bf16[3,256,256]{2,1,0:T(8,128)(2,1)} collective-permute-done((bf16[3,256,256]{2,1,0:T(8,128)(2,1)S(1)}, bf16[3,256,256]{2,1,0:T(8,128)(2,1)}, u32[]{:S(2)}, u32[]{:S(2)}) %collective-permute-start.5) | collective-permute-done | bytes 393248 | tf_op jit(solution)/shard_map/ppermute | solution.py:320
  53.8 16.4 %collective-permute-done.1 = bf16[2,64,2048]{2,1,0:T(8,128)(2,1)S(1)} collective-permute-done((bf16[2,64,2048]{2,1,0:T(8,128)(2,1)S(1)}, bf16[2,64,2048]{2,1,0:T(8,128)(2,1)S(1)}, u32[]{:S(2)}, u32[]{:S(2)}) %collective-permute-start.1) | collective-permute-done | bytes 524320 | tf_op jit(solution)/shard_map/ppermute | solution.py:320
  71.0 9.6 collective-permute-done.6
  99.7 9.2 collective-permute-done.11
  111.6 6.5 collective-permute-done.3
  140.8 16.8 %collective-permute-done.8.refs_3_ = bf16[2,3,256,256]{3,2,1,0:T(8,128)(2,1)} collective-permute-done((bf16[2,3,256,256]{3,2,1,0:T(8,128)(2,1)}, bf16[2,3,256,256]{3,2,1,0:T(8,128)(2,1)}, u32[]{:S(2)}, u32[]{:S(2)}) %collective-permute-start.8) | collective-permute-done | bytes 786464 | tf_op jit(solution)/shard_map/ppermute | solution.py:342
  157.6 7.5 shard_map.416
  174.5 16.4 %collective-permute-done.16.refs_3_ = bf16[2,3,256,256]{3,2,1,0:T(8,128)(2,1)} collective-permute-done((bf16[2,3,256,256]{3,2,1,0:T(8,128)(2,1)}, bf16[2,3,256,256]{3,2,1,0:T(8,128)(2,1)}, u32[]{:S(2)}, u32[]{:S(2)}) %collective-permute-start.16) | collective-permute-done | bytes 786464 | tf_op jit(solution)/shard_map/ppermute | solution.py:342
  190.9 7.5 shard_map.418
  217.3 6.6 collective-permute-done.40
  226.4 5.9 collective-permute-done.18
  252.6 8.4 collective-permute-done.25.refs_2_
  261.0 22.5 %collective-permute-done.26.refs_3_ = bf16[2,2,512,256]{3,2,1,0:T(8,128)(2,1)} collective-permute-done((bf16[2,2,512,256]{3,2,1,0:T(8,128)(2,1)}, bf16[2,2,512,256]{3,2,1,0:T(8,128)(2,1)}, u32[]{:S(2)}, u32[]{:S(2)}) %collective-permute-start.26) | collective-permute-done | bytes 1048608 | tf_op jit(solution)/shard_map/ppermute | solution.py:342
  283.5 8.1 shard_map.419
  342.2 17.6 %collective-permute-done.46 = bf16[128,2048]{1,0:T(8,128)(2,1)S(1)} collective-permute-done((bf16[128,2048]{1,0:T(8,128)(2,1)S(1)}, bf16[128,2048]{1,0:T(8,128)(2,1)S(1)}, u32[]{:S(2)}, u32[]{:S(2)}) %collective-permute-start.46) | collective-permute-done | bytes 524320 | tf_op jit(solution)/shard_map/ppermute | solution.py:275
  364.0 23.5 %all-gather.28.cloned.1.call-done = bf16[4,1024,256]{2,1,0:T(8,128)(2,1)} async-done(((bf16[2,1024,256]{2,1,0:T(8,128)(2,1)}), bf16[4,1024,256]{2,1,0:T(8,128)(2,1)}) %all-gather.28.cloned.1.call-update) | async-done | bytes 2097168 | tf_op jit(solution)/shard_map/all_gather | solution.py:336
  394.3 6.6 collective-permute-done.30.refs_3_
  402.5 8.1 shard_map.421
  410.6 8.6 collective-permute-done.35.refs_3_
  419.2 8.5 shard_map.422
  429.8 7.2 collective-permute-done.48
  438.9 7.4 collective-permute-done.49
  472.3 6.6 collective-permute-done.52
  490.6 7.0 collective-permute-done.55
  499.7 7.1 collective-permute-done.56
  508.0 8.4 collective-permute-done.65
  526.2 7.8 shard_map.425
  534.0 6.9 convert_reduce_fusion
  548.8 5.7 collective-permute-done.59
  577.7 6.9 shard_map.428
  590.8 5.8 collective-permute-done.74
  601.8 13.0 %collective-permute-done.67.refs_4_ = bf16[4,1024,256]{2,1,0:T(8,128)(2,1)} collective-permute-done((bf16[4,1024,256]{2,1,0:T(8,128)(2,1)}, bf16[4,1024,256]{2,1,0:T(8,128)(2,1)}, u32[]{:S(2)}, u32[]{:S(2)}) %collective-permute-start.67) | collective-permute-done | bytes 2097184 | tf_op jit(solution)/shard_map/ppermute | solution.py:392
  614.8 8.6 shard_map.426
  652.8 7.4 shard_map.430
  660.2 7.5 shard_map.434
  669.2 5.7 shard_map.433
  674.9 6.7 convolution_convert_fusion
  712.1 16.0 %collective-permute-done.108 = bf16[1024,256]{1,0:T(8,128)(2,1)S(1)} collective-permute-done((bf16[1024,256]{1,0:T(8,128)(2,1)S(1)}, bf16[1024,256]{1,0:T(8,128)(2,1)S(1)}, u32[]{:S(2)}, u32[]{:S(2)}) %collective-permute-start.108) | collective-permute-done | bytes 524320 | tf_op jit(solution)/shard_map/ppermute | solution.py:320
  731.3 8.1 collective-permute-done.77
  740.8 7.9 shard_map.431
  755.1 6.4 collective-permute-start.87
  790.3 10.1 %shard_map.437 = bf16[8,256,768]{2,1,0:T(8,128)(2,1)} custom-call(s32[8]{0:T(128)} %fusion.107.order, bf16[512,2048]{1,0:T(8,128)(2,1)} %copy-done.33, bf16[512,2048]{1,0:T(8,128)(2,1)} %pad_maximum_fusion.2.refs_1_, bf16[512,768]{1,0:T(8,128)(2,1)} %shard_map.432.refs_2_, bf16[512,768]{1,0:T(8,128)(2,1)} %shard_map.436.refs_3_), custom_call_target="tpu_custom_call" | custom-call | tf_op jit(solution)/shard_map/pallas_call | solution.py:226
  806.9 6.2 shard_map.438
  825.0 7.5 collective-permute-done.103
  856.7 31.0 %collective-permute-done.93 = bf16[128,2048]{1,0:T(8,128)(2,1)} collective-permute-done((bf16[128,2048]{1,0:T(8,128)(2,1)}, bf16[128,2048]{1,0:T(8,128)(2,1)}, u32[]{:S(2)}, u32[]{:S(2)}) %collective-permute-start.93) | collective-permute-done | bytes 524320 | tf_op jit(solution)/shard_map/ppermute | solution.py:275
  891.5 6.3 collective-permute-done.90
  907.7 8.3 collective-permute-done.100
  923.4 13.0 %collective-permute-done.95 = bf16[64,2048]{1,0:T(8,128)(2,1)S(1)} collective-permute-done((bf16[64,2048]{1,0:T(8,128)(2,1)S(1)}, bf16[64,2048]{1,0:T(8,128)(2,1)S(1)}, u32[]{:S(2)}, u32[]{:S(2)}) %collective-permute-start.95) | collective-permute-done | bytes 262176 | tf_op jit(solution)/shard_map/ppermute | solution.py:320
  (884 shorter events, 505.6 us)
Async XLA Ops:
  7.2 114.5 %all-gather.20.cloned.1.call-start = ((), (), s32[]{:S(2)}) async-start(), calls=%async_computation.7 | async-start | bytes 2359296 | tf_op jit(solution)/shard_map/all_gather | solution.py:336
  13.5 82.5 %collective-permute-start.9 = (s32[768]{0:T(1024)}, s32[768]{0:T(1024)}, u32[]{:S(2)}, u32[]{:S(2)}) collective-permute-start(s32[768]{0:T(1024)} %pad_add_fusion), channel_id=1, source_target_pairs={{0,8},{4,12},{8,0},{12,4},{16,24},{20,28},{24,16},{28,20},{1,9},{5... | collective-permute-start | bytes 9224 | tf_op jit(solution)/shard_map/ppermute | solution.py:320
  13.5 83.2 %collective-permute-start.23 = (bf16[256,1024]{1,0:T(8,128)(2,1)}, bf16[256,1024]{1,0:T(8,128)(2,1)}, u32[]{:S(2)}, u32[]{:S(2)}) collective-permute-start(bf16[256,1024]{1,0:T(8,128)(2,1)} %param.34), channel_id=1, source_target_pairs={{0,8},{4,12},{8,0},{12,4},{16,24},{20,28},{24,16},{28,20},{1,9},{5... | collective-permute-start | bytes 1572872 | tf_op jit(solution)/shard_map/ppermute | solution.py:320
  24.5 104.4 %all-gather.24.cloned.1.call-start = ((), (), s32[]{:S(2)}) async-start(), calls=%async_computation.9 | async-start | bytes 2359296 | tf_op jit(solution)/shard_map/all_gather | solution.py:336
  34.7 35.6 %collective-permute-start.1 = (bf16[2,64,2048]{2,1,0:T(8,128)(2,1)S(1)}, bf16[2,64,2048]{2,1,0:T(8,128)(2,1)S(1)}, u32[]{:S(2)}, u32[]{:S(2)}) collective-permute-start(bf16[2,64,2048]{2,1,0:T(8,128)(2,1)S(1)} %get-tuple-element.226), channel_id=1, source_target_pairs={{0,8},{4,12},{8,0},{12,4},{16,24},{20,28},{24,16},{28,20},{1,9},{5... | collective-permute-start | bytes 1572872 | tf_op jit(solution)/shard_map/ppermute | solution.py:320
  51.1 158.5 %all-gather.22.cloned.1.call-start = ((), (), s32[]{:S(2)}) async-start(), calls=%async_computation.8 | async-start | bytes 3145728 | tf_op jit(solution)/shard_map/all_gather | solution.py:336
  51.2 29.5 %collective-permute-start.6 = (bf16[2,512,256]{2,1,0:T(8,128)(2,1)S(1)}, bf16[2,512,256]{2,1,0:T(8,128)(2,1)S(1)}, u32[]{:S(2)}, u32[]{:S(2)}) collective-permute-start(bf16[2,512,256]{2,1,0:T(8,128)(2,1)S(1)} %get-tuple-element.62), channel_id=1, source_target_pairs={{0,8},{4,12},{8,0},{12,4},{16,24},{20,28},{24,16},{28,20},{1,9},{5... | collective-permute-start | bytes 1572872 | tf_op jit(solution)/shard_map/ppermute | solution.py:320
  81.7 209.9 %all-gather.14.cloned.1.call-start = ((), (), s32[]{:S(2)}) async-start(), calls=%async_computation.2 | async-start | bytes 5242880 | tf_op jit(solution)/shard_map/all_gather | solution.py:484
  99.5 195.4 %all-gather.26.cloned.1.call-start = ((), (), s32[]{:S(2)}) async-start(), calls=%async_computation.10 | async-start | bytes 3145728 | tf_op jit(solution)/shard_map/all_gather | solution.py:336
  123.8 33.9 %collective-permute-start.8 = (bf16[2,3,256,256]{3,2,1,0:T(8,128)(2,1)}, bf16[2,3,256,256]{3,2,1,0:T(8,128)(2,1)}, u32[]{:S(2)}, u32[]{:S(2)}) collective-permute-start(bf16[2,3,256,256]{3,2,1,0:T(8,128)(2,1)} %dynamic-slice_bitcast_fusion.4.refs_1_), channel_id=1, source_target_pairs={{0,4},{4,0},{8,12},{12,8},{16,20},{20,16},{24,28},{28,24},{1,5},{5... | collective-permute-start | bytes 2359304 | tf_op jit(solution)/shard_map/ppermute | solution.py:342
  127.3 47.2 %collective-permute-start.15 = (bf16[2,3,256,256]{3,2,1,0:T(8,128)(2,1)}, bf16[2,3,256,256]{3,2,1,0:T(8,128)(2,1)}, u32[]{:S(2)}, u32[]{:S(2)}) collective-permute-start(bf16[2,3,256,256]{3,2,1,0:T(8,128)(2,1)} %pad_maximum_fusion.23.refs_0_), channel_id=1, source_target_pairs={{0,4},{4,0},{8,12},{12,8},{16,20},{20,16},{24,28},{28,24},{1,5},{5... | collective-permute-start | bytes 2359304 | tf_op jit(solution)/shard_map/ppermute | solution.py:341
  131.0 59.9 %collective-permute-start.16 = (bf16[2,3,256,256]{3,2,1,0:T(8,128)(2,1)}, bf16[2,3,256,256]{3,2,1,0:T(8,128)(2,1)}, u32[]{:S(2)}, u32[]{:S(2)}) collective-permute-start(bf16[2,3,256,256]{3,2,1,0:T(8,128)(2,1)} %dynamic-slice_bitcast_fusion.3.refs_1_), channel_id=1, source_target_pairs={{0,4},{4,0},{8,12},{12,8},{16,20},{20,16},{24,28},{28,24},{1,5},{5... | collective-permute-start | bytes 2359304 | tf_op jit(solution)/shard_map/ppermute | solution.py:342
  134.3 77.6 %collective-permute-start.14 = (bf16[1024,256]{1,0:T(8,128)(2,1)}, bf16[1024,256]{1,0:T(8,128)(2,1)}, u32[]{:S(2)}, u32[]{:S(2)}) collective-permute-start(bf16[1024,256]{1,0:T(8,128)(2,1)} %get-tuple-element.65), channel_id=1, source_target_pairs={{0,8},{4,12},{8,0},{12,4},{16,24},{20,28},{24,16},{28,20},{1,9},{5... | collective-permute-start | bytes 1572872 | tf_op jit(solution)/shard_map/ppermute | solution.py:320
  140.8 71.1 %collective-permute-start.13 = (bf16[256,1024]{1,0:T(8,128)(2,1)}, bf16[256,1024]{1,0:T(8,128)(2,1)}, u32[]{:S(2)}, u32[]{:S(2)}) collective-permute-start(bf16[256,1024]{1,0:T(8,128)(2,1)} %get-tuple-element.64), channel_id=1, source_target_pairs={{0,8},{4,12},{8,0},{12,4},{16,24},{20,28},{24,16},{28,20},{1,9},{5... | collective-permute-start | bytes 1572872 | tf_op jit(solution)/shard_map/ppermute | solution.py:320
  234.8 26.2 %collective-permute-start.25 = (bf16[2,2,512,256]{3,2,1,0:T(8,128)(2,1)S(1)}, bf16[2,2,512,256]{3,2,1,0:T(8,128)(2,1)}, u32[]{:S(2)}, u32[]{:S(2)}) collective-permute-start(bf16[2,2,512,256]{3,2,1,0:T(8,128)(2,1)S(1)} %copy-done.31), channel_id=1, source_target_pairs={{0,4},{4,0},{8,12},{12,8},{16,20},{20,16},{24,28},{28,24},{1,5},{5... | collective-permute-start | bytes 3145736 | tf_op jit(solution)/shard_map/ppermute | solution.py:341
  238.5 149.0 %all-gather.28.cloned.1.call-start = ((), (), s32[]{:S(2)}) async-start(), calls=%async_computation.11 | async-start | bytes 3145728 | tf_op jit(solution)/shard_map/all_gather | solution.py:336
  238.8 44.7 %collective-permute-start.26 = (bf16[2,2,512,256]{3,2,1,0:T(8,128)(2,1)}, bf16[2,2,512,256]{3,2,1,0:T(8,128)(2,1)}, u32[]{:S(2)}, u32[]{:S(2)}) collective-permute-start(bf16[2,2,512,256]{3,2,1,0:T(8,128)(2,1)} %dynamic-slice_bitcast_fusion.2.refs_1_), channel_id=1, source_target_pairs={{0,4},{4,0},{8,12},{12,8},{16,20},{20,16},{24,28},{28,24},{1,5},{5... | collective-permute-start | bytes 3145736 | tf_op jit(solution)/shard_map/ppermute | solution.py:342
  244.7 55.2 %collective-permute-start.24 = (bf16[2,256,1024]{2,1,0:T(8,128)(2,1)S(1)}, bf16[2,256,1024]{2,1,0:T(8,128)(2,1)}, u32[]{:S(2)}, u32[]{:S(2)}) collective-permute-start(bf16[2,256,1024]{2,1,0:T(8,128)(2,1)S(1)} %copy-done.32), channel_id=1, source_target_pairs={{0,4},{4,0},{8,12},{12,8},{16,20},{20,16},{24,28},{28,24},{1,5},{5... | collective-permute-start | bytes 3145736 | tf_op jit(solution)/shard_map/ppermute | solution.py:341
  252.0 45.2 %collective-permute-start.21 = (bf16[128,2048]{1,0:T(8,128)(2,1)}, bf16[128,2048]{1,0:T(8,128)(2,1)}, u32[]{:S(2)}, u32[]{:S(2)}) collective-permute-start(bf16[128,2048]{1,0:T(8,128)(2,1)} %pad_maximum_fusion.26), channel_id=1, source_target_pairs={{0,8},{1,3},{2,10},{3,1},{4,12},{5,7},{6,14},{7,5},{8,0},{9,11},{1... | collective-permute-start | bytes 1572872 | tf_op jit(solution)/shard_map/ppermute | solution.py:265
  329.4 323.4 %all-gather.16.cloned.1.call-start = ((), (), s32[]{:S(2)}) async-start(), calls=%async_computation.3 | async-start | bytes 2621440 | tf_op jit(solution)/shard_map/all_gather | solution.py:666
  340.6 50.9 %collective-permute-start.29 = (bf16[64,2048]{1,0:T(8,128)(2,1)S(1)}, bf16[64,2048]{1,0:T(8,128)(2,1)S(1)}, u32[]{:S(2)}, u32[]{:S(2)}) collective-permute-start(bf16[64,2048]{1,0:T(8,128)(2,1)S(1)} %slice.824), channel_id=1, source_target_pairs={{0,2},{1,9},{2,0},{3,11},{4,6},{5,13},{6,4},{7,15},{8,10},{9,1},{1... | collective-permute-start | bytes 786440 | tf_op jit(solution)/shard_map/ppermute | solution.py:277
  360.9 30.5 %collective-permute-start.47 = (bf16[64,2048]{1,0:T(8,128)(2,1)S(1)}, bf16[64,2048]{1,0:T(8,128)(2,1)S(1)}, u32[]{:S(2)}, u32[]{:S(2)}) collective-permute-start(bf16[64,2048]{1,0:T(8,128)(2,1)S(1)} %slice.821), channel_id=1, source_target_pairs={{0,2},{1,9},{2,0},{3,11},{4,6},{5,13},{6,4},{7,15},{8,10},{9,1},{1... | collective-permute-start | bytes 786440 | tf_op jit(solution)/shard_map/ppermute | solution.py:277
  362.0 48.6 %collective-permute-start.34 = (bf16[2,1024,256]{2,1,0:T(8,128)(2,1)}, bf16[2,1024,256]{2,1,0:T(8,128)(2,1)}, u32[]{:S(2)}, u32[]{:S(2)}) collective-permute-start(bf16[2,1024,256]{2,1,0:T(8,128)(2,1)} %pad_maximum_fusion.12.refs_0_), channel_id=1, source_target_pairs={{0,4},{4,0},{8,12},{12,8},{16,20},{20,16},{24,28},{28,24},{1,5},{5... | collective-permute-start | bytes 3145736 | tf_op jit(solution)/shard_map/ppermute | solution.py:341
  363.7 37.2 %collective-permute-start.30 = (bf16[2,256,1024]{2,1,0:T(8,128)(2,1)}, bf16[2,256,1024]{2,1,0:T(8,128)(2,1)}, u32[]{:S(2)}, u32[]{:S(2)}) collective-permute-start(bf16[2,256,1024]{2,1,0:T(8,128)(2,1)} %dynamic-slice_bitcast_fusion.1.refs_1_), channel_id=1, source_target_pairs={{0,4},{4,0},{8,12},{12,8},{16,20},{20,16},{24,28},{28,24},{1,5},{5... | collective-permute-start | bytes 3145736 | tf_op jit(solution)/shard_map/ppermute | solution.py:342
  390.0 29.2 %collective-permute-start.35 = (bf16[2,1024,256]{2,1,0:T(8,128)(2,1)}, bf16[2,1024,256]{2,1,0:T(8,128)(2,1)}, u32[]{:S(2)}, u32[]{:S(2)}) collective-permute-start(bf16[2,1024,256]{2,1,0:T(8,128)(2,1)} %dynamic-slice_bitcast_fusion.refs_1_), channel_id=1, source_target_pairs={{0,4},{4,0},{8,12},{12,8},{16,20},{20,16},{24,28},{28,24},{1,5},{5... | collective-permute-start | bytes 3145736 | tf_op jit(solution)/shard_map/ppermute | solution.py:342
  400.9 28.5 %collective-permute-start.31 = (bf16[64,2048]{1,0:T(8,128)(2,1)S(1)}, bf16[64,2048]{1,0:T(8,128)(2,1)S(1)}, u32[]{:S(2)}, u32[]{:S(2)}) collective-permute-start(bf16[64,2048]{1,0:T(8,128)(2,1)S(1)} %get-tuple-element.71), channel_id=1, source_target_pairs={{0,2},{1,9},{2,0},{3,11},{4,6},{5,13},{6,4},{7,15},{8,10},{9,1},{1... | collective-permute-start | bytes 786440 | tf_op jit(solution)/shard_map/ppermute | solution.py:263
  566.0 48.8 %collective-permute-start.67 = (bf16[4,1024,256]{2,1,0:T(8,128)(2,1)}, bf16[4,1024,256]{2,1,0:T(8,128)(2,1)}, u32[]{:S(2)}, u32[]{:S(2)}) collective-permute-start(bf16[4,1024,256]{2,1,0:T(8,128)(2,1)} %shard_map.425), channel_id=1, source_target_pairs={{0,4},{4,0},{8,12},{12,8},{16,20},{20,16},{24,28},{28,24},{1,5},{5... | collective-permute-start | bytes 6291464 | tf_op jit(solution)/shard_map/ppermute | solution.py:392
  590.7 369.9 %reduce-scatter.3.cloned.1.call-start = ((), (), s32[]{:S(2)}) async-start(), calls=%async_computation.5 | async-start | bytes 5242880 | tf_op jit(solution)/shard_map/reduce_scatter | solution.py:630
  597.4 29.7 %collective-permute-start.75 = (bf16[128,2048]{1,0:T(8,128)(2,1)}, bf16[128,2048]{1,0:T(8,128)(2,1)}, u32[]{:S(2)}, u32[]{:S(2)}) collective-permute-start(bf16[128,2048]{1,0:T(8,128)(2,1)} %pad_maximum_fusion.33), channel_id=1, source_target_pairs={{0,8},{1,3},{2,10},{3,1},{4,12},{5,7},{6,14},{7,5},{8,0},{9,11},{1... | collective-permute-start | bytes 1572872 | tf_op jit(solution)/shard_map/ppermute | solution.py:265
  598.7 33.1 %collective-permute-start.63 = (bf16[256,2048]{1,0:T(8,128)(2,1)}, bf16[256,2048]{1,0:T(8,128)(2,1)}, u32[]{:S(2)}, u32[]{:S(2)}) collective-permute-start(bf16[256,2048]{1,0:T(8,128)(2,1)} %pad_maximum_fusion.17), channel_id=1, source_target_pairs={{0,1},{1,0},{2,3},{3,2},{4,5},{5,4},{6,7},{7,6},{8,9},{9,8},{10,11... | collective-permute-start | bytes 3145736 | tf_op jit(solution)/shard_map/ppermute | solution.py:266
  599.2 61.0 %collective-permute-start.84 = (bf16[4,256,1024]{2,1,0:T(8,128)(2,1)}, bf16[4,256,1024]{2,1,0:T(8,128)(2,1)}, u32[]{:S(2)}, u32[]{:S(2)}) collective-permute-start(bf16[4,256,1024]{2,1,0:T(8,128)(2,1)} %shard_map.428), channel_id=1, source_target_pairs={{0,4},{4,0},{8,12},{12,8},{16,20},{20,16},{24,28},{28,24},{1,5},{5... | collective-permute-start | bytes 6291464 | tf_op jit(solution)/shard_map/ppermute | solution.py:392
  623.4 44.2 %collective-permute-start.88 = (bf16[2,1024,256]{2,1,0:T(8,128)(2,1)}, bf16[2,1024,256]{2,1,0:T(8,128)(2,1)}, u32[]{:S(2)}, u32[]{:S(2)}) collective-permute-start(bf16[2,1024,256]{2,1,0:T(8,128)(2,1)} %get-tuple-element.76), channel_id=1, source_target_pairs={{0,16},{4,20},{8,24},{12,28},{16,0},{20,4},{24,8},{28,12},{1,17},{... | collective-permute-start | bytes 3145736 | tf_op jit(solution)/shard_map/ppermute | solution.py:398
  641.4 40.2 %collective-permute-start.71 = (bf16[256,2048]{1,0:T(8,128)(2,1)}, bf16[256,2048]{1,0:T(8,128)(2,1)}, u32[]{:S(2)}, u32[]{:S(2)}) collective-permute-start(bf16[256,2048]{1,0:T(8,128)(2,1)} %convolution_convert_fusion.2), channel_id=1, source_target_pairs={{0,1},{1,0},{2,3},{3,2},{4,5},{5,4},{6,7},{7,6},{8,9},{9,8},{10,11... | collective-permute-start | bytes 3145736 | tf_op jit(solution)/shard_map/ppermute | solution.py:271
  652.2 33.9 %collective-permute-start.81 = (bf16[256,2048]{1,0:T(8,128)(2,1)}, bf16[256,2048]{1,0:T(8,128)(2,1)}, u32[]{:S(2)}, u32[]{:S(2)}) collective-permute-start(bf16[256,2048]{1,0:T(8,128)(2,1)} %convolution_convert_fusion.1), channel_id=1, source_target_pairs={{0,1},{1,0},{2,3},{3,2},{4,5},{5,4},{6,7},{7,6},{8,9},{9,8},{10,11... | collective-permute-start | bytes 3145736 | tf_op jit(solution)/shard_map/ppermute | solution.py:271
  667.7 73.1 %collective-permute-start.80 = (bf16[4,256,512]{2,1,0:T(8,128)(2,1)}, bf16[4,256,512]{2,1,0:T(8,128)(2,1)}, u32[]{:S(2)}, u32[]{:S(2)}) collective-permute-start(bf16[4,256,512]{2,1,0:T(8,128)(2,1)} %shard_map.430), channel_id=1, source_target_pairs={{0,4},{4,0},{8,12},{12,8},{16,20},{20,16},{24,28},{28,24},{1,5},{5... | collective-permute-start | bytes 3145736 | tf_op jit(solution)/shard_map/ppermute | solution.py:392
  693.4 283.3 %reduce-scatter.5.cloned.1.call-start = ((), (), s32[]{:S(2)}) async-start(), calls=%async_computation.6 | async-start | bytes 3932160 | tf_op jit(solution)/shard_map/reduce_scatter | solution.py:375
  705.0 101.8 %collective-permute-start.106 = (bf16[2,256,1024]{2,1,0:T(8,128)(2,1)}, bf16[2,256,1024]{2,1,0:T(8,128)(2,1)}, u32[]{:S(2)}, u32[]{:S(2)}) collective-permute-start(bf16[2,256,1024]{2,1,0:T(8,128)(2,1)} %get-tuple-element.90), channel_id=1, source_target_pairs={{0,16},{4,20},{8,24},{12,28},{16,0},{20,4},{24,8},{28,12},{1,17},{... | collective-permute-start | bytes 3145736 | tf_op jit(solution)/shard_map/ppermute | solution.py:398
  705.1 101.7 %collective-permute-start.99 = (bf16[4,512,512]{2,1,0:T(8,128)(2,1)}, bf16[4,512,512]{2,1,0:T(8,128)(2,1)}, u32[]{:S(2)}, u32[]{:S(2)}) collective-permute-start(bf16[4,512,512]{2,1,0:T(8,128)(2,1)} %shard_map.433), channel_id=1, source_target_pairs={{0,4},{4,0},{8,12},{12,8},{16,20},{20,16},{24,28},{28,24},{1,5},{5... | collective-permute-start | bytes 6291464 | tf_op jit(solution)/shard_map/ppermute | solution.py:392
  748.7 64.3 %collective-permute-start.102 = (bf16[2,256,512]{2,1,0:T(8,128)(2,1)}, bf16[2,256,512]{2,1,0:T(8,128)(2,1)}, u32[]{:S(2)}, u32[]{:S(2)}) collective-permute-start(bf16[2,256,512]{2,1,0:T(8,128)(2,1)} %get-tuple-element.84), channel_id=1, source_target_pairs={{0,16},{4,20},{8,24},{12,28},{16,0},{20,4},{24,8},{28,12},{1,17},{... | collective-permute-start | bytes 1572872 | tf_op jit(solution)/shard_map/ppermute | solution.py:398
  804.4 28.4 %collective-permute-start.92 = (bf16[256,2048]{1,0:T(8,128)(2,1)}, bf16[256,2048]{1,0:T(8,128)(2,1)}, u32[]{:S(2)}, u32[]{:S(2)}) collective-permute-start(bf16[256,2048]{1,0:T(8,128)(2,1)} %convolution_convert_fusion.11), channel_id=1, source_target_pairs={{0,1},{1,0},{2,3},{3,2},{4,5},{5,4},{6,7},{7,6},{8,9},{9,8},{10,11... | collective-permute-start | bytes 3145736 | tf_op jit(solution)/shard_map/ppermute | solution.py:271
  806.8 31.2 %collective-permute-start.89 = (bf16[256,2048]{1,0:T(8,128)(2,1)}, bf16[256,2048]{1,0:T(8,128)(2,1)}, u32[]{:S(2)}, u32[]{:S(2)}) collective-permute-start(bf16[256,2048]{1,0:T(8,128)(2,1)} %convolution_convert_fusion.12), channel_id=1, source_target_pairs={{0,1},{1,0},{2,3},{3,2},{4,5},{5,4},{6,7},{7,6},{8,9},{9,8},{10,11... | collective-permute-start | bytes 3145736 | tf_op jit(solution)/shard_map/ppermute | solution.py:271
  821.1 157.5 %all-gather.18.cloned.1.call-start = ((), (), s32[]{:S(2)}) async-start(), calls=%async_computation.4 | async-start | bytes 2621440 | tf_op jit(solution)/shard_map/all_gather | solution.py:666
  822.0 115.7 %collective-permute-start.104 = (bf16[2,512,512]{2,1,0:T(8,128)(2,1)}, bf16[2,512,512]{2,1,0:T(8,128)(2,1)}, u32[]{:S(2)}, u32[]{:S(2)}) collective-permute-start(bf16[2,512,512]{2,1,0:T(8,128)(2,1)} %get-tuple-element.98), channel_id=1, source_target_pairs={{0,16},{4,20},{8,24},{12,28},{16,0},{20,4},{24,8},{28,12},{1,17},{... | collective-permute-start | bytes 3145736 | tf_op jit(solution)/shard_map/ppermute | solution.py:398
  832.6 68.9 %collective-permute-start.107 = (bf16[256,1024]{1,0:T(8,128)(2,1)}, bf16[256,1024]{1,0:T(8,128)(2,1)}, u32[]{:S(2)}, u32[]{:S(2)}) collective-permute-start(bf16[256,1024]{1,0:T(8,128)(2,1)} %fusion.55), channel_id=1, source_target_pairs={{0,8},{4,12},{8,0},{12,4},{16,24},{20,28},{24,16},{28,20},{1,9},{5... | collective-permute-start | bytes 1572872 | tf_op jit(solution)/shard_map/ppermute | solution.py:320
  836.0 51.8 %collective-permute-start.93 = (bf16[128,2048]{1,0:T(8,128)(2,1)}, bf16[128,2048]{1,0:T(8,128)(2,1)}, u32[]{:S(2)}, u32[]{:S(2)}) collective-permute-start(bf16[128,2048]{1,0:T(8,128)(2,1)} %slice.802), channel_id=1, source_target_pairs={{0,8},{1,3},{2,10},{3,1},{4,12},{5,7},{6,14},{7,5},{8,0},{9,11},{1... | collective-permute-start | bytes 1572872 | tf_op jit(solution)/shard_map/ppermute | solution.py:275
  842.5 55.3 %collective-permute-start.90 = (bf16[128,2048]{1,0:T(8,128)(2,1)}, bf16[128,2048]{1,0:T(8,128)(2,1)}, u32[]{:S(2)}, u32[]{:S(2)}) collective-permute-start(bf16[128,2048]{1,0:T(8,128)(2,1)} %slice.803), channel_id=1, source_target_pairs={{0,8},{1,3},{2,10},{3,1},{4,12},{5,7},{6,14},{7,5},{8,0},{9,11},{1... | collective-permute-start | bytes 1572872 | tf_op jit(solution)/shard_map/ppermute | solution.py:275
  853.2 62.8 %collective-permute-start.100 = (bf16[2,256,256]{2,1,0:T(8,128)(2,1)}, bf16[2,256,256]{2,1,0:T(8,128)(2,1)}, u32[]{:S(2)}, u32[]{:S(2)}) collective-permute-start(bf16[2,256,256]{2,1,0:T(8,128)(2,1)} %get-tuple-element.102), channel_id=1, source_target_pairs={{0,16},{4,20},{8,24},{12,28},{16,0},{20,4},{24,8},{28,12},{1,17},{... | collective-permute-start | bytes 786440 | tf_op jit(solution)/shard_map/ppermute | solution.py:398
  889.8 26.2 %collective-permute-start.94 = (bf16[64,2048]{1,0:T(8,128)(2,1)}, bf16[64,2048]{1,0:T(8,128)(2,1)S(1)}, u32[]{:S(2)}, u32[]{:S(2)}) collective-permute-start(bf16[64,2048]{1,0:T(8,128)(2,1)} %slice.814), channel_id=1, source_target_pairs={{0,2},{1,9},{2,0},{3,11},{4,6},{5,13},{6,4},{7,15},{8,10},{9,1},{1... | collective-permute-start | bytes 786440 | tf_op jit(solution)/shard_map/ppermute | solution.py:277
  (244 other events, 2822.8 us)
Sparse Core Ops, SparseCore 0:
  24.6 45.7 all-gather.19
  72.5 45.0 all-gather.23
  119.8 55.4 all-gather.21
  177.3 33.4 all-gather.13
  238.6 56.1 all-gather.25
  329.5 57.9 all-gather.27
  590.8 23.9 all-gather.15
  693.5 46.9 reduce-scatter.2
  821.2 114.0 reduce-scatter.4
  937.3 22.3 all-gather.17
